TPU v7x, 256 devices: a whole 4x4x8 slice. The times are simulated.
256 devices in a mesh: region: 8 (over x, core), sector: 32 (over z, y).
Axes of the slice: x: 4, y: 4, z: 8, core: 2. Of those that a mesh axis runs over, the one named last changes fastest.
Arguments:
- psi: bfloat16 [8, 32, 256, 256], P('region', 'sector'), may hold values from -12 to 12
- left_env: bfloat16 [8, 32, 18, 256, 256], P('region', 'sector'), may hold values from -4 to 4
- right_env: bfloat16 [8, 32, 18, 256, 256], P('region', 'sector'), may hold values from -4 to 4
- diagonal: bfloat16 [8, 32, 256, 256], P('region', 'sector'), may hold values from -2 to 0
- left_coeff: float32 [18, 18], replicated, may hold values from -2 to 2
- right_coeff: float32 [18, 18], replicated, may hold values from -2 to 2
- mpo_mask: int32 [18, 18], replicated, may hold values 0 or 1
- sector_target: int32 [32, 18], P('sector'), may hold values from 0 to 31
- block_size: int32 [32], P('sector'), may hold values from 128 to 256, as said below
Outputs:
- bond: bfloat16 [8, 32, 256, 256], P('region', 'sector')
- energy: float32 [8], P('region')
Inputs may be any that keep to these rules, and one draw needn't show every extreme that they name: `block_size`: one sector block has all 256 rows live, and one has exactly 128.
All inputs are finite; a program needn't handle non-finite values.
Results may differ from a plain program's by a relative error of at most 0.017.
Values may be sent and summed in bfloat16 or wider, within the bound.
No kernel may reach another device: no remote copies, remote signals or barrier semaphores. Data moves between devices by JAX's collectives and lax.ppermute only.
A program may use at most 64 MiB of HBM per device.

v0:
```python
import math

import jax
import jax.numpy as jnp
from jax import lax
from jax.sharding import PartitionSpec as P

ITERS = 2


step_size = 0.5


def shifted(value, axis, steps):
    count = lax.axis_size(axis)
    leading, last = (max(0, -steps), min(count, count - steps))
    return lax.ppermute(value, axis, [(source, source + steps) for source in range(leading, last)])


def carry_left(masked, env_blocks, mixing, rescale):
    left_half = jnp.einsum(
        "wij,jk->wik", env_blocks, masked, preferred_element_type=jnp.float32
    ).astype(jnp.bfloat16)
    left_terms = jnp.einsum("ji,wjk->wik", masked, left_half, preferred_element_type=jnp.float32)
    mixed = jnp.einsum("vw,wik->vik", mixing, left_terms, precision=lax.Precision.HIGHEST)
    return (rescale * mixed).astype(jnp.bfloat16)


def carry_right(masked, env_blocks, mixing, rescale):
    right_half = jnp.einsum(
        "wij,kj->wik", env_blocks, masked, preferred_element_type=jnp.float32
    ).astype(jnp.bfloat16)
    right_terms = jnp.einsum("ij,wjk->wik", masked, right_half, preferred_element_type=jnp.float32)
    mixed = jnp.einsum("vw,wik->vik", mixing, right_terms, precision=lax.Precision.HIGHEST)
    return (rescale * mixed).astype(jnp.bfloat16)


def local(
    psi, left_env, right_env, diagonal, left_coeff, right_coeff, mpo_mask, sector_target, block_size
):
    sectors = lax.axis_size("sector")
    block_width = psi.shape[-1]
    mpo_terms = left_env.shape[2]
    live_rows = jnp.arange(block_width, dtype=jnp.int32) < block_size[0]
    keep_mask = (live_rows[:, None] & live_rows[None, :]).astype(jnp.float32)
    masked = (psi[0, 0].astype(jnp.float32) * keep_mask).astype(jnp.bfloat16)
    wide = masked.astype(jnp.float32)
    start_norm = lax.psum(jnp.sum(wide * wide), "sector")
    rescale = sectors * block_width / start_norm
    pattern = mpo_mask.astype(jnp.float32)
    left_out = carry_left(masked, left_env[0, 0], left_coeff * pattern, rescale)
    right_out = carry_right(masked, right_env[0, 0], right_coeff * pattern, rescale)
    region_index = lax.axis_index("region")
    at_start = region_index == 0
    at_end = region_index == lax.axis_size("region") - 1
    from_left = shifted(left_out, "region", 1)
    from_right = shifted(right_out, "region", -1)
    left_used = jnp.where(at_start, left_env[0, 0], from_left)
    right_used = jnp.where(at_end, right_env[0, 0], from_right)
    routing = (sector_target[0][:, None] == jnp.arange(sectors, dtype=jnp.int32)[None, :]).astype(
        jnp.float32
    )
    inv_root = 1.0 / math.sqrt(mpo_terms)
    diag_here = diagonal[0, 0].astype(jnp.float32)
    total_cells = sectors * block_width * block_width
    vector = (wide * jnp.sqrt(total_cells / start_norm)).astype(jnp.bfloat16)
    energy = jnp.zeros((), jnp.float32)
    for step in range(ITERS):
        applied = jnp.einsum(
            "wij,jk->wik", left_used, vector, preferred_element_type=jnp.float32
        ).astype(jnp.bfloat16)
        product = jnp.einsum(
            "wik,wkl->wil", applied, right_used, preferred_element_type=jnp.float32
        )
        partials = (
            jnp.einsum("wt,wil->til", routing, product, precision=lax.Precision.HIGHEST) * inv_root
        )
        summed = lax.psum_scatter(
            partials.astype(jnp.bfloat16), "sector", scatter_dimension=0, tiled=True
        ).astype(jnp.float32)
        current = vector.astype(jnp.float32)
        applied_h = (summed[0] + diag_here * current) * keep_mask
        intersection, cross = lax.psum(
            (jnp.sum(current * current), jnp.sum(current * applied_h)), "sector"
        )
        energy = cross / intersection
        update = current - step_size * (applied_h - energy * current)
        norm_sq = lax.psum(jnp.sum(update * update), "sector")
        vector = (update * jnp.sqrt(total_cells / norm_sq)).astype(jnp.bfloat16)
    return (vector[None, None], jnp.reshape(energy, (1,)))


def solution(mesh):
    in_specs = (
        P("region", "sector", None, None),
        P("region", "sector", None, None, None),
        P("region", "sector", None, None, None),
        P("region", "sector", None, None),
        P(),
        P(),
        P(),
        P("sector", None),
        P("sector"),
    )
    out_specs = (P("region", "sector", None, None), P("region"))
    return jax.shard_map(local, mesh=mesh, in_specs=in_specs, out_specs=out_specs, check_vma=False)
```

profile of v0, /device:TPU:6, one launch (start us, length us, event | category | flops | bytes accessed | tf_op | source)
XLA Modules:
  0.0 949.4 jit_solution(9426039613454539660)
XLA Ops:
  7.2 0.0 reduce-scatter.3.cloned.1.call-start
  7.9 1.7 fusion.44
  9.5 78.5 %psum.49 = f32[]{:T(128)} all-reduce(f32[]{:T(128)} %fusion.44), channel_id=1, replica_groups=mesh['region'=8,'sector'=32] {'sector'}, use_global_device_ids=true, to_apply=%region_1.0 | all-reduce | flops 1 | bytes 8 | tf_op jit(solution)/shard_map/psum | solution.py:48
  88.1 5.5 fusion.26
  93.5 6.3 copy.19
  100.6 0.0 copy-done.5
  100.6 0.0 copy-done.6
  100.6 7.4 multiply_convert_fusion.3
  108.0 0.0 copy-start.1
  108.0 0.0 copy-start.2
  108.0 1.9 copy.20
  109.9 1.9 collective-permute-start
  111.8 0.0 copy-done.1
  111.9 0.0 copy-done.2
  111.9 3.7 fusion.35
  115.5 6.3 copy.21
  121.9 0.0 copy-done.7
  121.9 7.4 multiply_convert_fusion.2
  129.3 0.0 copy-start
  129.3 2.0 copy.22
  131.3 3.8 collective-permute-start.1
  135.8 0.0 copy-start.8
  135.8 4.6 collective-permute-done
  140.4 21.2 %collective-permute-done.1 = bf16[18,256,256]{2,1,0:T(8,128)(2,1)} collective-permute-done((bf16[18,256,256]{2,1,0:T(8,128)(2,1)}, bf16[18,256,256]{2,1,0:T(8,128)(2,1)}, u32[]{:S(2)}, u32[]{:S(2)}) %collective-permute-start.1) | collective-permute-done | bytes 2359328 | tf_op jit(solution)/shard_map/ppermute | solution.py:17
  161.6 0.0 copy-done
  161.6 6.8 fusion.19
  168.4 0.0 copy-done.8
  168.4 10.3 %multiply_convert_fusion.1 = bf16[32,256,256]{2,0,1:T(8,128)(2,1)S(1)} fusion(f32[18,256,256]{2,1,0:T(8,128)} %fusion.19, s32[18]{0:T(128)S(1)} %bitcast.169), kind=kOutput, calls=%fused_computation.1 | convolution fusion | flops 457179712 | bytes 8912968 | tf_op jit(solution)/shard_map/wt,wil->til/dot_general | solution.py:76
  178.6 4.3 copy.24
  183.0 0.0 reduce-scatter.3.cloned.1.call-update
  183.0 0.0 reduce-scatter.5.cloned.1.call-start
  183.1 216.6 %reduce-scatter.3.cloned.1.call-done = bf16[1,256,256]{2,1,0:T(8,128)(2,1)} async-done(((bf16[32,256,256]{2,1,0:T(8,128)(2,1)}), bf16[1,256,256]{2,1,0:T(8,128)(2,1)}) %reduce-scatter.3.cloned.1.call-update) | async-done | bytes 131088 | tf_op jit(solution)/shard_map/reduce_scatter | solution.py:78
  399.7 0.0 copy-done.3
  399.7 1.7 fusion.61
  401.4 72.8 %all-reduce.1 = (f32[]{:T(128)}, f32[]{:T(128)}) all-reduce(f32[]{:T(128)} %get-tuple-element.3, f32[]{:T(128)} %get-tuple-element.2), channel_id=1, replica_groups=mesh['region'=8,'sector'=32] {'sector'}, use_global_device_ids=true, to_apply=%region_4.5 | all-reduce | flops 2 | bytes 16 | tf_op jit(solution)/shard_map/psum | solution.py:83
  475.6 1.7 multiply_reduce_fusion
  477.4 70.5 %psum.52 = f32[]{:T(128)} all-reduce(f32[]{:T(128)} %multiply_reduce_fusion), channel_id=1, replica_groups=mesh['region'=8,'sector'=32] {'sector'}, use_global_device_ids=true, to_apply=%region_8.9 | all-reduce | flops 1 | bytes 8 | tf_op jit(solution)/shard_map/psum | solution.py:88
  548.5 1.1 multiply_convert_fusion.4
  549.7 6.7 fusion.16
  556.4 10.3 %multiply_convert_fusion = bf16[32,256,256]{2,0,1:T(8,128)(2,1)S(1)} fusion(f32[18,256,256]{2,1,0:T(8,128)} %fusion.16, s32[18]{0:T(128)S(1)} %bitcast.170), kind=kOutput, calls=%fused_computation | convolution fusion | flops 457179712 | bytes 8912968 | tf_op jit(solution)/shard_map/wt,wil->til/dot_general | solution.py:76
  566.7 4.3 copy.26
  571.0 0.0 reduce-scatter.5.cloned.1.call-update
  571.0 220.1 %reduce-scatter.5.cloned.1.call-done = bf16[1,256,256]{2,1,0:T(8,128)(2,1)} async-done(((bf16[32,256,256]{2,1,0:T(8,128)(2,1)}), bf16[1,256,256]{2,1,0:T(8,128)(2,1)}) %reduce-scatter.5.cloned.1.call-update) | async-done | bytes 131088 | tf_op jit(solution)/shard_map/reduce_scatter | solution.py:78
  791.2 1.7 fusion.65
  792.8 72.8 %all-reduce = (f32[]{:T(128)}, f32[]{:T(128)}) all-reduce(f32[]{:T(128)} %get-tuple-element.5, f32[]{:T(128)} %get-tuple-element.4), channel_id=1, replica_groups=mesh['region'=8,'sector'=32] {'sector'}, use_global_device_ids=true, to_apply=%region_11.12 | all-reduce | flops 2 | bytes 16 | tf_op jit(solution)/shard_map/psum | solution.py:83
  866.9 1.7 fusion.69
  868.6 70.2 %psum.55 = f32[]{:T(128)} all-reduce(f32[]{:T(128)} %fusion.69), channel_id=1, replica_groups=mesh['region'=8,'sector'=32] {'sector'}, use_global_device_ids=true, to_apply=%region_15.16 | all-reduce | flops 1 | bytes 8 | tf_op jit(solution)/shard_map/psum | solution.py:88
  939.6 1.8 fusion.57
  (7 shorter events, 0.0 us)
Async XLA Ops:
  7.2 392.5 %reduce-scatter.3.cloned.1.call-start = ((), (), s32[]{:S(2)}) async-start(), calls=%async_computation.2 | async-start | bytes 4325376 | tf_op jit(solution)/shard_map/reduce_scatter | solution.py:78
  93.5 7.0 copy-start.5
  93.5 7.1 copy-start.6
  108.0 3.8 copy-start.1
  108.0 3.8 copy-start.2
  109.9 30.5 %collective-permute-start = (bf16[18,256,256]{2,1,0:T(8,128)(2,1)}, bf16[18,256,256]{2,1,0:T(8,128)(2,1)}, u32[]{:S(2)}, u32[]{:S(2)}) collective-permute-start(bf16[18,256,256]{2,1,0:T(8,128)(2,1)} %copy.20), channel_id=1, source_target_pairs={{0,32},{32,64},{64,96},{96,128},{128,160},{160,192},{192,224},{1,3... | collective-permute-start | bytes 7077896 | tf_op jit(solution)/shard_map/ppermute | solution.py:17
  115.5 6.3 copy-start.7
  129.3 32.3 %copy-start = (bf16[1,1,18,256,256]{4,3,2,1,0:T(8,128)(2,1)S(1)}, bf16[1,1,18,256,256]{4,3,2,1,0:T(8,128)(2,1)}, u32[]{:S(2)}) copy-start(bf16[1,1,18,256,256]{4,3,2,1,0:T(8,128)(2,1)} %param.10) | copy-start | bytes 7077892
  131.3 30.3 %collective-permute-start.1 = (bf16[18,256,256]{2,1,0:T(8,128)(2,1)}, bf16[18,256,256]{2,1,0:T(8,128)(2,1)}, u32[]{:S(2)}, u32[]{:S(2)}) collective-permute-start(bf16[18,256,256]{2,1,0:T(8,128)(2,1)} %copy.22), channel_id=1, source_target_pairs={{32,0},{64,32},{96,64},{128,96},{160,128},{192,160},{224,192},{33,... | collective-permute-start | bytes 7077896 | tf_op jit(solution)/shard_map/ppermute | solution.py:17
  135.8 32.5 %copy-start.8 = (s32[1,18]{1,0:T(1,128)S(1)}, s32[1,18]{1,0:T(1,128)}, u32[]{:S(2)}) copy-start(s32[1,18]{1,0:T(1,128)} %param.16) | copy-start | bytes 220
  183.0 216.7 %copy-start.3 = (bf16[1,1,256,256]{3,2,1,0:T(8,128)(2,1)S(1)}, bf16[1,1,256,256]{3,2,1,0:T(8,128)(2,1)}, u32[]{:S(2)}) copy-start(bf16[1,1,256,256]{3,2,1,0:T(8,128)(2,1)} %param.12) | copy-start | bytes 393220
  183.0 608.2 %reduce-scatter.5.cloned.1.call-start = ((), (), s32[]{:S(2)}) async-start(), calls=%async_computation.3 | async-start | bytes 4325376 | tf_op jit(solution)/shard_map/reduce_scatter | solution.py:78
  571.0 368.6 %copy-start.4 = (bf16[1,256,256]{2,1,0:T(8,128)(2,1)S(1)}, bf16[1,256,256]{2,1,0:T(8,128)(2,1)}, u32[]{:S(2)}) copy-start(bf16[1,256,256]{2,1,0:T(8,128)(2,1)} %reduce-scatter.3.cloned.1.call-done) | copy-start | bytes 393220
Sparse Core Ops, SparseCore 0:
  183.1 216.5 reduce-scatter.2
  571.2 219.9 reduce-scatter.4
where the time goes:
time: 951 us; the launch traced here: 949 us
  waiting for transfers between devices  463 us (49%)
  blocking collectives  365 us (38%)
  matrix products  58 us (6%)
  local copies, waits for them, and re-layouts  25.3 us (3%)
  between operations  21.5 us (2%)
  other arithmetic  11.4 us (1%)
    reduce_scatter x2, waiting for transfers between devices, local(): lax.psum_scatter(partials.astype(jnp.bfloat16), 'sector', scatter_dimensi...  437 us
    psum x2, blocking collectives, local(): lax.psum((jnp.sum(current * current), jnp.sum(current * applied_h)), 'sec...  146 us
    psum x2, blocking collectives, local(): norm_sq = lax.psum(jnp.sum(update * update), 'sector')  141 us
    psum x1, blocking collectives, local(): start_norm = lax.psum(jnp.sum(wide * wide), 'sector')  78.5 us
    ppermute x2, waiting for transfers between devices, shifted(): lax.ppermute(value, axis, [(source, source + steps) for source in range(l...  25.7 us
    dot_general x2, matrix products, local(): jnp.einsum('wt,wil->til', routing, product, precision=lax.Precision.HIGHEST)  20.5 us
  transfers between devices with their start and end apart: 4, of which 4 were waited for; matrix products, arithmetic and copies ran while one was open for 2% of the time, Pallas kernels for 0%

commit v1 on v0

v1 whole, which is shorter than its diff:
```python
import functools
import math

import jax
import jax.numpy as jnp
from jax import lax
from jax.experimental import pallas as pl
from jax.experimental.pallas import tpu as pltpu
from jax.sharding import Mesh
from jax.sharding import PartitionSpec as P

STEP = 0.5
ROWS_Z = 96
F32 = jnp.float32
BF16 = jnp.bfloat16
Z, Y = "z", "y"
REGION = ("x", "core")
SECTOR = ("z", "y")
VMEM_BYTES = 48 * 1024 * 1024


def along(value, axis, steps):
    count = lax.axis_size(axis)
    return lax.ppermute(value, axis, [(i, (i + steps) % count) for i in range(count)])


def exchanged(value, axis, bit):
    count = lax.axis_size(axis)
    return lax.ppermute(value, axis, [(i, i ^ bit) for i in range(count)])


def to_region(value, steps):
    count = lax.axis_size(REGION)
    leading, last = (max(0, -steps), min(count, count - steps))
    return lax.ppermute(value, REGION, [(i, i + steps) for i in range(leading, last)])


def sector_sum(value):
    for axis in (Y, Z):
        bit = 1
        while bit < lax.axis_size(axis):
            value = value + exchanged(value, axis, bit)
            bit *= 2
    return value


def add(*terms):
    total = terms[0].astype(F32)
    for term in terms[1:]:
        total = total + term.astype(F32)
    return total.astype(BF16)


def carry_kernel(mix_ref, first_ref, second_ref, env_ref, out_ref, terms_ref):
    count = env_ref.shape[0]
    width = env_ref.shape[1]
    group = 3 if count % 3 == 0 else 1

    @pl.loop(0, count // group)
    def _(step):
        for lane in range(group):
            w = step * group + lane
            half = jnp.dot(env_ref[w], first_ref[...], preferred_element_type=F32).astype(BF16)
            terms_ref[w] = jnp.dot(second_ref[...], half, preferred_element_type=F32)

    tile = 16
    block = 9 if count % 9 == 0 else count

    @pl.loop(0, width // tile)
    def _(step):
        rows = pl.ds(pl.multiple_of(step * tile, tile), tile)
        for start in range(0, count, block):
            totals = [None] * block
            for w in range(count):
                term = terms_ref[w, rows, :]
                for k in range(block):
                    part = mix_ref[start + k, w] * term
                    totals[k] = part if w == 0 else totals[k] + part
            for k in range(block):
                out_ref[start + k, rows, :] = totals[k].astype(BF16)


def carry(mix, first, second, env):
    count, width, _ = env.shape
    vmem = pl.BlockSpec(memory_space=pltpu.VMEM)
    return pl.pallas_call(
        carry_kernel,
        out_shape=jax.ShapeDtypeStruct(env.shape, BF16),
        in_specs=[pl.BlockSpec(memory_space=pltpu.SMEM), vmem, vmem, vmem],
        out_specs=vmem,
        scratch_shapes=[pltpu.VMEM((count, width, width), F32)],
        compiler_params=pltpu.CompilerParams(vmem_limit_bytes=VMEM_BYTES),
        cost_estimate=pl.CostEstimate(
            flops=4 * count * width**3, bytes_accessed=4 * count * width**2, transcendentals=0
        ),
    )(mix, first, second, env)


def apply_kernel(
    scale_ref, place_ref, target_ref,
    vector_ref, left_own, left_got, right_own, right_got,
    far_up, far_down, up2, up1, down2, down1, here, by_y,
    left_ref, right_ref, terms_ref, order_ref, first_ref, seen_ref, left_sem, right_sem,
):
    count = left_ref.shape[0]
    width = left_ref.shape[1]
    y_count, z_count = by_y.shape[0], by_y.shape[1]
    sectors = y_count * z_count
    my_z, at_start, at_end = place_ref[0], place_ref[1], place_ref[2]

    for chosen, own, got, held, sem in (
        (at_start, left_own, left_got, left_ref, left_sem),
        (at_end, right_own, right_got, right_ref, right_sem),
    ):

        @pl.when(chosen == 1)
        def _(own=own, held=held, sem=sem):
            for w in range(count):
                pltpu.make_async_copy(own.at[w], held.at[w], sem.at[w]).start()

        @pl.when(chosen != 1)
        def _(got=got, held=held, sem=sem):
            for w in range(count):
                pltpu.make_async_copy(got.at[w], held.at[w], sem.at[w]).start()

    @pl.loop(0, sectors + 1)
    def _(t):
        first_ref[t] = 0

    @pl.loop(0, count)
    def _(w):
        t = target_ref[w]
        first_ref[t + 1] = first_ref[t + 1] + 1

    @pl.loop(0, sectors)
    def _(t):
        seen_ref[t] = first_ref[t]
        first_ref[t + 1] = first_ref[t + 1] + first_ref[t]

    @pl.loop(0, count)
    def _(w):
        t = target_ref[w]
        order_ref[seen_ref[t]] = w
        seen_ref[t] = seen_ref[t] + 1

    left_scale, right_scale = scale_ref[0], scale_ref[1]
    group = 3 if count % 3 == 0 else 1

    @pl.loop(0, count // group)
    def _(step):
        for lane in range(group):
            w = step * group + lane
            pltpu.make_async_copy(left_got.at[w], left_ref.at[w], left_sem.at[w]).wait()
            pltpu.make_async_copy(right_got.at[w], right_ref.at[w], right_sem.at[w]).wait()
        for lane in range(group):
            w = step * group + lane
            applied = jnp.dot(left_ref[w], vector_ref[...], preferred_element_type=F32)
            applied = (applied * left_scale).astype(BF16)
            terms_ref[w] = jnp.dot(applied, right_ref[w], preferred_element_type=F32)

    tile = 32

    def emit(t, ref, rows_from, rows):
        low, high = first_ref[t], first_ref[t + 1]

        @pl.when(low == high)
        def _():
            ref[...] = jnp.zeros(ref.shape, BF16)

        @pl.when(low < high)
        def _():
            @pl.loop(0, rows // tile)
            def _(step):
                at = pl.multiple_of(step * tile, tile)
                source = pl.ds(rows_from + at, tile)
                total = lax.fori_loop(
                    low + 1,
                    high,
                    lambda i, total: total + terms_ref[order_ref[i], source, :],
                    terms_ref[order_ref[low], source, :],
                )
                ref[pl.ds(at, tile), :] = (total * right_scale).astype(BF16)

    z_rows = here.shape[1]
    half = y_count // 2
    for offset, parts in (
        (0, ((here, 0, 0, y_count),)),
        (1, ((up1, 0, 0, y_count),)),
        (2, ((up2, 0, 0, y_count),)),
        (3, ((far_up, half, 0, y_count),)),
        (4, ((far_up, 0, 0, half), (far_down, -half, half, y_count))),
        (5, ((far_down, half, 0, y_count),)),
        (6, ((down2, 0, 0, y_count),)),
        (7, ((down1, 0, 0, y_count),)),
    ):
        to_z = lax.rem(my_z + offset, z_count)
        for ref, shift, low_y, high_y in parts:

            @pl.loop(low_y, high_y)
            def _(to_y, ref=ref, shift=shift, to_z=to_z):
                t = to_z * y_count + to_y
                emit(t, ref.at[to_y + shift], 0, z_rows)
                emit(t, by_y.at[to_y, to_z], z_rows, width - z_rows)


def apply(scales, place, target, vector, left_own, left_got, right_own, right_got):
    count, width, _ = left_own.shape
    z_count, y_count = lax.axis_size(Z), lax.axis_size(Y)
    a, b = ROWS_Z, width - ROWS_Z
    smem = pl.BlockSpec(memory_space=pltpu.SMEM)
    vmem = pl.BlockSpec(memory_space=pltpu.VMEM)
    anywhere = pl.BlockSpec(memory_space=pl.ANY)
    near = jax.ShapeDtypeStruct((y_count, a, width), BF16)
    far = jax.ShapeDtypeStruct((y_count + y_count // 2, a, width), BF16)
    return pl.pallas_call(
        apply_kernel,
        out_shape=[far, far, near, near, near, near, near,
                   jax.ShapeDtypeStruct((y_count, z_count, b, width), BF16)],
        in_specs=[smem, smem, smem, vmem] + [anywhere] * 4,
        out_specs=[vmem] * 8,
        scratch_shapes=[
            pltpu.VMEM((count, width, width), BF16),
            pltpu.VMEM((count, width, width), BF16),
            pltpu.VMEM((count, width, width), F32),
            pltpu.SMEM((count,), jnp.int32),
            pltpu.SMEM((z_count * y_count + 1,), jnp.int32),
            pltpu.SMEM((z_count * y_count,), jnp.int32),
            pltpu.SemaphoreType.DMA((count,)),
            pltpu.SemaphoreType.DMA((count,)),
        ],
        compiler_params=pltpu.CompilerParams(vmem_limit_bytes=VMEM_BYTES),
        cost_estimate=pl.CostEstimate(
            flops=4 * count * width**3, bytes_accessed=8 * count * width**2, transcendentals=0
        ),
    )(scales, place, target, vector, left_own, left_got, right_own, right_got)


def target_sum(parts):
    far_up, far_down, up2, up1, down2, down1, here, by_y = parts
    y_count = by_y.shape[0]
    half = y_count // 2
    columns = lax.all_to_all(by_y, Y, 0, 0, tiled=True)
    from_down = along(far_up, Z, 2)
    from_up = along(far_down, Z, -2)
    send_up2 = jnp.concatenate([add(up2[:half], from_down[:half]), up2[half:]], 0)
    send_down2 = jnp.concatenate([down2[:half], add(down2[half:], from_up[:half])], 0)
    send_up1 = add(up1, from_down[half:])
    send_down1 = add(down1, from_up[half:])
    mine_z = add(
        here,
        along(send_up2, Z, 2),
        along(send_down2, Z, -2),
        along(send_up1, Z, 1),
        along(send_down1, Z, -1),
    )
    column = add(*[columns[k] for k in range(y_count)])
    rows_low = lax.all_to_all(mine_z, Y, 0, 0, tiled=True)
    rows_high = lax.all_to_all(column, Z, 0, 0, tiled=True)
    low = jnp.sum(rows_low.astype(F32), 0)
    high = jnp.sum(rows_high.astype(F32), 0)
    return jnp.concatenate([low, high], 0)


def spread(values):
    rows = [jnp.broadcast_to(v.reshape(1, 1), (1, 128)) for v in values]
    rows.append(jnp.zeros((8 - len(rows), 128), F32))
    return jnp.concatenate(rows, 0)


def local(
    psi, left_env, right_env, diagonal, left_coeff, right_coeff, mpo_mask, sector_target, block_size
):
    sectors = lax.axis_size(SECTOR)
    width = psi.shape[-1]
    count = left_env.shape[2]
    left_own, right_own = left_env[0, 0], right_env[0, 0]
    live_rows = jnp.arange(width, dtype=jnp.int32) < block_size[0]
    keep = (live_rows[:, None] & live_rows[None, :]).astype(F32)
    wide = psi[0, 0].astype(F32) * keep
    masked = wide.astype(BF16)
    turned = masked.T
    pattern = mpo_mask.astype(F32)
    region = lax.axis_index(REGION)
    at_start = region == 0
    at_end = region == lax.axis_size(REGION) - 1

    norm = jnp.broadcast_to(jnp.sum(wide * wide).reshape(1, 1), (1, 128))
    left_out = carry(left_coeff * pattern, masked, turned, left_own)
    left_got = to_region(left_out, 1)
    norm_before, norm_after = to_region(norm, 1), to_region(norm, -1)
    right_out = carry(right_coeff * pattern, turned, masked, right_own)
    right_got = to_region(right_out, -1)
    norms = jnp.concatenate([norm, norm_before, norm_after, jnp.zeros((5, 128), F32)], 0)
    norms = sector_sum(norms)

    inv_root = 1.0 / math.sqrt(count)
    cells = sectors * width * width
    left_scale = jnp.where(at_start, 1.0, sectors * width / norms[1, 0])
    right_scale = jnp.where(at_end, 1.0, sectors * width / norms[2, 0]) * inv_root
    scales = jnp.stack([left_scale, right_scale])
    place = jnp.stack(
        [lax.axis_index(Z), at_start.astype(jnp.int32), at_end.astype(jnp.int32)]
    ).astype(jnp.int32)
    diag = diagonal[0, 0].astype(F32)

    vector = (wide * jnp.sqrt(cells / norms[0, 0])).astype(BF16)
    envs = (left_own, left_got, right_own, right_got)
    current = vector.astype(F32)
    once = (target_sum(apply(scales, place, sector_target[0], vector, *envs)) + diag * current) * keep
    twice = target_sum(apply(scales, place, sector_target[0], once.astype(BF16), *envs))
    sums = sector_sum(
        spread([jnp.sum(current * current), jnp.sum(current * once), jnp.sum(once * once)])
    )
    vv, vh, hh = sums[0, 0], sums[1, 0], sums[2, 0]
    energy = vh / vv
    factor = jnp.sqrt(cells / (vv + STEP * STEP * jnp.maximum(hh - energy * vh, 0.0)))
    grow, shrink = factor * (1.0 + STEP * energy), factor * STEP

    current, applied = (
        grow * current - shrink * once,
        grow * once - shrink * ((twice + diag * once) * keep),
    )
    mine = spread(
        [jnp.sum(current * current), jnp.sum(current * applied), jnp.sum(applied * applied)]
    )
    everyone = lax.all_to_all(
        jnp.broadcast_to(mine[None], (sectors, 8, 128)), SECTOR, 0, 0, tiled=True
    )
    sums = jnp.sum(everyone, 0)
    vv, vh, hh = sums[0, 0], sums[1, 0], sums[2, 0]
    energy = vh / vv
    factor = jnp.sqrt(cells / (vv + STEP * STEP * jnp.maximum(hh - energy * vh, 0.0)))
    bond = factor * ((1.0 + STEP * energy) * current - STEP * applied)
    return bond.astype(BF16)[None, None], jnp.reshape(energy, (1,))


def solution(mesh):
    shape = (4, 2, 8, 4)
    grid = Mesh(mesh.devices.reshape(shape), ("x", "core", "z", "y"))
    blocks = functools.partial(P, REGION, SECTOR)
    in_specs = (
        blocks(None, None),
        blocks(None, None, None),
        blocks(None, None, None),
        blocks(None, None),
        P(),
        P(),
        P(),
        P(SECTOR, None),
        P(SECTOR),
    )
    out_specs = (blocks(None, None), P(REGION))
    return jax.shard_map(local, mesh=grid, in_specs=in_specs, out_specs=out_specs, check_vma=False)
```

time: 951 us -> 307 us (0.32)
  waiting for transfers between devices: 463 us -> 99 us
  blocking collectives: 365 us -> 18.5 us
  starting transfers between devices: 5.81 us -> 106 us
  matrix products: 58 us -> 0 us
  Pallas kernels: 0 us -> 42.4 us
  local copies, waits for them, and re-layouts: 25.3 us -> 8.77 us
  between operations: 21.5 us -> 11.8 us
    reduce_scatter x2 -> x0, waiting for transfers between devices: 437 us -> none  [local(): lax.psum_scatter(partials.astype(jnp.bfloat16), 'sector', scatter_dimensi...]
    psum x5 -> x0, blocking collectives: 365 us -> none  [the longest x2 146 us: local(): lax.psum((jnp.sum(current * current), jnp.sum(current * applied_h)), 'sec...]
    ppermute x2 -> x26, starting transfers between devices: 5.73 us -> 70.9 us  [the longest x12 30.7 us: along(): lax.ppermute(value, axis, [(i, (i + steps) % count) for i in range(count)])]
    dot_general x8 -> x0, matrix products: 58 us -> none  [the longest x2 20.5 us: local(): jnp.einsum('wt,wil->til', routing, product, precision=lax.Precision.HIGHEST)]
    ppermute x2 -> x26, waiting for transfers between devices: 25.7 us -> 76.5 us  [the longest x12 29.8 us: along(): lax.ppermute(value, axis, [(i, (i + steps) % count) for i in range(count)])]
    pallas_call x0 -> x4, Pallas kernels: none -> 42.4 us  [the longest x2 23.6 us: carry(): pl.pallas_call(carry_kernel, out_shape=jax.ShapeDtypeStruct(env.shape, BF...]
    all_to_all x0 -> x6, starting transfers between devices: none -> 35.1 us  [the longest x2 14.6 us: target_sum(): rows_low = lax.all_to_all(mine_z, Y, 0, 0, tiled=True)]
    all_to_all x0 -> x6, waiting for transfers between devices: none -> 22.5 us  [the longest x2 15.6 us: target_sum(): rows_high = lax.all_to_all(column, Z, 0, 0, tiled=True)]
  transfers between devices with their start and end apart: 4 -> 32, of which waited for: 4 -> 25; matrix products, arithmetic and copies ran while one was open for 2% -> 4% of each run, Pallas kernels for 0% -> 4%
where the time goes in v1:
time: 307 us; the launch traced here: 306 us
  starting transfers between devices  106 us (35%)
  waiting for transfers between devices  99 us (32%)
  Pallas kernels  42.4 us (14%)
  other arithmetic  19.7 us (6%)
  blocking collectives  18.5 us (6%)
  between operations  11.8 us (4%)
  local copies, waits for them, and re-layouts  8.77 us (3%)
    ppermute x12, starting transfers between devices, along(): lax.ppermute(value, axis, [(i, (i + steps) % count) for i in range(count)])  30.7 us
    ppermute x12, waiting for transfers between devices, along(): lax.ppermute(value, axis, [(i, (i + steps) % count) for i in range(count)])  29.8 us
    ppermute x10, starting transfers between devices, exchanged(): return lax.ppermute(value, axis, [(i, i ^ bit) for i in range(count)])  29 us
    ppermute x4, waiting for transfers between devices, to_region(): lax.ppermute(value, REGION, [(i, i + steps) for i in range(leading, last)])  26.3 us
    pallas_call x2, Pallas kernels, carry(): pl.pallas_call(carry_kernel, out_shape=jax.ShapeDtypeStruct(env.shape, BF...  23.6 us
    ppermute x10, waiting for transfers between devices, exchanged(): return lax.ppermute(value, axis, [(i, i ^ bit) for i in range(count)])  20.3 us
    pallas_call x2, Pallas kernels, apply(): pl.pallas_call(apply_kernel, out_shape=[far, far, near, near, near, near,...  18.7 us
    all_to_all x1, blocking collectives, local(): lax.all_to_all(jnp.broadcast_to(mine[None], (sectors, 8, 128)), SECTOR, 0...  18.5 us
  transfers between devices with their start and end apart: 32, of which 25 were waited for; matrix products, arithmetic and copies ran while one was open for 4% of the time, Pallas kernels for 4%

profile of v1, /device:TPU:6, one launch (start us, length us, event | category | flops | bytes accessed | tf_op | source)
XLA Modules:
  0.0 306.2 jit_solution(13478315544624423983)
XLA Ops:
  3.6 1.9 collective-permute-start
  5.5 3.6 %collective-permute-start.1 = (f32[1,128]{1,0:T(1,128)S(1)}, f32[1,128]{1,0:T(1,128)S(1)}, u32[]{:S(2)}, u32[]{:S(2)}) collective-permute-start(f32[1,128]{1,0:T(1,128)S(1)} %broadcast_in_dim.16), channel_id=1, source_target_pairs={{32,0},{64,32},{96,64},{128,96},{160,128},{192,160},{224,192},{33,... | collective-permute-start | bytes 1544 | tf_op jit(solution)/shard_map/ppermute | solution.py:35
  12.1 2.0 collective-permute-done.2
  14.2 3.2 %collective-permute-start.3 = (f32[8,128]{1,0:T(8,128)S(1)}, f32[8,128]{1,0:T(8,128)S(1)}, u32[]{:S(2)}, u32[]{:S(2)}) collective-permute-start(f32[8,128]{1,0:T(8,128)S(1)} %fusion.27), channel_id=1, source_target_pairs={{0,2},{1,3},{2,0},{3,1},{4,6},{5,7},{6,4},{7,5},{8,10},{9,11},{10,... | collective-permute-start | bytes 12296 | tf_op jit(solution)/shard_map/ppermute | solution.py:29
  17.4 1.9 collective-permute-done.3
  19.4 1.9 collective-permute-start.4
  23.1 3.3 %collective-permute-start.5 = (f32[8,128]{1,0:T(8,128)S(1)}, f32[8,128]{1,0:T(8,128)S(1)}, u32[]{:S(2)}, u32[]{:S(2)}) collective-permute-start(f32[8,128]{1,0:T(8,128)S(1)} %add.135), channel_id=1, source_target_pairs={{0,8},{4,12},{8,0},{12,4},{16,24},{20,28},{24,16},{28,20},{1,9},{5... | collective-permute-start | bytes 12296 | tf_op jit(solution)/shard_map/ppermute | solution.py:29
  27.9 6.8 %collective-permute-start.6 = (f32[8,128]{1,0:T(8,128)S(1)}, f32[8,128]{1,0:T(8,128)S(1)}, u32[]{:S(2)}, u32[]{:S(2)}) collective-permute-start(f32[8,128]{1,0:T(8,128)S(1)} %add.136), channel_id=1, source_target_pairs={{0,16},{4,20},{8,24},{12,28},{16,0},{20,4},{24,8},{28,12},{1,17},{... | collective-permute-start | bytes 12296 | tf_op jit(solution)/shard_map/ppermute | solution.py:29
  40.5 11.8 %shard_map.105 = bf16[18,256,256]{2,1,0:T(8,128)(2,1)} custom-call(f32[18,18]{1,0:T(8,128)S(1)} %get-tuple-element.43.mix_ref, bf16[256,256]{1,0:T(8,128)(2,1)S(1)} %copy.13.second_ref.first_ref, bf16[256,256]{1,0:T(8,128)(2,1)S(1)} %get-tuple-element.41.first_ref.second_ref, bf16[18,256,256]{2,1,0:T(8,128)(2,1)S(1)} %bitcast.77), custom_call_target="tpu_custom_call" | custom-call | flops 1207959552 | bytes 4718592 | tf_op jit(solution)/shard_map/pallas_call | solution.py:86
  54.2 11.8 %shard_map.104 = bf16[18,256,256]{2,1,0:T(8,128)(2,1)} custom-call(f32[18,18]{1,0:T(8,128)S(1)} %get-tuple-element.44.mix_ref, bf16[256,256]{1,0:T(8,128)(2,1)S(1)} %get-tuple-element.41.first_ref.second_ref, bf16[256,256]{1,0:T(8,128)(2,1)S(1)} %copy.13.second_ref.first_ref, bf16[18,256,256]{2,1,0:T(8,128)(2,1)S(1)} %bitcast.72), custom_call_target="tpu_custom_call" | custom-call | flops 1207959552 | bytes 4718592 | tf_op jit(solution)/shard_map/pallas_call | solution.py:86
  66.0 3.8 %collective-permute-start.7 = (bf16[18,256,256]{2,1,0:T(8,128)(2,1)}, bf16[18,256,256]{2,1,0:T(8,128)(2,1)}, u32[]{:S(2)}, u32[]{:S(2)}) collective-permute-start(bf16[18,256,256]{2,1,0:T(8,128)(2,1)} %shard_map.104), channel_id=1, source_target_pairs={{0,32},{32,64},{64,96},{96,128},{128,160},{160,192},{192,224},{1,3... | collective-permute-start | bytes 7077896 | tf_op jit(solution)/shard_map/ppermute | solution.py:35
  71.3 9.5 %collective-permute-done.8.right_got = bf16[18,256,256]{2,1,0:T(8,128)(2,1)} collective-permute-done((bf16[18,256,256]{2,1,0:T(8,128)(2,1)}, bf16[18,256,256]{2,1,0:T(8,128)(2,1)}, u32[]{:S(2)}, u32[]{:S(2)}) %collective-permute-start.8) | collective-permute-done | bytes 2359328 | tf_op jit(solution)/shard_map/ppermute | solution.py:35
  80.8 15.7 %collective-permute-done.7.left_got = bf16[18,256,256]{2,1,0:T(8,128)(2,1)} collective-permute-done((bf16[18,256,256]{2,1,0:T(8,128)(2,1)}, bf16[18,256,256]{2,1,0:T(8,128)(2,1)}, u32[]{:S(2)}, u32[]{:S(2)}) %collective-permute-start.7) | collective-permute-done | bytes 2359328 | tf_op jit(solution)/shard_map/ppermute | solution.py:35
  96.5 9.4 %shard_map.106 = (bf16[6,96,256]{2,1,0:T(8,128)(2,1)S(1)}, bf16[6,96,256]{2,1,0:T(8,128)(2,1)S(1)}, bf16[4,96,256]{2,1,0:T(8,128)(2,1)S(1)}, bf16[4,96,256]{2,1,...) custom-call(f32[2]{0:T(128)S(1)} %pad_maximum_fusion.4.scale_ref, ...), custom_call_target="tpu_custom_call" | custom-call | flops 1207959552 | bytes 9437184 | tf_op jit(solution)/shard_map/pallas_call | solution.py:215
  107.3 4.6 %all-to-all-start.1 = ((bf16[4,8,160,256]{3,2,1,0:T(8,128)(2,1)}), bf16[4,8,160,256]{3,2,1,0:T(8,128)(2,1)}, u32[]{:S(2)}, u32[]{:S(2)}) async-start(bf16[4,8,160,256]{3,2,1,0:T(8,128)(2,1)} %get-tuple-element.25), calls=%async_computation.1 | async-start | bytes 5242880 | tf_op jit(solution)/shard_map/all_to_all | solution.py:242
  111.9 2.1 collective-permute-start.9
  114.0 3.2 %collective-permute-start.11 = (bf16[6,96,256]{2,1,0:T(8,128)(2,1)}, bf16[6,96,256]{2,1,0:T(8,128)(2,1)S(1)}, u32[]{:S(2)}, u32[]{:S(2)}) collective-permute-start(bf16[6,96,256]{2,1,0:T(8,128)(2,1)} %copy-done.5), channel_id=1, source_target_pairs={{0,24},{4,28},{8,0},{12,4},{16,8},{20,12},{24,16},{28,20},{1,25},{... | collective-permute-start | bytes 884744 | tf_op jit(solution)/shard_map/ppermute | solution.py:24
  117.2 5.4 %collective-permute-done.9 = bf16[6,96,256]{2,1,0:T(8,128)(2,1)S(1)} collective-permute-done((bf16[6,96,256]{2,1,0:T(8,128)(2,1)}, bf16[6,96,256]{2,1,0:T(8,128)(2,1)S(1)}, u32[]{:S(2)}, u32[]{:S(2)}) %collective-permute-start.9) | collective-permute-done | bytes 294944 | tf_op jit(solution)/shard_map/ppermute | solution.py:24
  122.7 3.6 %collective-permute-start.10 = (bf16[4,96,256]{2,1,0:T(8,128)(2,1)S(1)}, bf16[4,96,256]{2,1,0:T(8,128)(2,1)S(1)}, u32[]{:S(2)}, u32[]{:S(2)}) collective-permute-start(bf16[4,96,256]{2,1,0:T(8,128)(2,1)S(1)} %pad_maximum_fusion), channel_id=1, source_target_pairs={{0,8},{4,12},{8,16},{12,20},{16,24},{20,28},{24,0},{28,4},{1,9},{5... | collective-permute-start | bytes 589832 | tf_op jit(solution)/shard_map/ppermute | solution.py:24
  126.7 2.8 collective-permute-start.12
  130.7 2.3 collective-permute-start.14
  133.0 4.0 %collective-permute-done.12 = bf16[4,96,256]{2,1,0:T(8,128)(2,1)S(1)} collective-permute-done((bf16[4,96,256]{2,1,0:T(8,128)(2,1)S(1)}, bf16[4,96,256]{2,1,0:T(8,128)(2,1)S(1)}, u32[]{:S(2)}, u32[]{:S(2)}) %collective-permute-start.12) | collective-permute-done | bytes 196640 | tf_op jit(solution)/shard_map/ppermute | solution.py:24
  138.5 3.7 %collective-permute-done.14 = bf16[4,96,256]{2,1,0:T(8,128)(2,1)S(1)} collective-permute-done((bf16[4,96,256]{2,1,0:T(8,128)(2,1)S(1)}, bf16[4,96,256]{2,1,0:T(8,128)(2,1)S(1)}, u32[]{:S(2)}, u32[]{:S(2)}) %collective-permute-start.14) | collective-permute-done | bytes 196640 | tf_op jit(solution)/shard_map/ppermute | solution.py:24
  143.0 7.0 %all-to-all-start = ((bf16[4,96,256]{2,1,0:T(8,128)(2,1)}), bf16[4,96,256]{2,1,0:T(8,128)(2,1)S(1)}, u32[]{:S(2)}, u32[]{:S(2)}) async-start(bf16[4,96,256]{2,1,0:T(8,128)(2,1)} %add_convert_fusion.5), calls=%async_computation | async-start | bytes 393216 | tf_op jit(solution)/shard_map/all_to_all | solution.py:257
  150.0 2.9 fusion
  152.8 3.5 %all-to-all-done = bf16[4,96,256]{2,1,0:T(8,128)(2,1)S(1)} async-done(((bf16[4,96,256]{2,1,0:T(8,128)(2,1)}), bf16[4,96,256]{2,1,0:T(8,128)(2,1)S(1)}, u32[]{:S(2)}, u32[]{:S(2)}) %all-to-all-start) | async-done | bytes 196640 | tf_op jit(solution)/shard_map/all_to_all | solution.py:257
  157.0 6.4 %all-to-all-start.2 = ((bf16[8,160,256]{2,1,0:T(8,128)(2,1)}), bf16[8,160,256]{2,1,0:T(8,128)(2,1)S(1)}, u32[]{:S(2)}, u32[]{:S(2)}) async-start(bf16[8,160,256]{2,1,0:T(8,128)(2,1)} %fusion), calls=%async_computation.2 | async-start | bytes 1310720 | tf_op jit(solution)/shard_map/all_to_all | solution.py:258
  164.4 15.6 %all-to-all-done.2 = bf16[8,160,256]{2,1,0:T(8,128)(2,1)S(1)} async-done(((bf16[8,160,256]{2,1,0:T(8,128)(2,1)}), bf16[8,160,256]{2,1,0:T(8,128)(2,1)S(1)}, u32[]{:S(2)}, u32[]{:S(2)}) %all-to-all-start.2) | async-done | bytes 655392 | tf_op jit(solution)/shard_map/all_to_all | solution.py:258
  181.7 9.4 %shard_map.107 = (bf16[6,96,256]{2,1,0:T(8,128)(2,1)S(1)}, bf16[6,96,256]{2,1,0:T(8,128)(2,1)S(1)}, bf16[4,96,256]{2,1,0:T(8,128)(2,1)S(1)}, bf16[4,96,256]{2,1,...) custom-call(f32[2]{0:T(128)S(1)} %pad_maximum_fusion.4.scale_ref, ...), custom_call_target="tpu_custom_call" | custom-call | flops 1207959552 | bytes 9437184 | tf_op jit(solution)/shard_map/pallas_call | solution.py:215
  192.5 5.6 %all-to-all-start.4 = ((bf16[4,8,160,256]{3,2,1,0:T(8,128)(2,1)}), bf16[4,8,160,256]{3,2,1,0:T(8,128)(2,1)}, u32[]{:S(2)}, u32[]{:S(2)}) async-start(bf16[4,8,160,256]{3,2,1,0:T(8,128)(2,1)} %get-tuple-element.33), calls=%async_computation.4 | async-start | bytes 5242880 | tf_op jit(solution)/shard_map/all_to_all | solution.py:242
  198.1 3.3 %collective-permute-start.20 = (bf16[6,96,256]{2,1,0:T(8,128)(2,1)S(1)}, bf16[6,96,256]{2,1,0:T(8,128)(2,1)S(1)}, u32[]{:S(2)}, u32[]{:S(2)}) collective-permute-start(bf16[6,96,256]{2,1,0:T(8,128)(2,1)S(1)} %copy-done.7), channel_id=1, source_target_pairs={{0,8},{4,12},{8,16},{12,20},{16,24},{20,28},{24,0},{28,4},{1,9},{5... | collective-permute-start | bytes 884744 | tf_op jit(solution)/shard_map/ppermute | solution.py:24
  202.4 5.9 %collective-permute-done.20 = bf16[6,96,256]{2,1,0:T(8,128)(2,1)S(1)} collective-permute-done((bf16[6,96,256]{2,1,0:T(8,128)(2,1)S(1)}, bf16[6,96,256]{2,1,0:T(8,128)(2,1)S(1)}, u32[]{:S(2)}, u32[]{:S(2)}) %collective-permute-start.20) | collective-permute-done | bytes 294944 | tf_op jit(solution)/shard_map/ppermute | solution.py:24
  209.4 3.3 %collective-permute-done.22 = bf16[6,96,256]{2,1,0:T(8,128)(2,1)S(1)} collective-permute-done((bf16[6,96,256]{2,1,0:T(8,128)(2,1)S(1)}, bf16[6,96,256]{2,1,0:T(8,128)(2,1)S(1)}, u32[]{:S(2)}, u32[]{:S(2)}) %collective-permute-start.22) | collective-permute-done | bytes 294944 | tf_op jit(solution)/shard_map/ppermute | solution.py:24
  212.9 10.2 %collective-permute-start.24 = (bf16[4,96,256]{2,1,0:T(8,128)(2,1)S(1)}, bf16[4,96,256]{2,1,0:T(8,128)(2,1)S(1)}, u32[]{:S(2)}, u32[]{:S(2)}) collective-permute-start(bf16[4,96,256]{2,1,0:T(8,128)(2,1)S(1)} %add_convert_fusion.4), channel_id=1, source_target_pairs={{0,4},{4,8},{8,12},{12,16},{16,20},{20,24},{24,28},{28,0},{1,5},{5... | collective-permute-start | bytes 589832 | tf_op jit(solution)/shard_map/ppermute | solution.py:24
  223.3 3.0 collective-permute-done.24
  226.4 2.6 collective-permute-done.25
  229.8 7.6 %all-to-all-start.3 = ((bf16[4,96,256]{2,1,0:T(8,128)(2,1)}), bf16[4,96,256]{2,1,0:T(8,128)(2,1)S(1)}, u32[]{:S(2)}, u32[]{:S(2)}) async-start(bf16[4,96,256]{2,1,0:T(8,128)(2,1)} %add_convert_fusion.2), calls=%async_computation.3 | async-start | bytes 393216 | tf_op jit(solution)/shard_map/all_to_all | solution.py:257
  237.4 2.9 fusion.1
  240.3 3.5 %all-to-all-done.3 = bf16[4,96,256]{2,1,0:T(8,128)(2,1)S(1)} async-done(((bf16[4,96,256]{2,1,0:T(8,128)(2,1)}), bf16[4,96,256]{2,1,0:T(8,128)(2,1)S(1)}, u32[]{:S(2)}, u32[]{:S(2)}) %all-to-all-start.3) | async-done | bytes 196640 | tf_op jit(solution)/shard_map/all_to_all | solution.py:257
  243.7 3.9 %all-to-all-start.5 = ((bf16[8,160,256]{2,1,0:T(8,128)(2,1)}), bf16[8,160,256]{2,1,0:T(8,128)(2,1)S(1)}, u32[]{:S(2)}, u32[]{:S(2)}) async-start(bf16[8,160,256]{2,1,0:T(8,128)(2,1)} %fusion.1), calls=%async_computation.5 | async-start | bytes 1310720 | tf_op jit(solution)/shard_map/all_to_all | solution.py:258
  247.6 2.1 maximum_maximum_fusion.2
  250.3 3.0 collective-permute-done.15
  254.2 4.4 %collective-permute-done.16 = f32[8,128]{1,0:T(8,128)S(1)} collective-permute-done((f32[8,128]{1,0:T(8,128)S(1)}, f32[8,128]{1,0:T(8,128)S(1)}, u32[]{:S(2)}, u32[]{:S(2)}) %collective-permute-start.16) | collective-permute-done | bytes 4128 | tf_op jit(solution)/shard_map/ppermute | solution.py:29
  258.6 2.0 collective-permute-start.17
  262.2 2.9 collective-permute-start.18
  266.8 5.9 %collective-permute-start.19 = (f32[8,128]{1,0:T(8,128)S(1)}, f32[8,128]{1,0:T(8,128)S(1)}, u32[]{:S(2)}, u32[]{:S(2)}) collective-permute-start(f32[8,128]{1,0:T(8,128)S(1)} %add.155), channel_id=1, source_target_pairs={{0,16},{4,20},{8,24},{12,28},{16,0},{20,4},{24,8},{28,12},{1,17},{... | collective-permute-start | bytes 12296 | tf_op jit(solution)/shard_map/ppermute | solution.py:29
  279.3 2.0 maximum_maximum_fusion.1
  281.5 18.5 %all_to_all.35 = f32[32,8,128]{2,1,0:T(8,128)S(1)} all-to-all(f32[32,8,128]{2,1,0:T(8,128)S(1)} %broadcast_in_dim.23), channel_id=1, replica_groups=mesh['x'=4,'core'=2,'z'=8,'y'=4] {'z','y'}, dimensions={0} | all-to-all | bytes 262144 | tf_op jit(solution)/shard_map/all_to_all | solution.py:326
  (116 shorter events, 38.6 us)
Async XLA Ops:
  3.6 5.7 %collective-permute-start = (f32[1,128]{1,0:T(1,128)S(1)}, f32[1,128]{1,0:T(1,128)S(1)}, u32[]{:S(2)}, u32[]{:S(2)}) collective-permute-start(f32[1,128]{1,0:T(1,128)S(1)} %broadcast_in_dim.16), channel_id=1, source_target_pairs={{0,32},{32,64},{64,96},{96,128},{128,160},{160,192},{192,224},{1,3... | collective-permute-start | bytes 1544 | tf_op jit(solution)/shard_map/ppermute | solution.py:35
  5.5 4.9 %collective-permute-start.1 = (f32[1,128]{1,0:T(1,128)S(1)}, f32[1,128]{1,0:T(1,128)S(1)}, u32[]{:S(2)}, u32[]{:S(2)}) collective-permute-start(f32[1,128]{1,0:T(1,128)S(1)} %broadcast_in_dim.16), channel_id=1, source_target_pairs={{32,0},{64,32},{96,64},{128,96},{160,128},{192,160},{224,192},{33,... | collective-permute-start | bytes 1544 | tf_op jit(solution)/shard_map/ppermute | solution.py:35
  10.5 3.6 %collective-permute-start.2 = (f32[8,128]{1,0:T(8,128)S(1)}, f32[8,128]{1,0:T(8,128)S(1)}, u32[]{:S(2)}, u32[]{:S(2)}) collective-permute-start(f32[8,128]{1,0:T(8,128)S(1)} %maximum_maximum_fusion), channel_id=1, source_target_pairs={{0,1},{1,0},{2,3},{3,2},{4,5},{5,4},{6,7},{7,6},{8,9},{9,8},{10,11... | collective-permute-start | bytes 12296 | tf_op jit(solution)/shard_map/ppermute | solution.py:29
  14.2 5.1 %collective-permute-start.3 = (f32[8,128]{1,0:T(8,128)S(1)}, f32[8,128]{1,0:T(8,128)S(1)}, u32[]{:S(2)}, u32[]{:S(2)}) collective-permute-start(f32[8,128]{1,0:T(8,128)S(1)} %fusion.27), channel_id=1, source_target_pairs={{0,2},{1,3},{2,0},{3,1},{4,6},{5,7},{6,4},{7,5},{8,10},{9,11},{10,... | collective-permute-start | bytes 12296 | tf_op jit(solution)/shard_map/ppermute | solution.py:29
  19.4 3.6 %collective-permute-start.4 = (f32[8,128]{1,0:T(8,128)S(1)}, f32[8,128]{1,0:T(8,128)S(1)}, u32[]{:S(2)}, u32[]{:S(2)}) collective-permute-start(f32[8,128]{1,0:T(8,128)S(1)} %fusion.32), channel_id=1, source_target_pairs={{0,4},{4,0},{8,12},{12,8},{16,20},{20,16},{24,28},{28,24},{1,5},{5... | collective-permute-start | bytes 12296 | tf_op jit(solution)/shard_map/ppermute | solution.py:29
  23.1 4.9 %collective-permute-start.5 = (f32[8,128]{1,0:T(8,128)S(1)}, f32[8,128]{1,0:T(8,128)S(1)}, u32[]{:S(2)}, u32[]{:S(2)}) collective-permute-start(f32[8,128]{1,0:T(8,128)S(1)} %add.135), channel_id=1, source_target_pairs={{0,8},{4,12},{8,0},{12,4},{16,24},{20,28},{24,16},{28,20},{1,9},{5... | collective-permute-start | bytes 12296 | tf_op jit(solution)/shard_map/ppermute | solution.py:29
  27.9 8.4 %collective-permute-start.6 = (f32[8,128]{1,0:T(8,128)S(1)}, f32[8,128]{1,0:T(8,128)S(1)}, u32[]{:S(2)}, u32[]{:S(2)}) collective-permute-start(f32[8,128]{1,0:T(8,128)S(1)} %add.136), channel_id=1, source_target_pairs={{0,16},{4,20},{8,24},{12,28},{16,0},{20,4},{24,8},{28,12},{1,17},{... | collective-permute-start | bytes 12296 | tf_op jit(solution)/shard_map/ppermute | solution.py:29
  38.8 1.7 copy-start.1
  40.5 13.7 %copy-start = (bf16[1,1,18,256,256]{4,3,2,1,0:T(8,128)(2,1)S(1)}, bf16[1,1,18,256,256]{4,3,2,1,0:T(8,128)(2,1)}, u32[]{:S(2)}) copy-start(bf16[1,1,18,256,256]{4,3,2,1,0:T(8,128)(2,1)} %param.10) | copy-start | bytes 7077892
  52.3 28.6 %collective-permute-start.8 = (bf16[18,256,256]{2,1,0:T(8,128)(2,1)}, bf16[18,256,256]{2,1,0:T(8,128)(2,1)}, u32[]{:S(2)}, u32[]{:S(2)}) collective-permute-start(bf16[18,256,256]{2,1,0:T(8,128)(2,1)} %shard_map.105), channel_id=1, source_target_pairs={{32,0},{64,32},{96,64},{128,96},{160,128},{192,160},{224,192},{33,... | collective-permute-start | bytes 7077896 | tf_op jit(solution)/shard_map/ppermute | solution.py:35
  54.2 42.3 %copy-start.2 = (s32[1,18]{1,0:T(1,128)S(1)}, s32[1,18]{1,0:T(1,128)}, u32[]{:S(2)}) copy-start(s32[1,18]{1,0:T(1,128)} %param.16) | copy-start | bytes 220
  66.0 30.5 %collective-permute-start.7 = (bf16[18,256,256]{2,1,0:T(8,128)(2,1)}, bf16[18,256,256]{2,1,0:T(8,128)(2,1)}, u32[]{:S(2)}, u32[]{:S(2)}) collective-permute-start(bf16[18,256,256]{2,1,0:T(8,128)(2,1)} %shard_map.104), channel_id=1, source_target_pairs={{0,32},{32,64},{64,96},{96,128},{128,160},{160,192},{192,224},{1,3... | collective-permute-start | bytes 7077896 | tf_op jit(solution)/shard_map/ppermute | solution.py:35
  105.9 0.8 copy-start.5
  106.6 0.7 copy-start.8
  107.3 35.6 %all-to-all-start.1 = ((bf16[4,8,160,256]{3,2,1,0:T(8,128)(2,1)}), bf16[4,8,160,256]{3,2,1,0:T(8,128)(2,1)}, u32[]{:S(2)}, u32[]{:S(2)}) async-start(bf16[4,8,160,256]{3,2,1,0:T(8,128)(2,1)} %get-tuple-element.25), calls=%async_computation.1 | async-start | bytes 5242880 | tf_op jit(solution)/shard_map/all_to_all | solution.py:242
  111.9 10.7 %collective-permute-start.9 = (bf16[6,96,256]{2,1,0:T(8,128)(2,1)}, bf16[6,96,256]{2,1,0:T(8,128)(2,1)S(1)}, u32[]{:S(2)}, u32[]{:S(2)}) collective-permute-start(bf16[6,96,256]{2,1,0:T(8,128)(2,1)} %copy-done.8), channel_id=1, source_target_pairs={{0,8},{4,12},{8,16},{12,20},{16,24},{20,28},{24,0},{28,4},{1,9},{5... | collective-permute-start | bytes 884744 | tf_op jit(solution)/shard_map/ppermute | solution.py:24
  114.0 12.7 %collective-permute-start.11 = (bf16[6,96,256]{2,1,0:T(8,128)(2,1)}, bf16[6,96,256]{2,1,0:T(8,128)(2,1)S(1)}, u32[]{:S(2)}, u32[]{:S(2)}) collective-permute-start(bf16[6,96,256]{2,1,0:T(8,128)(2,1)} %copy-done.5), channel_id=1, source_target_pairs={{0,24},{4,28},{8,0},{12,4},{16,8},{20,12},{24,16},{28,20},{1,25},{... | collective-permute-start | bytes 884744 | tf_op jit(solution)/shard_map/ppermute | solution.py:24
  122.7 10.4 %collective-permute-start.10 = (bf16[4,96,256]{2,1,0:T(8,128)(2,1)S(1)}, bf16[4,96,256]{2,1,0:T(8,128)(2,1)S(1)}, u32[]{:S(2)}, u32[]{:S(2)}) collective-permute-start(bf16[4,96,256]{2,1,0:T(8,128)(2,1)S(1)} %pad_maximum_fusion), channel_id=1, source_target_pairs={{0,8},{4,12},{8,16},{12,20},{16,24},{20,28},{24,0},{28,4},{1,9},{5... | collective-permute-start | bytes 589832 | tf_op jit(solution)/shard_map/ppermute | solution.py:24
  126.7 10.3 %collective-permute-start.12 = (bf16[4,96,256]{2,1,0:T(8,128)(2,1)S(1)}, bf16[4,96,256]{2,1,0:T(8,128)(2,1)S(1)}, u32[]{:S(2)}, u32[]{:S(2)}) collective-permute-start(bf16[4,96,256]{2,1,0:T(8,128)(2,1)S(1)} %pad_maximum_fusion.1), channel_id=1, source_target_pairs={{0,24},{4,28},{8,0},{12,4},{16,8},{20,12},{24,16},{28,20},{1,25},{... | collective-permute-start | bytes 589832 | tf_op jit(solution)/shard_map/ppermute | solution.py:24
  129.6 8.9 %collective-permute-start.13 = (bf16[4,96,256]{2,1,0:T(8,128)(2,1)S(1)}, bf16[4,96,256]{2,1,0:T(8,128)(2,1)S(1)}, u32[]{:S(2)}, u32[]{:S(2)}) collective-permute-start(bf16[4,96,256]{2,1,0:T(8,128)(2,1)S(1)} %add_convert_fusion.7), channel_id=1, source_target_pairs={{0,4},{4,8},{8,12},{12,16},{16,20},{20,24},{24,28},{28,0},{1,5},{5... | collective-permute-start | bytes 589832 | tf_op jit(solution)/shard_map/ppermute | solution.py:24
  130.7 11.4 %collective-permute-start.14 = (bf16[4,96,256]{2,1,0:T(8,128)(2,1)S(1)}, bf16[4,96,256]{2,1,0:T(8,128)(2,1)S(1)}, u32[]{:S(2)}, u32[]{:S(2)}) collective-permute-start(bf16[4,96,256]{2,1,0:T(8,128)(2,1)S(1)} %add_convert_fusion.6), channel_id=1, source_target_pairs={{0,28},{4,0},{8,4},{12,8},{16,12},{20,16},{24,20},{28,24},{1,29},{... | collective-permute-start | bytes 589832 | tf_op jit(solution)/shard_map/ppermute | solution.py:24
  143.0 13.4 %all-to-all-start = ((bf16[4,96,256]{2,1,0:T(8,128)(2,1)}), bf16[4,96,256]{2,1,0:T(8,128)(2,1)S(1)}, u32[]{:S(2)}, u32[]{:S(2)}) async-start(bf16[4,96,256]{2,1,0:T(8,128)(2,1)} %add_convert_fusion.5), calls=%async_computation | async-start | bytes 393216 | tf_op jit(solution)/shard_map/all_to_all | solution.py:257
  152.8 27.2 %copy-start.14 = (bf16[1,1,256,256]{3,2,1,0:T(8,128)(2,1)S(1)}, bf16[1,1,256,256]{3,2,1,0:T(8,128)(2,1)}, u32[]{:S(2)}) copy-start(bf16[1,1,256,256]{3,2,1,0:T(8,128)(2,1)} %param.12) | copy-start | bytes 393220
  157.0 23.0 %all-to-all-start.2 = ((bf16[8,160,256]{2,1,0:T(8,128)(2,1)}), bf16[8,160,256]{2,1,0:T(8,128)(2,1)S(1)}, u32[]{:S(2)}, u32[]{:S(2)}) async-start(bf16[8,160,256]{2,1,0:T(8,128)(2,1)} %fusion), calls=%async_computation.2 | async-start | bytes 1310720 | tf_op jit(solution)/shard_map/all_to_all | solution.py:258
  164.4 16.6 %copy-start.16 = (f32[96,256]{1,0:T(8,128)}, f32[96,256]{1,0:T(8,128)S(1)}, u32[]{:S(2)}) copy-start(f32[96,256]{1,0:T(8,128)S(1)} %convert_reduce_fusion.3) | copy-start | bytes 294916
  180.1 0.9 copy-start.11
  191.0 0.7 copy-start.3
  192.5 5.6 %copy-start.7 = (bf16[6,96,256]{2,1,0:T(8,128)(2,1)S(1)}, bf16[6,96,256]{2,1,0:T(8,128)(2,1)}, u32[]{:S(2)}) copy-start(bf16[6,96,256]{2,1,0:T(8,128)(2,1)} %copy-done.6) | copy-start | bytes 884740
  192.5 9.0 %copy-start.4 = (bf16[6,96,256]{2,1,0:T(8,128)(2,1)S(1)}, bf16[6,96,256]{2,1,0:T(8,128)(2,1)}, u32[]{:S(2)}) copy-start(bf16[6,96,256]{2,1,0:T(8,128)(2,1)} %copy-done.3) | copy-start | bytes 884740
  192.5 37.3 %all-to-all-start.4 = ((bf16[4,8,160,256]{3,2,1,0:T(8,128)(2,1)}), bf16[4,8,160,256]{3,2,1,0:T(8,128)(2,1)}, u32[]{:S(2)}, u32[]{:S(2)}) async-start(bf16[4,8,160,256]{3,2,1,0:T(8,128)(2,1)} %get-tuple-element.33), calls=%async_computation.4 | async-start | bytes 5242880 | tf_op jit(solution)/shard_map/all_to_all | solution.py:242
  198.1 10.1 %collective-permute-start.20 = (bf16[6,96,256]{2,1,0:T(8,128)(2,1)S(1)}, bf16[6,96,256]{2,1,0:T(8,128)(2,1)S(1)}, u32[]{:S(2)}, u32[]{:S(2)}) collective-permute-start(bf16[6,96,256]{2,1,0:T(8,128)(2,1)S(1)} %copy-done.7), channel_id=1, source_target_pairs={{0,8},{4,12},{8,16},{12,20},{16,24},{20,28},{24,0},{28,4},{1,9},{5... | collective-permute-start | bytes 884744 | tf_op jit(solution)/shard_map/ppermute | solution.py:24
  201.5 11.2 %collective-permute-start.22 = (bf16[6,96,256]{2,1,0:T(8,128)(2,1)S(1)}, bf16[6,96,256]{2,1,0:T(8,128)(2,1)S(1)}, u32[]{:S(2)}, u32[]{:S(2)}) collective-permute-start(bf16[6,96,256]{2,1,0:T(8,128)(2,1)S(1)} %copy-done.4), channel_id=1, source_target_pairs={{0,24},{4,28},{8,0},{12,4},{16,8},{20,12},{24,16},{28,20},{1,25},{... | collective-permute-start | bytes 884744 | tf_op jit(solution)/shard_map/ppermute | solution.py:24
  208.3 15.0 %collective-permute-start.21 = (bf16[4,96,256]{2,1,0:T(8,128)(2,1)S(1)}, bf16[4,96,256]{2,1,0:T(8,128)(2,1)S(1)}, u32[]{:S(2)}, u32[]{:S(2)}) collective-permute-start(bf16[4,96,256]{2,1,0:T(8,128)(2,1)S(1)} %pad_maximum_fusion.2), channel_id=1, source_target_pairs={{0,8},{4,12},{8,16},{12,20},{16,24},{20,28},{24,0},{28,4},{1,9},{5... | collective-permute-start | bytes 589832 | tf_op jit(solution)/shard_map/ppermute | solution.py:24
  212.8 10.6 %collective-permute-start.23 = (bf16[4,96,256]{2,1,0:T(8,128)(2,1)S(1)}, bf16[4,96,256]{2,1,0:T(8,128)(2,1)S(1)}, u32[]{:S(2)}, u32[]{:S(2)}) collective-permute-start(bf16[4,96,256]{2,1,0:T(8,128)(2,1)S(1)} %pad_maximum_fusion.3), channel_id=1, source_target_pairs={{0,24},{4,28},{8,0},{12,4},{16,8},{20,12},{24,16},{28,20},{1,25},{... | collective-permute-start | bytes 589832 | tf_op jit(solution)/shard_map/ppermute | solution.py:24
  212.9 13.4 %collective-permute-start.24 = (bf16[4,96,256]{2,1,0:T(8,128)(2,1)S(1)}, bf16[4,96,256]{2,1,0:T(8,128)(2,1)S(1)}, u32[]{:S(2)}, u32[]{:S(2)}) collective-permute-start(bf16[4,96,256]{2,1,0:T(8,128)(2,1)S(1)} %add_convert_fusion.4), channel_id=1, source_target_pairs={{0,4},{4,8},{8,12},{12,16},{16,20},{20,24},{24,28},{28,0},{1,5},{5... | collective-permute-start | bytes 589832 | tf_op jit(solution)/shard_map/ppermute | solution.py:24
  223.2 5.7 %collective-permute-start.25 = (bf16[4,96,256]{2,1,0:T(8,128)(2,1)S(1)}, bf16[4,96,256]{2,1,0:T(8,128)(2,1)S(1)}, u32[]{:S(2)}, u32[]{:S(2)}) collective-permute-start(bf16[4,96,256]{2,1,0:T(8,128)(2,1)S(1)} %add_convert_fusion.3), channel_id=1, source_target_pairs={{0,28},{4,0},{8,4},{12,8},{16,12},{20,16},{24,20},{28,24},{1,29},{... | collective-permute-start | bytes 589832 | tf_op jit(solution)/shard_map/ppermute | solution.py:24
  229.8 13.9 %all-to-all-start.3 = ((bf16[4,96,256]{2,1,0:T(8,128)(2,1)}), bf16[4,96,256]{2,1,0:T(8,128)(2,1)S(1)}, u32[]{:S(2)}, u32[]{:S(2)}) async-start(bf16[4,96,256]{2,1,0:T(8,128)(2,1)} %add_convert_fusion.2), calls=%async_computation.3 | async-start | bytes 393216 | tf_op jit(solution)/shard_map/all_to_all | solution.py:257
  240.3 38.2 %copy-start.10 = (f32[256,256]{1,0:T(8,128)S(1)}, f32[256,256]{1,0:T(8,128)}, u32[]{:S(2)}) copy-start(f32[256,256]{1,0:T(8,128)} %copy-done.9) | copy-start | bytes 786436
  240.3 38.2 %copy-start.15 = (bf16[1,1,256,256]{3,2,1,0:T(8,128)(2,1)S(1)}, bf16[1,1,256,256]{3,2,1,0:T(8,128)(2,1)}, u32[]{:S(2)}) copy-start(bf16[1,1,256,256]{3,2,1,0:T(8,128)(2,1)} %param.12) | copy-start | bytes 393220
  243.7 34.6 %all-to-all-start.5 = ((bf16[8,160,256]{2,1,0:T(8,128)(2,1)}), bf16[8,160,256]{2,1,0:T(8,128)(2,1)S(1)}, u32[]{:S(2)}, u32[]{:S(2)}) async-start(bf16[8,160,256]{2,1,0:T(8,128)(2,1)} %fusion.1), calls=%async_computation.5 | async-start | bytes 1310720 | tf_op jit(solution)/shard_map/all_to_all | solution.py:258
  247.6 56.5 %copy-start.12 = (f32[160,256]{1,0:T(8,128)S(1)}, f32[160,256]{1,0:T(8,128)}, u32[]{:S(2)}) copy-start(f32[160,256]{1,0:T(8,128)} %copy-done.11) | copy-start | bytes 491524
  247.6 56.5 %copy-start.13 = (bf16[1,1,256,256]{3,2,1,0:T(8,128)(2,1)S(1)}, bf16[1,1,256,256]{3,2,1,0:T(8,128)(2,1)}, u32[]{:S(2)}) copy-start(bf16[1,1,256,256]{3,2,1,0:T(8,128)(2,1)} %param.9) | copy-start | bytes 393220
  247.6 56.5 %copy-start.17 = (f32[96,256]{1,0:T(8,128)S(1)}, f32[96,256]{1,0:T(8,128)}, u32[]{:S(2)}) copy-start(f32[96,256]{1,0:T(8,128)} %copy-done.16) | copy-start | bytes 294916
  249.8 3.6 %collective-permute-start.15 = (f32[8,128]{1,0:T(8,128)S(1)}, f32[8,128]{1,0:T(8,128)S(1)}, u32[]{:S(2)}, u32[]{:S(2)}) collective-permute-start(f32[8,128]{1,0:T(8,128)S(1)} %broadcast.95), channel_id=1, source_target_pairs={{0,1},{1,0},{2,3},{3,2},{4,5},{5,4},{6,7},{7,6},{8,9},{9,8},{10,11... | collective-permute-start | bytes 12296 | tf_op jit(solution)/shard_map/ppermute | solution.py:29
  253.5 5.1 %collective-permute-start.16 = (f32[8,128]{1,0:T(8,128)S(1)}, f32[8,128]{1,0:T(8,128)S(1)}, u32[]{:S(2)}, u32[]{:S(2)}) collective-permute-start(f32[8,128]{1,0:T(8,128)S(1)} %broadcast_add_fusion), channel_id=1, source_target_pairs={{0,2},{1,3},{2,0},{3,1},{4,6},{5,7},{6,4},{7,5},{8,10},{9,11},{10,... | collective-permute-start | bytes 12296 | tf_op jit(solution)/shard_map/ppermute | solution.py:29
  258.6 3.6 %collective-permute-start.17 = (f32[8,128]{1,0:T(8,128)S(1)}, f32[8,128]{1,0:T(8,128)S(1)}, u32[]{:S(2)}, u32[]{:S(2)}) collective-permute-start(f32[8,128]{1,0:T(8,128)S(1)} %fusion.31), channel_id=1, source_target_pairs={{0,4},{4,0},{8,12},{12,8},{16,20},{20,16},{24,28},{28,24},{1,5},{5... | collective-permute-start | bytes 12296 | tf_op jit(solution)/shard_map/ppermute | solution.py:29
  262.2 4.5 %collective-permute-start.18 = (f32[8,128]{1,0:T(8,128)S(1)}, f32[8,128]{1,0:T(8,128)S(1)}, u32[]{:S(2)}, u32[]{:S(2)}) collective-permute-start(f32[8,128]{1,0:T(8,128)S(1)} %add.154), channel_id=1, source_target_pairs={{0,8},{4,12},{8,0},{12,4},{16,24},{20,28},{24,16},{28,20},{1,9},{5... | collective-permute-start | bytes 12296 | tf_op jit(solution)/shard_map/ppermute | solution.py:29
  266.8 7.5 %collective-permute-start.19 = (f32[8,128]{1,0:T(8,128)S(1)}, f32[8,128]{1,0:T(8,128)S(1)}, u32[]{:S(2)}, u32[]{:S(2)}) collective-permute-start(f32[8,128]{1,0:T(8,128)S(1)} %add.155), channel_id=1, source_target_pairs={{0,16},{4,20},{8,24},{12,28},{16,0},{20,4},{24,8},{28,12},{1,17},{... | collective-permute-start | bytes 12296 | tf_op jit(solution)/shard_map/ppermute | solution.py:29
  (3 other events, 2.1 us)

commit v2 on v0

v2 whole, which is shorter than its diff:
```python
import functools
import math

import jax
import jax.numpy as jnp
from jax import lax
from jax.experimental import pallas as pl
from jax.experimental.pallas import tpu as pltpu
from jax.sharding import Mesh
from jax.sharding import PartitionSpec as P

STEP = 0.5
Z_ROWS = 128
CHUNK = 8
F32 = jnp.float32
BF16 = jnp.bfloat16
Z, Y = "z", "y"
REGION = ("x", "core")
SECTOR = ("z", "y")
SMEM_SPEC = pl.BlockSpec(memory_space=pltpu.SMEM)
VMEM_SPEC = pl.BlockSpec(memory_space=pltpu.VMEM)
HBM_SPEC = pl.BlockSpec(memory_space=pltpu.HBM)
MIB = 1024 * 1024
CARRY_PARAMS = pltpu.CompilerParams(vmem_limit_bytes=20 * MIB)
APPLY_PARAMS = pltpu.CompilerParams(vmem_limit_bytes=16 * MIB)
SMALL_PARAMS = pltpu.CompilerParams(vmem_limit_bytes=8 * MIB)


def along(value, axis, steps):
    count = lax.axis_size(axis)
    return lax.ppermute(value, axis, [(i, (i + steps) % count) for i in range(count)])


def to_region(value, steps):
    count = lax.axis_size(REGION)
    leading, last = (max(0, -steps), min(count, count - steps))
    return lax.ppermute(value, REGION, [(i, i + steps) for i in range(leading, last)])


def in_hbm(value):
    return pltpu.with_memory_space_constraint(value, pltpu.HBM)


def add(*terms):
    total = terms[0].astype(F32)
    for term in terms[1:]:
        total = total + term.astype(F32)
    return total.astype(BF16)


def after(value, *others):
    return lax.optimization_barrier((value, *others))[0]


def live(size, width):
    rows = lax.broadcasted_iota(jnp.int32, (width, width), 0) < size
    return rows & (lax.broadcasted_iota(jnp.int32, (width, width), 1) < size)


def spread_mix(coeff):
    count = coeff.shape[0]
    size = count * CHUNK

    def one_hot(shape, dim):
        at = lax.broadcasted_iota(jnp.int32, shape, dim) // CHUNK
        return (at == lax.broadcasted_iota(jnp.int32, shape, 1 - dim)).astype(F32).astype(BF16)

    down, across = one_hot((size, count), 0), one_hot((count, size), 1)
    rows = lax.broadcasted_iota(jnp.int32, (size, size), 0) % CHUNK
    same = rows == lax.broadcasted_iota(jnp.int32, (size, size), 1) % CHUNK
    high = coeff.astype(BF16)
    parts = []
    for part in (high, (coeff - high.astype(F32)).astype(BF16)):
        tall = jnp.dot(down, part, preferred_element_type=F32).astype(BF16)
        wide = jnp.dot(tall, across, preferred_element_type=F32)
        parts.append(jnp.where(same, wide, 0.0).astype(BF16))
    return jnp.concatenate(parts, 0)


def carry_kernel(
    flip, size_ref, coeff_ref, pattern_ref, psi_ref, source, target,
    env_ref, out_ref, mix_ref, first_ref, second_ref, half_ref, mixed_ref, in_sem, out_sem,
):
    count, width, _ = env_ref.shape
    pairs, chunks = count // 2, width // CHUNK
    for pair in range(pairs):
        two = pl.ds(2 * pair, 2)
        pltpu.make_async_copy(source.at[two], env_ref.at[two], in_sem.at[pair]).start()
    masked = jnp.where(live(size_ref[0], width), psi_ref[...].astype(F32), 0.0)
    turned = masked.T
    first_ref[...] = (turned if flip else masked).astype(BF16)
    second_ref[...] = (masked if flip else turned).astype(BF16)
    mix_ref[...] = spread_mix(coeff_ref[...] * pattern_ref[...].astype(F32))
    group = 3 if pairs % 3 == 0 else 1

    @pl.loop(0, pairs // group)
    def _(step):
        for lane in range(group):
            pair = step * group + lane
            two = pl.ds(2 * pair, 2)
            pltpu.make_async_copy(source.at[two], env_ref.at[two], in_sem.at[pair]).wait()
        for lane in range(group):
            pair = step * group + lane
            both = [
                jnp.dot(env_ref[2 * pair + k], first_ref[...], preferred_element_type=F32).reshape(
                    chunks, CHUNK, width
                )
                for k in range(2)
            ]
            half_ref[:, pl.ds(pair, 1)] = (
                jnp.concatenate(both, 1).astype(BF16).reshape(chunks, 1, 2 * CHUNK, width)
            )

    size = count * CHUNK
    unroll = 2

    @pl.loop(0, chunks // (2 * unroll))
    def _(step):
        for lane in range(unroll):
            two = step * unroll + lane
            both = []
            for k in range(2):
                product = jnp.dot(
                    mix_ref[...],
                    half_ref[2 * two + k].reshape(size, width),
                    preferred_element_type=F32,
                )
                both.append((product[:size] + product[size:]).reshape(count, CHUNK, width))
            rows = pl.ds(pl.multiple_of(two * 2 * CHUNK, 2 * CHUNK), 2 * CHUNK)
            mixed_ref[:, rows, :] = jnp.concatenate(both, 1).astype(BF16)

    group = 6 if count % 6 == 0 else 1

    @pl.loop(0, count // group)
    def _(step):
        for lane in range(group):
            v = step * group + lane
            out_ref[v] = jnp.dot(
                second_ref[...], mixed_ref[v], preferred_element_type=F32
            ).astype(BF16)
        done = pl.ds(step * group, group)
        pltpu.make_async_copy(out_ref.at[done], target.at[done], out_sem.at[step]).start()

    for step in range(count // group):
        done = pl.ds(step * group, group)
        pltpu.make_async_copy(out_ref.at[done], target.at[done], out_sem.at[step]).wait()


def carry(flip, size, coeff, pattern, psi, env):
    count, width, _ = env.shape
    chunks = width // CHUNK
    return pl.pallas_call(
        functools.partial(carry_kernel, flip),
        out_shape=jax.ShapeDtypeStruct(env.shape, BF16),
        in_specs=[SMEM_SPEC] + [pl.BlockSpec()] * 3 + [HBM_SPEC],
        out_specs=HBM_SPEC,
        scratch_shapes=[
            pltpu.VMEM(env.shape, BF16),
            pltpu.VMEM(env.shape, BF16),
            pltpu.VMEM((2 * count * CHUNK, count * CHUNK), BF16),
            pltpu.VMEM((width, width), BF16),
            pltpu.VMEM((width, width), BF16),
            pltpu.VMEM((chunks, count // 2, 2 * CHUNK, width), BF16),
            pltpu.VMEM((count, width, width), BF16),
            pltpu.SemaphoreType.DMA((count // 2,)),
            pltpu.SemaphoreType.DMA((count,)),
        ],
        compiler_params=CARRY_PARAMS,
        cost_estimate=pl.CostEstimate(
            flops=8 * count * width**3, bytes_accessed=4 * count * width**2, transcendentals=0
        ),
    )(size, *map(in_hbm, (coeff, pattern, psi, env)))


def slot_table(slot):
    at = jnp.arange(slot.shape[0], dtype=jnp.int32)
    before = (slot[None, :] < slot[:, None]) | (
        (slot[None, :] == slot[:, None]) & (at[None, :] < at[:, None])
    )
    rank = jnp.sum(before.astype(jnp.int32), 1)
    chosen = (rank[:, None] == at[None, :]).astype(jnp.int32)
    return jnp.stack([jnp.sum(chosen * at[:, None], 0), jnp.sum(chosen * slot[:, None], 0)])


def apply_kernel(
    row_from, ranges, place_ref, table_ref, left_norm, right_norm,
    vector_ref, left_own, left_got, right_own, right_got, *refs,
):
    out_refs = refs[: len(ranges)]
    left_ref, right_ref, total_ref, slots_ref, left_sem, right_sem, out_sem = refs[len(ranges) :]
    count, rows, width = left_ref.shape
    sectors = slots_ref.shape[0]
    at_start, at_end = place_ref[0], place_ref[1]
    part = pl.ds(row_from, rows)

    @pl.when(at_start == 1)
    def _():
        for i in range(count):
            w = table_ref[0, i]
            pltpu.make_async_copy(left_own.at[w, part], left_ref.at[i], left_sem.at[i]).start()

    @pl.when(at_start != 1)
    def _():
        for i in range(count):
            w = table_ref[0, i]
            pltpu.make_async_copy(left_got.at[w, part], left_ref.at[i], left_sem.at[i]).start()

    @pl.when(at_end == 1)
    def _():
        for i in range(count):
            w = table_ref[0, i]
            pltpu.make_async_copy(right_own.at[w], right_ref.at[i], right_sem.at[i]).start()

    @pl.when(at_end != 1)
    def _():
        for i in range(count):
            w = table_ref[0, i]
            pltpu.make_async_copy(right_got.at[w], right_ref.at[i], right_sem.at[i]).start()

    @pl.loop(0, sectors)
    def _(s):
        slots_ref[s] = jnp.zeros((rows, width), BF16)

    scale = float(sectors * width)
    one = jnp.ones((1, width), F32)
    left_scale = jnp.where(at_start == 1, one, scale / left_norm[...])
    right_scale = jnp.where(at_end == 1, one, scale / right_norm[...]) * (1.0 / math.sqrt(count))
    group = 3 if count % 3 == 0 else 1

    @pl.loop(0, count // group)
    def _(step):
        for lane in range(group):
            i = step * group + lane
            pltpu.make_async_copy(left_got.at[0, part], left_ref.at[i], left_sem.at[i]).wait()
            pltpu.make_async_copy(right_got.at[0], right_ref.at[i], right_sem.at[i]).wait()
        for lane in range(group):
            i = step * group + lane
            s = table_ref[1, i]
            fresh = (i == 0) | (s != table_ref[1, jnp.maximum(i - 1, 0)])
            applied = jnp.dot(left_ref[i], vector_ref[...], preferred_element_type=F32)
            applied = (applied * left_scale).astype(BF16)
            term = jnp.dot(applied, right_ref[i], preferred_element_type=F32)
            total = jnp.where(fresh, term, total_ref[...] + term)
            total_ref[...] = total
            slots_ref[s] = (total * right_scale).astype(BF16)

    copies = [
        pltpu.make_async_copy(slots_ref.at[pl.ds(start, size)], ref, out_sem.at[k])
        for k, ((start, size), ref) in enumerate(zip(ranges, out_refs))
    ]
    for copy in copies:
        copy.start()
    for copy in copies:
        copy.wait()


def apply(row_from, rows, ranges, place, table, norms, vector, envs):
    count, width, _ = envs[0].shape
    sectors = lax.axis_size(SECTOR)
    return pl.pallas_call(
        functools.partial(apply_kernel, row_from, ranges),
        out_shape=[jax.ShapeDtypeStruct((size, rows, width), BF16) for _, size in ranges],
        in_specs=[SMEM_SPEC, SMEM_SPEC] + [VMEM_SPEC] * 3 + [HBM_SPEC] * 4,
        out_specs=[HBM_SPEC] * len(ranges),
        scratch_shapes=[
            pltpu.VMEM((count, rows, width), BF16),
            pltpu.VMEM((count, width, width), BF16),
            pltpu.VMEM((rows, width), F32),
            pltpu.VMEM((sectors, rows, width), BF16),
            pltpu.SemaphoreType.DMA((count,)),
            pltpu.SemaphoreType.DMA((count,)),
            pltpu.SemaphoreType.DMA((len(ranges),)),
        ],
        compiler_params=APPLY_PARAMS,
        cost_estimate=pl.CostEstimate(
            flops=4 * count * rows * width**2, bytes_accessed=8 * count * width**2, transcendentals=0
        ),
    )(place, table, *norms, vector, *map(in_hbm, envs))


def add_at(value, other, start):
    room = value.shape[0] - start - other.shape[0]
    return add(value, jnp.pad(other.astype(F32), ((start, room), (0, 0), (0, 0))))


def y_ranges(y_count, z_count):
    half = z_count // 2
    return (
        (2 * z_count, half), (2 * z_count + half, z_count - half),
        (z_count, z_count), (3 * z_count, z_count), (0, z_count),
    )


def z_ranges(y_count, z_count):
    far, half = z_count // 2 * y_count, y_count // 2
    ranges = [(far, half), (far + half, y_count - half)]
    for near in range(z_count // 2 - 1, 0, -1):
        ranges += [(near * y_count, y_count), ((z_count - near) * y_count, y_count)]
    return tuple(ranges + [(0, y_count)])


def target_sums(apply_y, apply_z):
    y_up, y_down, up, down, y_here = apply_y()
    y_up_got, y_down_got = along(y_up, Y, 1), along(y_down, Y, -1)
    z_parts = apply_z()
    y_up_got, y_down_got, *z_parts = lax.optimization_barrier((y_up_got, y_down_got, *z_parts))
    z_half = z_parts[0].shape[0]
    going_up, going_down = z_parts[:2]
    for k in range(2, len(z_parts) - 1, 2):
        up_got, down_got = along(going_up, Z, 1), along(going_down, Z, -1)
        if k == 2:
            going_up, going_down = add_at(z_parts[k], up_got, 0), add_at(z_parts[k + 1], down_got, z_half)
        else:
            going_up, going_down = add(z_parts[k], up_got), add(z_parts[k + 1], down_got)
    up = add_at(up, y_up_got, 0)
    down = add_at(down, y_down_got, y_up.shape[0])
    column = add(y_here, along(up, Y, 1), along(down, Y, -1))
    column, *arrived = lax.optimization_barrier(
        (column, z_parts[-1], along(going_up, Z, 1), along(going_down, Z, -1))
    )
    high = lax.all_to_all(column, Z, 0, 0, tiled=True)
    low = [
        along(add(*[part[ahead] for part in arrived]), Y, ahead)
        for ahead in range(1, arrived[0].shape[0])
    ]
    low = sum(part.astype(F32) for part in low + [part[0] for part in arrived])
    return [low], [high]


def block_sum(size_ref, diag_ref, vector, low_count, part_refs):
    pieces = []
    for refs in (part_refs[:low_count], part_refs[low_count:]):
        terms = []
        for ref in refs:
            terms += [ref[...]] if len(ref.shape) == 2 else [ref[k] for k in range(ref.shape[0])]
        total = terms[0].astype(F32)
        for term in terms[1:]:
            total = total + term.astype(F32)
        pieces.append(total)
    total = jnp.concatenate(pieces, 0) + diag_ref[...].astype(F32) * vector
    return jnp.where(live(size_ref[0], total.shape[1]), total, 0.0)


def first_kernel(low_count, size_ref, vector_ref, diag_ref, *refs):
    *part_refs, once_ref, sent_ref = refs
    once = block_sum(size_ref, diag_ref, vector_ref[...].astype(F32), low_count, part_refs)
    once_ref[...] = once
    sent_ref[...] = once.astype(BF16)


def first_sum(size, vector, diag, low, high):
    return pl.pallas_call(
        functools.partial(first_kernel, len(low)),
        out_shape=[
            jax.ShapeDtypeStruct(vector.shape, F32),
            jax.ShapeDtypeStruct(vector.shape, BF16),
        ],
        in_specs=[SMEM_SPEC] + [pl.BlockSpec()] * (2 + len(low + high)),
        out_specs=[VMEM_SPEC] * 2,
        compiler_params=SMALL_PARAMS,
    )(size, vector, diag, *low, *high)


def total_of(value):
    return jnp.sum(jnp.sum(value, 0, keepdims=True), 1, keepdims=True)


def largest(value):
    top = jnp.max(jnp.max(jnp.abs(value), 0, keepdims=True), 1, keepdims=True)
    return jnp.maximum(top, 1e-30)


def second_kernel(low_count, size_ref, vector_ref, once_ref, diag_ref, *refs):
    *part_refs, twice_ref, moments_ref = refs
    vector = vector_ref[...].astype(F32)
    once = once_ref[...]
    twice = block_sum(size_ref, diag_ref, once, low_count, part_refs)
    twice_ref[...] = twice
    top_once, top_twice = largest(once), largest(twice)
    once, twice = once / top_once, twice / top_twice
    rows = [
        total_of(vector * vector),
        total_of(vector * once),
        total_of(once * once),
        total_of(vector * twice),
        total_of(once * twice),
        total_of(twice * twice),
        top_once,
        top_twice,
    ]
    lanes = moments_ref.shape[2]
    table = jnp.concatenate([jnp.broadcast_to(row, (1, lanes)) for row in rows], 0)
    moments_ref[...] = jnp.broadcast_to(table[None], moments_ref.shape)


def second_sum(size, vector, once, diag, low, high):
    sectors = lax.axis_size(SECTOR)
    return pl.pallas_call(
        functools.partial(second_kernel, len(low)),
        out_shape=[
            jax.ShapeDtypeStruct(vector.shape, F32),
            jax.ShapeDtypeStruct((sectors, 8, 128), F32),
        ],
        in_specs=[SMEM_SPEC] + [pl.BlockSpec()] * (3 + len(low + high)),
        out_specs=[VMEM_SPEC] * 2,
        compiler_params=SMALL_PARAMS,
    )(size, vector, once, diag, *low, *high)


def last_kernel(moments_ref, vector_ref, once_ref, twice_ref, bond_ref, energy_ref):
    sectors = moments_ref.shape[0]
    width = vector_ref.shape[0]
    cells = float(sectors * width * width)
    each = [moments_ref[:, k, :] for k in range(8)]
    top_h = jnp.max(each[6], 0, keepdims=True)
    top_g = jnp.max(each[7], 0, keepdims=True)
    h, g = each[6] / top_h, each[7] / top_g
    vv = jnp.sum(each[0], 0, keepdims=True)
    vh = jnp.sum(each[1] * h, 0, keepdims=True)
    hh = jnp.sum(each[2] * h * h, 0, keepdims=True)
    vg = jnp.sum(each[3] * g, 0, keepdims=True)
    hg = jnp.sum(each[4] * h * g, 0, keepdims=True)
    gg = jnp.sum(each[5] * g * g, 0, keepdims=True)
    energy = vh * top_h / vv
    norm = vv + STEP * STEP * jnp.maximum(top_h * (hh * top_h - energy * vh), 0.0)
    factor = jnp.sqrt(cells / norm)
    on_v = factor * (1.0 + STEP * energy)
    on_h = -STEP * factor * top_h
    to_h = on_v * top_h
    to_g = -STEP * factor * top_g
    cross = on_v * (to_h * vh + to_g * vg) + on_h * (to_h * hh + to_g * hg)
    square = to_h * (to_h * hh + 2.0 * to_g * hg) + to_g * to_g * gg
    energy = cross / cells
    norm = cells + STEP * STEP * jnp.maximum(square - energy * cross, 0.0)
    factor = jnp.sqrt(cells / norm)
    grow, shrink = factor * (1.0 + STEP * energy), factor * STEP
    energy_ref[...] = energy

    def row(value):
        return jnp.concatenate([value] * (width // value.shape[1]), 1)

    bond = row(grow * on_v) * vector_ref[...].astype(F32)
    bond = bond + row(grow * on_h - shrink * to_h) * (once_ref[...] * row(1.0 / top_h))
    bond = bond - row(shrink * to_g) * (twice_ref[...] * row(1.0 / top_g))
    bond_ref[...] = bond.astype(BF16)


def last_step(moments, vector, once, twice):
    return pl.pallas_call(
        last_kernel,
        out_shape=[
            jax.ShapeDtypeStruct(vector.shape, BF16),
            jax.ShapeDtypeStruct((1, moments.shape[2]), F32),
        ],
        in_specs=[VMEM_SPEC] * 4,
        out_specs=[VMEM_SPEC] * 2,
        compiler_params=SMALL_PARAMS,
    )(moments, vector, once, twice)


def local(
    psi, left_env, right_env, diagonal, left_coeff, right_coeff, mpo_mask, sector_target, block_size
):
    sectors = lax.axis_size(SECTOR)
    width = psi.shape[-1]
    left_own, right_own, diag = left_env[0, 0], right_env[0, 0], diagonal[0, 0]
    region = lax.axis_index(REGION)

    left_out = carry(False, block_size, left_coeff, mpo_mask, psi[0, 0], left_own)
    left_got = to_region(left_out, 1)
    right_out = carry(True, block_size, right_coeff, mpo_mask, psi[0, 0], right_own)
    right_got = to_region(right_out, -1)

    live_rows = jnp.arange(width, dtype=jnp.int32) < block_size[0]
    keep = (live_rows[:, None] & live_rows[None, :]).astype(F32)
    wide = after(psi[0, 0], right_out).astype(F32) * keep
    norm = jnp.broadcast_to(jnp.sum(wide * wide).reshape(1, 1, 1), (sectors, 8, 128))
    norm = jnp.sum(lax.all_to_all(norm, SECTOR, 0, 0, tiled=True), 0)[:1]
    norm = jnp.concatenate([norm] * (width // norm.shape[1]), 1)
    norms = to_region(norm, 1), to_region(norm, -1)
    vector = (wide * jnp.sqrt(sectors * width * width / norm)).astype(BF16)

    place = jnp.stack([region == 0, region == lax.axis_size(REGION) - 1]).astype(jnp.int32)
    z_count, y_count = lax.axis_size(Z), lax.axis_size(Y)
    to_z, to_y = sector_target[0] // y_count, sector_target[0] % y_count
    ahead_z = (to_z - lax.axis_index(Z) + z_count) % z_count
    ahead_y = (to_y - lax.axis_index(Y) + y_count) % y_count
    y_first = slot_table(ahead_y * z_count + to_z)
    z_first = slot_table(ahead_z * y_count + ahead_y)
    envs = (left_own, left_got, right_own, right_got)

    def applied(value):
        def piece(start, rows, ranges, table):
            return apply(start, rows, ranges(y_count, z_count), place, table, norms, value, envs)

        return target_sums(
            lambda: piece(Z_ROWS, width - Z_ROWS, y_ranges, y_first),
            lambda: piece(0, Z_ROWS, z_ranges, z_first),
        )

    once, sent = first_sum(block_size, vector, diag, *applied(vector))
    twice, moments = second_sum(block_size, vector, once, diag, *applied(sent))
    moments = lax.all_to_all(moments, SECTOR, 0, 0, tiled=True)
    bond, energy = last_step(moments, vector, once, twice)
    return bond[None, None], energy[0, :1]


def solution(mesh):
    shape = (4, 2, 8, 4)
    grid = Mesh(mesh.devices.reshape(shape), ("x", "core", "z", "y"))
    blocks = functools.partial(P, REGION, SECTOR)
    in_specs = (
        blocks(None, None),
        blocks(None, None, None),
        blocks(None, None, None),
        blocks(None, None),
        P(),
        P(),
        P(),
        P(SECTOR, None),
        P(SECTOR),
    )
    out_specs = (blocks(None, None), P(REGION))
    return jax.shard_map(local, mesh=grid, in_specs=in_specs, out_specs=out_specs, check_vma=False)
```

time: 951 us -> 208 us (0.22)
  waiting for transfers between devices: 463 us -> 64.1 us
  blocking collectives: 365 us -> 14.8 us
  starting transfers between devices: 5.81 us -> 84.6 us
  matrix products: 58 us -> 0 us
  Pallas kernels: 0 us -> 36.3 us
  local copies, waits for them, and re-layouts: 25.3 us -> 1.38 us
  between operations: 21.5 us -> 1.71 us
    reduce_scatter x2 -> x0, waiting for transfers between devices: 437 us -> none  [local(): lax.psum_scatter(partials.astype(jnp.bfloat16), 'sector', scatter_dimensi...]
    psum x5 -> x0, blocking collectives: 365 us -> none  [the longest x2 146 us: local(): lax.psum((jnp.sum(current * current), jnp.sum(current * applied_h)), 'sec...]
    ppermute x2 -> x34, starting transfers between devices: 5.73 us -> 65.2 us  [the longest x30 53.9 us: along(): lax.ppermute(value, axis, [(i, (i + steps) % count) for i in range(count)])]
    dot_general x8 -> x0, matrix products: 58 us -> none  [the longest x2 20.5 us: local(): jnp.einsum('wt,wil->til', routing, product, precision=lax.Precision.HIGHEST)]
    pallas_call x0 -> x9, Pallas kernels: none -> 36.3 us  [the longest x4 19.1 us: apply(): pl.pallas_call(functools.partial(apply_kernel, row_from, ranges), out_sha...]
    ppermute x2 -> x34, waiting for transfers between devices: 25.7 us -> 49.2 us  [the longest x30 48.1 us: along(): lax.ppermute(value, axis, [(i, (i + steps) % count) for i in range(count)])]
    all_to_all x0 -> x3, starting transfers between devices: none -> 19.4 us  [the longest x1 11.5 us: local(): norm = jnp.sum(lax.all_to_all(norm, SECTOR, 0, 0, tiled=True), 0)[:1]]
    all_to_all x0 -> x3, waiting for transfers between devices: none -> 14.9 us  [the longest x1 9.89 us: local(): norm = jnp.sum(lax.all_to_all(norm, SECTOR, 0, 0, tiled=True), 0)[:1]]
  transfers between devices with their start and end apart: 4 -> 37, of which waited for: 4 -> 21; matrix products, arithmetic and copies ran while one was open for 2% -> 3% of each run, Pallas kernels for 0% -> 9%
where the time goes in v2:
time: 208 us
  starting transfers between devices  84.6 us (41%)
  waiting for transfers between devices  64.1 us (31%)
  Pallas kernels  36.3 us (17%)
  blocking collectives  14.8 us (7%)
  other arithmetic  4.87 us (2%)
    ppermute x30, starting transfers between devices, along(): lax.ppermute(value, axis, [(i, (i + steps) % count) for i in range(count)])  53.9 us
    ppermute x30, waiting for transfers between devices, along(): lax.ppermute(value, axis, [(i, (i + steps) % count) for i in range(count)])  48.1 us
    pallas_call x4, Pallas kernels, apply(): pl.pallas_call(functools.partial(apply_kernel, row_from, ranges), out_sha...  19.1 us
    pallas_call x2, Pallas kernels, carry(): pl.pallas_call(functools.partial(carry_kernel, flip), out_shape=jax.Shape...  15.8 us
    all_to_all x1, blocking collectives, local(): moments = lax.all_to_all(moments, SECTOR, 0, 0, tiled=True)  14.8 us
    all_to_all x1, starting transfers between devices, local(): norm = jnp.sum(lax.all_to_all(norm, SECTOR, 0, 0, tiled=True), 0)[:1]  11.5 us
    ppermute x4, starting transfers between devices, to_region(): lax.ppermute(value, REGION, [(i, i + steps) for i in range(leading, last)])  11.3 us
    all_to_all x1, waiting for transfers between devices, local(): norm = jnp.sum(lax.all_to_all(norm, SECTOR, 0, 0, tiled=True), 0)[:1]  9.89 us
  transfers between devices with their start and end apart: 37, of which 21 were waited for; matrix products, arithmetic and copies ran while one was open for 3% of the time, Pallas kernels for 9%

profile of v2, /device:TPU:6, one launch (start us, length us, event | category | flops | bytes accessed | tf_op | source)
XLA Modules:
  0.0 207.8 jit_solution(11269572564329235370)
XLA Ops:
  1.3 7.9 %shard_map.104 = bf16[18,256,256]{2,1,0:T(8,128)(2,1)} custom-call(s32[1]{0:T(128)} %copy.11.size_ref, f32[18,18]{1,0:T(8,128)} %coeff_ref.2, s32[18,18]{1,0:T(8,128)} %pattern_ref.3, bf16[256,256]{1,0:T(8,128)(2,1)} %bitcast.80, bf16[18,256,256]{2,1,0:T(8,128)(2,1)} %bitcast.75), custom_call_target="tpu_custom_call" | custom-call | flops 2415919104 | bytes 4718592 | tf_op jit(solution)/shard_map/pallas_call | solution.py:152
  9.1 2.2 %collective-permute-start.3 = (bf16[18,256,256]{2,1,0:T(8,128)(2,1)}, bf16[18,256,256]{2,1,0:T(8,128)(2,1)}, u32[]{:S(2)}, u32[]{:S(2)}) collective-permute-start(bf16[18,256,256]{2,1,0:T(8,128)(2,1)} %shard_map.104), channel_id=1, source_target_pairs={{32,0},{64,32},{96,64},{128,96},{160,128},{192,160},{224,192},{33,... | collective-permute-start | bytes 7077896 | tf_op jit(solution)/shard_map/ppermute | solution.py:37
  11.4 7.9 %shard_map.105 = bf16[18,256,256]{2,1,0:T(8,128)(2,1)} custom-call(s32[1]{0:T(128)} %copy.11.size_ref, f32[18,18]{1,0:T(8,128)} %coeff_ref.3, s32[18,18]{1,0:T(8,128)} %pattern_ref.3, bf16[256,256]{1,0:T(8,128)(2,1)} %bitcast.81, bf16[18,256,256]{2,1,0:T(8,128)(2,1)} %bitcast.70), custom_call_target="tpu_custom_call" | custom-call | flops 2415919104 | bytes 4718592 | tf_op jit(solution)/shard_map/pallas_call | solution.py:152
  19.3 3.5 %collective-permute-start.2 = (bf16[18,256,256]{2,1,0:T(8,128)(2,1)}, bf16[18,256,256]{2,1,0:T(8,128)(2,1)}, u32[]{:S(2)}, u32[]{:S(2)}) collective-permute-start(bf16[18,256,256]{2,1,0:T(8,128)(2,1)} %shard_map.105), channel_id=1, source_target_pairs={{0,32},{32,64},{64,96},{96,128},{128,160},{160,192},{192,224},{1,3... | collective-permute-start | bytes 7077896 | tf_op jit(solution)/shard_map/ppermute | solution.py:37
  23.7 1.4 broadcast_in_dim.4
  25.0 11.5 %all-to-all-start = ((f32[32,8,128]{2,1,0:T(8,128)}), f32[32,8,128]{2,1,0:T(8,128)S(1)}, u32[]{:S(2)}, u32[]{:S(2)}) async-start(f32[32,8,128]{2,1,0:T(8,128)} %broadcast_in_dim.4), calls=%async_computation | async-start | bytes 262144 | tf_op jit(solution)/shard_map/all_to_all | solution.py:478
  37.1 9.9 %all-to-all-done = f32[32,8,128]{2,1,0:T(8,128)S(1)} async-done(((f32[32,8,128]{2,1,0:T(8,128)}), f32[32,8,128]{2,1,0:T(8,128)S(1)}, u32[]{:S(2)}, u32[]{:S(2)}) %all-to-all-start) | async-done | bytes 131104 | tf_op jit(solution)/shard_map/all_to_all | solution.py:478
  47.1 1.9 collective-permute-start
  49.0 3.6 %collective-permute-start.1 = (f32[1,256]{1,0:T(1,128)S(1)}, f32[1,256]{1,0:T(1,128)S(1)}, u32[]{:S(2)}, u32[]{:S(2)}) collective-permute-start(f32[1,256]{1,0:T(1,128)S(1)} %pad_maximum_fusion), channel_id=1, source_target_pairs={{32,0},{64,32},{96,64},{128,96},{160,128},{192,160},{224,192},{33,... | collective-permute-start | bytes 3080 | tf_op jit(solution)/shard_map/ppermute | solution.py:37
  52.8 1.1 collective-permute-done.1.right_norm
  53.9 4.6 %shard_map.106 = (bf16[4,128,256]{2,1,0:T(8,128)(2,1)S(1)}, bf16[4,128,256]{2,1,0:T(8,128)(2,1)S(1)}, bf16[8,128,256]{2,1,0:T(8,128)(2,1)S(1)}, bf16[8,128,256]{2,1,0:T(8,128)(2,1)S(1)}, bf16[8,128,256]{2,1,0:T(8,128)(2,1)S(1)}) custom-call(s32[2]{0:T(128)S(1)} %add_convert_fusion.24.place_ref, s32[2,18]{1,0:T(2,128)S(1)} %pad_add_fusion.table_ref, ...), custom_call_target="tpu_custom_call" | custom-call | flops 603979776 | bytes 9437184 | tf_op jit(solution)/shard_map/pallas_call | solution.py:260
  58.7 3.1 %collective-permute-start.5 = (bf16[4,128,256]{2,1,0:T(8,128)(2,1)S(1)}, bf16[4,128,256]{2,1,0:T(8,128)(2,1)S(1)}, u32[]{:S(2)}, u32[]{:S(2)}) collective-permute-start(bf16[4,128,256]{2,1,0:T(8,128)(2,1)S(1)} %get-tuple-element.71), channel_id=1, source_target_pairs={{0,3},{1,0},{2,1},{3,2},{4,7},{5,4},{6,5},{7,6},{8,11},{9,8},{10,9... | collective-permute-start | bytes 786440 | tf_op jit(solution)/shard_map/ppermute | solution.py:31
  61.9 5.0 %shard_map.107 = (bf16[2,128,256]{2,1,0:T(8,128)(2,1)S(1)}, bf16[2,128,256]{2,1,0:T(8,128)(2,1)S(1)}, bf16[4,128,256]{2,1,0:T(8,128)(2,1)S(1)}, bf16[4,128,256]{...) custom-call(s32[2]{0:T(128)S(1)} %add_convert_fusion.24.place_ref, ...), custom_call_target="tpu_custom_call" | custom-call | flops 603979776 | bytes 9437184 | tf_op jit(solution)/shard_map/pallas_call | solution.py:260
  67.0 1.8 collective-permute-start.12
  69.9 2.1 collective-permute-done.12
  72.0 3.0 %collective-permute-start.13 = (bf16[4,128,256]{2,1,0:T(8,128)(2,1)S(1)}, bf16[4,128,256]{2,1,0:T(8,128)(2,1)S(1)}, u32[]{:S(2)}, u32[]{:S(2)}) collective-permute-start(bf16[4,128,256]{2,1,0:T(8,128)(2,1)S(1)} %add_convert_fusion.14), channel_id=1, source_target_pairs={{0,28},{4,0},{8,4},{12,8},{16,12},{20,16},{24,20},{28,24},{1,29},{... | collective-permute-start | bytes 786440 | tf_op jit(solution)/shard_map/ppermute | solution.py:31
  75.2 3.3 %collective-permute-start.7 = (bf16[8,128,256]{2,1,0:T(8,128)(2,1)S(1)}, bf16[8,128,256]{2,1,0:T(8,128)(2,1)S(1)}, u32[]{:S(2)}, u32[]{:S(2)}) collective-permute-start(bf16[8,128,256]{2,1,0:T(8,128)(2,1)S(1)} %add_convert_fusion.4), channel_id=1, source_target_pairs={{0,3},{1,0},{2,1},{3,2},{4,7},{5,4},{6,5},{7,6},{8,11},{9,8},{10,9... | collective-permute-start | bytes 1572872 | tf_op jit(solution)/shard_map/ppermute | solution.py:31
  79.2 3.8 %collective-permute-start.14 = (bf16[4,128,256]{2,1,0:T(8,128)(2,1)S(1)}, bf16[4,128,256]{2,1,0:T(8,128)(2,1)S(1)}, u32[]{:S(2)}, u32[]{:S(2)}) collective-permute-start(bf16[4,128,256]{2,1,0:T(8,128)(2,1)S(1)} %add_convert_fusion.13), channel_id=1, source_target_pairs={{0,28},{4,0},{8,4},{12,8},{16,12},{20,16},{24,20},{28,24},{1,29},{... | collective-permute-start | bytes 786440 | tf_op jit(solution)/shard_map/ppermute | solution.py:31
  83.3 4.8 %collective-permute-done.14 = bf16[4,128,256]{2,1,0:T(8,128)(2,1)S(1)} collective-permute-done((bf16[4,128,256]{2,1,0:T(8,128)(2,1)S(1)}, bf16[4,128,256]{2,1,0:T(8,128)(2,1)S(1)}, u32[]{:S(2)}, u32[]{:S(2)}) %collective-permute-start.14) | collective-permute-done | bytes 262176 | tf_op jit(solution)/shard_map/ppermute | solution.py:31
  88.2 3.8 %collective-permute-start.15 = (bf16[4,128,256]{2,1,0:T(8,128)(2,1)S(1)}, bf16[4,128,256]{2,1,0:T(8,128)(2,1)S(1)}, u32[]{:S(2)}, u32[]{:S(2)}) collective-permute-start(bf16[4,128,256]{2,1,0:T(8,128)(2,1)S(1)} %add_convert_fusion.12), channel_id=1, source_target_pairs={{0,28},{4,0},{8,4},{12,8},{16,12},{20,16},{24,20},{28,24},{1,29},{... | collective-permute-start | bytes 786440 | tf_op jit(solution)/shard_map/ppermute | solution.py:31
  93.7 2.2 %collective-permute-done.15 = bf16[4,128,256]{2,1,0:T(8,128)(2,1)S(1)} collective-permute-done((bf16[4,128,256]{2,1,0:T(8,128)(2,1)S(1)}, bf16[4,128,256]{2,1,0:T(8,128)(2,1)S(1)}, u32[]{:S(2)}, u32[]{:S(2)}) %collective-permute-start.15) | collective-permute-done | bytes 262176 | tf_op jit(solution)/shard_map/ppermute | solution.py:31
  95.9 4.3 %collective-permute-done.11 = bf16[4,128,256]{2,1,0:T(8,128)(2,1)S(1)} collective-permute-done((bf16[4,128,256]{2,1,0:T(8,128)(2,1)S(1)}, bf16[4,128,256]{2,1,0:T(8,128)(2,1)S(1)}, u32[]{:S(2)}, u32[]{:S(2)}) %collective-permute-start.11) | collective-permute-done | bytes 262176 | tf_op jit(solution)/shard_map/ppermute | solution.py:31
  100.2 3.5 %all-to-all-start.1 = ((bf16[8,128,256]{2,1,0:T(8,128)(2,1)}), bf16[8,128,256]{2,1,0:T(8,128)(2,1)S(1)}, u32[]{:S(2)}, u32[]{:S(2)}) async-start(bf16[8,128,256]{2,1,0:T(8,128)(2,1)} %add_convert_fusion.3), calls=%async_computation.1 | async-start | bytes 1048576 | tf_op jit(solution)/shard_map/all_to_all | solution.py:321
  103.8 8.0 %collective-permute-start.16 = (bf16[128,256]{1,0:T(8,128)(2,1)S(1)}, bf16[128,256]{1,0:T(8,128)(2,1)S(1)}, u32[]{:S(2)}, u32[]{:S(2)}) collective-permute-start(bf16[128,256]{1,0:T(8,128)(2,1)S(1)} %get-tuple-element.145), channel_id=1, source_target_pairs={{0,1},{1,2},{2,3},{3,0},{4,5},{5,6},{6,7},{7,4},{8,9},{9,10},{10,1... | collective-permute-start | bytes 196616 | tf_op jit(solution)/shard_map/ppermute | solution.py:31
  111.8 3.0 %collective-permute-start.17 = (bf16[128,256]{1,0:T(8,128)(2,1)S(1)}, bf16[128,256]{1,0:T(8,128)(2,1)S(1)}, u32[]{:S(2)}, u32[]{:S(2)}) collective-permute-start(bf16[128,256]{1,0:T(8,128)(2,1)S(1)} %get-tuple-element.147), channel_id=1, source_target_pairs={{0,2},{1,3},{2,0},{3,1},{4,6},{5,7},{6,4},{7,5},{8,10},{9,11},{10,... | collective-permute-start | bytes 196616 | tf_op jit(solution)/shard_map/ppermute | solution.py:31
  114.8 2.5 %collective-permute-start.18 = (bf16[128,256]{1,0:T(8,128)(2,1)S(1)}, bf16[128,256]{1,0:T(8,128)(2,1)S(1)}, u32[]{:S(2)}, u32[]{:S(2)}) collective-permute-start(bf16[128,256]{1,0:T(8,128)(2,1)S(1)} %get-tuple-element.146), channel_id=1, source_target_pairs={{0,3},{1,0},{2,1},{3,2},{4,7},{5,4},{6,5},{7,6},{8,11},{9,8},{10,9... | collective-permute-start | bytes 196616 | tf_op jit(solution)/shard_map/ppermute | solution.py:31
  117.7 1.6 collective-permute-done.18
  119.5 4.6 %shard_map.109 = (bf16[4,128,256]{2,1,0:T(8,128)(2,1)S(1)}, bf16[4,128,256]{2,1,0:T(8,128)(2,1)S(1)}, bf16[8,128,256]{2,1,0:T(8,128)(2,1)S(1)}, bf16[8,128,256]{2,1,0:T(8,128)(2,1)S(1)}, bf16[8,128,256]{2,1,0:T(8,128)(2,1)S(1)}) custom-call(s32[2]{0:T(128)S(1)} %add_convert_fusion.24.place_ref, s32[2,18]{1,0:T(2,128)S(1)} %pad_add_fusion.table_ref, ...), custom_call_target="tpu_custom_call" | custom-call | flops 603979776 | bytes 9437184 | tf_op jit(solution)/shard_map/pallas_call | solution.py:260
  124.1 5.5 %collective-permute-start.19 = (bf16[4,128,256]{2,1,0:T(8,128)(2,1)S(1)}, bf16[4,128,256]{2,1,0:T(8,128)(2,1)S(1)}, u32[]{:S(2)}, u32[]{:S(2)}) collective-permute-start(bf16[4,128,256]{2,1,0:T(8,128)(2,1)S(1)} %get-tuple-element.101), channel_id=1, source_target_pairs={{0,1},{1,2},{2,3},{3,0},{4,5},{5,6},{6,7},{7,4},{8,9},{9,10},{10,1... | collective-permute-start | bytes 786440 | tf_op jit(solution)/shard_map/ppermute | solution.py:31
  129.6 5.0 %shard_map.110 = (bf16[2,128,256]{2,1,0:T(8,128)(2,1)S(1)}, bf16[2,128,256]{2,1,0:T(8,128)(2,1)S(1)}, bf16[4,128,256]{2,1,0:T(8,128)(2,1)S(1)}, bf16[4,128,256]{...) custom-call(s32[2]{0:T(128)S(1)} %add_convert_fusion.24.place_ref, ...), custom_call_target="tpu_custom_call" | custom-call | flops 603979776 | bytes 9437184 | tf_op jit(solution)/shard_map/pallas_call | solution.py:260
  135.1 4.6 %collective-permute-done.20 = bf16[4,128,256]{2,1,0:T(8,128)(2,1)S(1)} collective-permute-done((bf16[4,128,256]{2,1,0:T(8,128)(2,1)S(1)}, bf16[4,128,256]{2,1,0:T(8,128)(2,1)S(1)}, u32[]{:S(2)}, u32[]{:S(2)}) %collective-permute-start.20) | collective-permute-done | bytes 262176 | tf_op jit(solution)/shard_map/ppermute | solution.py:31
  139.7 2.0 collective-permute-start.23
  141.8 1.6 collective-permute-start.21
  143.3 2.6 %collective-permute-done.27 = bf16[2,128,256]{2,1,0:T(8,128)(2,1)S(1)} collective-permute-done((bf16[2,128,256]{2,1,0:T(8,128)(2,1)S(1)}, bf16[2,128,256]{2,1,0:T(8,128)(2,1)S(1)}, u32[]{:S(2)}, u32[]{:S(2)}) %collective-permute-start.27) | collective-permute-done | bytes 131104 | tf_op jit(solution)/shard_map/ppermute | solution.py:31
  146.1 2.1 collective-permute-start.24
  148.6 3.8 %collective-permute-done.28 = bf16[4,128,256]{2,1,0:T(8,128)(2,1)S(1)} collective-permute-done((bf16[4,128,256]{2,1,0:T(8,128)(2,1)S(1)}, bf16[4,128,256]{2,1,0:T(8,128)(2,1)S(1)}, u32[]{:S(2)}, u32[]{:S(2)}) %collective-permute-start.28) | collective-permute-done | bytes 262176 | tf_op jit(solution)/shard_map/ppermute | solution.py:31
  152.5 1.3 collective-permute-start.29
  154.8 9.5 %collective-permute-done.29 = bf16[4,128,256]{2,1,0:T(8,128)(2,1)S(1)} collective-permute-done((bf16[4,128,256]{2,1,0:T(8,128)(2,1)S(1)}, bf16[4,128,256]{2,1,0:T(8,128)(2,1)S(1)}, u32[]{:S(2)}, u32[]{:S(2)}) %collective-permute-start.29) | collective-permute-done | bytes 262176 | tf_op jit(solution)/shard_map/ppermute | solution.py:31
  164.9 1.2 collective-permute-done.25
  167.6 3.2 %collective-permute-done.30 = bf16[4,128,256]{2,1,0:T(8,128)(2,1)S(1)} collective-permute-done((bf16[4,128,256]{2,1,0:T(8,128)(2,1)S(1)}, bf16[4,128,256]{2,1,0:T(8,128)(2,1)S(1)}, u32[]{:S(2)}, u32[]{:S(2)}) %collective-permute-start.30) | collective-permute-done | bytes 262176 | tf_op jit(solution)/shard_map/ppermute | solution.py:31
  170.8 3.1 %collective-permute-done.26 = bf16[4,128,256]{2,1,0:T(8,128)(2,1)S(1)} collective-permute-done((bf16[4,128,256]{2,1,0:T(8,128)(2,1)S(1)}, bf16[4,128,256]{2,1,0:T(8,128)(2,1)S(1)}, u32[]{:S(2)}, u32[]{:S(2)}) %collective-permute-start.26) | collective-permute-done | bytes 262176 | tf_op jit(solution)/shard_map/ppermute | solution.py:31
  173.9 4.5 %all-to-all-start.2 = ((bf16[8,128,256]{2,1,0:T(8,128)(2,1)}), bf16[8,128,256]{2,1,0:T(8,128)(2,1)S(1)}, u32[]{:S(2)}, u32[]{:S(2)}) async-start(bf16[8,128,256]{2,1,0:T(8,128)(2,1)} %add_convert_fusion), calls=%async_computation.2 | async-start | bytes 1048576 | tf_op jit(solution)/shard_map/all_to_all | solution.py:321
  178.4 2.4 %collective-permute-start.31 = (bf16[128,256]{1,0:T(8,128)(2,1)S(1)}, bf16[128,256]{1,0:T(8,128)(2,1)S(1)}, u32[]{:S(2)}, u32[]{:S(2)}) collective-permute-start(bf16[128,256]{1,0:T(8,128)(2,1)S(1)} %get-tuple-element.142), channel_id=1, source_target_pairs={{0,1},{1,2},{2,3},{3,0},{4,5},{5,6},{6,7},{7,4},{8,9},{9,10},{10,1... | collective-permute-start | bytes 196616 | tf_op jit(solution)/shard_map/ppermute | solution.py:31
  180.8 1.2 collective-permute-start.32
  182.0 1.6 collective-permute-start.33
  184.0 2.6 %collective-permute-done.32 = bf16[128,256]{1,0:T(8,128)(2,1)S(1)} collective-permute-done((bf16[128,256]{1,0:T(8,128)(2,1)S(1)}, bf16[128,256]{1,0:T(8,128)(2,1)S(1)}, u32[]{:S(2)}, u32[]{:S(2)}) %collective-permute-start.32) | collective-permute-done | bytes 65568 | tf_op jit(solution)/shard_map/ppermute | solution.py:31
  186.7 5.0 %all-to-all-done.2.refs_1_ = bf16[8,128,256]{2,1,0:T(8,128)(2,1)S(1)} async-done(((bf16[8,128,256]{2,1,0:T(8,128)(2,1)}), bf16[8,128,256]{2,1,0:T(8,128)(2,1)S(1)}, u32[]{:S(2)}, u32[]{:S(2)}) %all-to-all-start.2) | async-done | bytes 524320 | tf_op jit(solution)/shard_map/all_to_all | solution.py:321
  192.1 14.8 %all_to_all.20.moments_ref = f32[32,8,128]{2,1,0:T(8,128)S(1)} all-to-all(f32[32,8,128]{2,1,0:T(8,128)S(1)} %get-tuple-element.128), channel_id=1, replica_groups=mesh['x'=4,'core'=2,'z'=8,'y'=4] {'z','y'}, dimensions={0} | all-to-all | bytes 262144 | tf_op jit(solution)/shard_map/all_to_all | solution.py:503
  (83 shorter events, 12.7 us)
Async XLA Ops:
  9.1 44.8 %collective-permute-start.3 = (bf16[18,256,256]{2,1,0:T(8,128)(2,1)}, bf16[18,256,256]{2,1,0:T(8,128)(2,1)}, u32[]{:S(2)}, u32[]{:S(2)}) collective-permute-start(bf16[18,256,256]{2,1,0:T(8,128)(2,1)} %shard_map.104), channel_id=1, source_target_pairs={{32,0},{64,32},{96,64},{128,96},{160,128},{192,160},{224,192},{33,... | collective-permute-start | bytes 7077896 | tf_op jit(solution)/shard_map/ppermute | solution.py:37
  11.3 11.5 %copy-start.1 = (bf16[1,1,256,256]{3,2,1,0:T(8,128)(2,1)S(1)}, bf16[1,1,256,256]{3,2,1,0:T(8,128)(2,1)}, u32[]{:S(2)}) copy-start(bf16[1,1,256,256]{3,2,1,0:T(8,128)(2,1)} %param.9) | copy-start | bytes 393220
  11.3 25.2 %copy-start.2 = (s32[1,18]{1,0:T(1,128)S(1)}, s32[1,18]{1,0:T(1,128)}, u32[]{:S(2)}) copy-start(s32[1,18]{1,0:T(1,128)} %param.16) | copy-start | bytes 220
  19.3 34.7 %collective-permute-start.2 = (bf16[18,256,256]{2,1,0:T(8,128)(2,1)}, bf16[18,256,256]{2,1,0:T(8,128)(2,1)}, u32[]{:S(2)}, u32[]{:S(2)}) collective-permute-start(bf16[18,256,256]{2,1,0:T(8,128)(2,1)} %shard_map.105), channel_id=1, source_target_pairs={{0,32},{32,64},{64,96},{96,128},{128,160},{160,192},{192,224},{1,3... | collective-permute-start | bytes 7077896 | tf_op jit(solution)/shard_map/ppermute | solution.py:37
  25.0 22.0 %all-to-all-start = ((f32[32,8,128]{2,1,0:T(8,128)}), f32[32,8,128]{2,1,0:T(8,128)S(1)}, u32[]{:S(2)}, u32[]{:S(2)}) async-start(f32[32,8,128]{2,1,0:T(8,128)} %broadcast_in_dim.4), calls=%async_computation | async-start | bytes 262144 | tf_op jit(solution)/shard_map/all_to_all | solution.py:478
  47.1 5.7 %collective-permute-start = (f32[1,256]{1,0:T(1,128)S(1)}, f32[1,256]{1,0:T(1,128)S(1)}, u32[]{:S(2)}, u32[]{:S(2)}) collective-permute-start(f32[1,256]{1,0:T(1,128)S(1)} %pad_maximum_fusion), channel_id=1, source_target_pairs={{0,32},{32,64},{64,96},{96,128},{128,160},{160,192},{192,224},{1,3... | collective-permute-start | bytes 3080 | tf_op jit(solution)/shard_map/ppermute | solution.py:37
  49.0 4.9 %collective-permute-start.1 = (f32[1,256]{1,0:T(1,128)S(1)}, f32[1,256]{1,0:T(1,128)S(1)}, u32[]{:S(2)}, u32[]{:S(2)}) collective-permute-start(f32[1,256]{1,0:T(1,128)S(1)} %pad_maximum_fusion), channel_id=1, source_target_pairs={{32,0},{64,32},{96,64},{128,96},{160,128},{192,160},{224,192},{33,... | collective-permute-start | bytes 3080 | tf_op jit(solution)/shard_map/ppermute | solution.py:37
  58.5 8.4 %collective-permute-start.4 = (bf16[4,128,256]{2,1,0:T(8,128)(2,1)S(1)}, bf16[4,128,256]{2,1,0:T(8,128)(2,1)S(1)}, u32[]{:S(2)}, u32[]{:S(2)}) collective-permute-start(bf16[4,128,256]{2,1,0:T(8,128)(2,1)S(1)} %get-tuple-element.70), channel_id=1, source_target_pairs={{0,1},{1,2},{2,3},{3,0},{4,5},{5,6},{6,7},{7,4},{8,9},{9,10},{10,1... | collective-permute-start | bytes 786440 | tf_op jit(solution)/shard_map/ppermute | solution.py:31
  58.7 8.3 %collective-permute-start.5 = (bf16[4,128,256]{2,1,0:T(8,128)(2,1)S(1)}, bf16[4,128,256]{2,1,0:T(8,128)(2,1)S(1)}, u32[]{:S(2)}, u32[]{:S(2)}) collective-permute-start(bf16[4,128,256]{2,1,0:T(8,128)(2,1)S(1)} %get-tuple-element.71), channel_id=1, source_target_pairs={{0,3},{1,0},{2,1},{3,2},{4,7},{5,4},{6,5},{7,6},{8,11},{9,8},{10,9... | collective-permute-start | bytes 786440 | tf_op jit(solution)/shard_map/ppermute | solution.py:31
  67.0 5.0 %collective-permute-start.12 = (bf16[2,128,256]{2,1,0:T(8,128)(2,1)S(1)}, bf16[2,128,256]{2,1,0:T(8,128)(2,1)S(1)}, u32[]{:S(2)}, u32[]{:S(2)}) collective-permute-start(bf16[2,128,256]{2,1,0:T(8,128)(2,1)S(1)} %get-tuple-element.92), channel_id=1, source_target_pairs={{0,28},{4,0},{8,4},{12,8},{16,12},{20,16},{24,20},{28,24},{1,29},{... | collective-permute-start | bytes 393224 | tf_op jit(solution)/shard_map/ppermute | solution.py:31
  68.7 6.3 %collective-permute-start.8 = (bf16[2,128,256]{2,1,0:T(8,128)(2,1)S(1)}, bf16[2,128,256]{2,1,0:T(8,128)(2,1)S(1)}, u32[]{:S(2)}, u32[]{:S(2)}) collective-permute-start(bf16[2,128,256]{2,1,0:T(8,128)(2,1)S(1)} %get-tuple-element.88), channel_id=1, source_target_pairs={{0,4},{4,8},{8,12},{12,16},{16,20},{20,24},{24,28},{28,0},{1,5},{5... | collective-permute-start | bytes 393224 | tf_op jit(solution)/shard_map/ppermute | solution.py:31
  69.1 23.5 %collective-permute-start.6 = (bf16[8,128,256]{2,1,0:T(8,128)(2,1)S(1)}, bf16[8,128,256]{2,1,0:T(8,128)(2,1)S(1)}, u32[]{:S(2)}, u32[]{:S(2)}) collective-permute-start(bf16[8,128,256]{2,1,0:T(8,128)(2,1)S(1)} %add_convert_fusion.5), channel_id=1, source_target_pairs={{0,1},{1,2},{2,3},{3,0},{4,5},{5,6},{6,7},{7,4},{8,9},{9,10},{10,1... | collective-permute-start | bytes 1572872 | tf_op jit(solution)/shard_map/ppermute | solution.py:31
  72.0 7.1 %collective-permute-start.13 = (bf16[4,128,256]{2,1,0:T(8,128)(2,1)S(1)}, bf16[4,128,256]{2,1,0:T(8,128)(2,1)S(1)}, u32[]{:S(2)}, u32[]{:S(2)}) collective-permute-start(bf16[4,128,256]{2,1,0:T(8,128)(2,1)S(1)} %add_convert_fusion.14), channel_id=1, source_target_pairs={{0,28},{4,0},{8,4},{12,8},{16,12},{20,16},{24,20},{28,24},{1,29},{... | collective-permute-start | bytes 786440 | tf_op jit(solution)/shard_map/ppermute | solution.py:31
  75.1 8.0 %collective-permute-start.9 = (bf16[4,128,256]{2,1,0:T(8,128)(2,1)S(1)}, bf16[4,128,256]{2,1,0:T(8,128)(2,1)S(1)}, u32[]{:S(2)}, u32[]{:S(2)}) collective-permute-start(bf16[4,128,256]{2,1,0:T(8,128)(2,1)S(1)} %add_convert_fusion.17), channel_id=1, source_target_pairs={{0,4},{4,8},{8,12},{12,16},{16,20},{20,24},{24,28},{28,0},{1,5},{5... | collective-permute-start | bytes 786440 | tf_op jit(solution)/shard_map/ppermute | solution.py:31
  75.2 17.5 %collective-permute-start.7 = (bf16[8,128,256]{2,1,0:T(8,128)(2,1)S(1)}, bf16[8,128,256]{2,1,0:T(8,128)(2,1)S(1)}, u32[]{:S(2)}, u32[]{:S(2)}) collective-permute-start(bf16[8,128,256]{2,1,0:T(8,128)(2,1)S(1)} %add_convert_fusion.4), channel_id=1, source_target_pairs={{0,3},{1,0},{2,1},{3,2},{4,7},{5,4},{6,5},{7,6},{8,11},{9,8},{10,9... | collective-permute-start | bytes 1572872 | tf_op jit(solution)/shard_map/ppermute | solution.py:31
  79.2 9.0 %collective-permute-start.14 = (bf16[4,128,256]{2,1,0:T(8,128)(2,1)S(1)}, bf16[4,128,256]{2,1,0:T(8,128)(2,1)S(1)}, u32[]{:S(2)}, u32[]{:S(2)}) collective-permute-start(bf16[4,128,256]{2,1,0:T(8,128)(2,1)S(1)} %add_convert_fusion.13), channel_id=1, source_target_pairs={{0,28},{4,0},{8,4},{12,8},{16,12},{20,16},{24,20},{28,24},{1,29},{... | collective-permute-start | bytes 786440 | tf_op jit(solution)/shard_map/ppermute | solution.py:31
  83.1 9.4 %collective-permute-start.10 = (bf16[4,128,256]{2,1,0:T(8,128)(2,1)S(1)}, bf16[4,128,256]{2,1,0:T(8,128)(2,1)S(1)}, u32[]{:S(2)}, u32[]{:S(2)}) collective-permute-start(bf16[4,128,256]{2,1,0:T(8,128)(2,1)S(1)} %add_convert_fusion.16), channel_id=1, source_target_pairs={{0,4},{4,8},{8,12},{12,16},{16,20},{20,24},{24,28},{28,0},{1,5},{5... | collective-permute-start | bytes 786440 | tf_op jit(solution)/shard_map/ppermute | solution.py:31
  88.2 7.7 %collective-permute-start.15 = (bf16[4,128,256]{2,1,0:T(8,128)(2,1)S(1)}, bf16[4,128,256]{2,1,0:T(8,128)(2,1)S(1)}, u32[]{:S(2)}, u32[]{:S(2)}) collective-permute-start(bf16[4,128,256]{2,1,0:T(8,128)(2,1)S(1)} %add_convert_fusion.12), channel_id=1, source_target_pairs={{0,28},{4,0},{8,4},{12,8},{16,12},{20,16},{24,20},{28,24},{1,29},{... | collective-permute-start | bytes 786440 | tf_op jit(solution)/shard_map/ppermute | solution.py:31
  92.6 26.8 %copy-start = (bf16[1,1,256,256]{3,2,1,0:T(8,128)(2,1)S(1)}, bf16[1,1,256,256]{3,2,1,0:T(8,128)(2,1)}, u32[]{:S(2)}) copy-start(bf16[1,1,256,256]{3,2,1,0:T(8,128)(2,1)} %param.12) | copy-start | bytes 393220
  92.6 7.7 %collective-permute-start.11 = (bf16[4,128,256]{2,1,0:T(8,128)(2,1)S(1)}, bf16[4,128,256]{2,1,0:T(8,128)(2,1)S(1)}, u32[]{:S(2)}, u32[]{:S(2)}) collective-permute-start(bf16[4,128,256]{2,1,0:T(8,128)(2,1)S(1)} %add_convert_fusion.15), channel_id=1, source_target_pairs={{0,4},{4,8},{8,12},{12,16},{16,20},{20,24},{24,28},{28,0},{1,5},{5... | collective-permute-start | bytes 786440 | tf_op jit(solution)/shard_map/ppermute | solution.py:31
  100.2 19.1 %all-to-all-start.1 = ((bf16[8,128,256]{2,1,0:T(8,128)(2,1)}), bf16[8,128,256]{2,1,0:T(8,128)(2,1)S(1)}, u32[]{:S(2)}, u32[]{:S(2)}) async-start(bf16[8,128,256]{2,1,0:T(8,128)(2,1)} %add_convert_fusion.3), calls=%async_computation.1 | async-start | bytes 1048576 | tf_op jit(solution)/shard_map/all_to_all | solution.py:321
  103.8 13.5 %collective-permute-start.16 = (bf16[128,256]{1,0:T(8,128)(2,1)S(1)}, bf16[128,256]{1,0:T(8,128)(2,1)S(1)}, u32[]{:S(2)}, u32[]{:S(2)}) collective-permute-start(bf16[128,256]{1,0:T(8,128)(2,1)S(1)} %get-tuple-element.145), channel_id=1, source_target_pairs={{0,1},{1,2},{2,3},{3,0},{4,5},{5,6},{6,7},{7,4},{8,9},{9,10},{10,1... | collective-permute-start | bytes 196616 | tf_op jit(solution)/shard_map/ppermute | solution.py:31
  111.8 5.9 %collective-permute-start.17 = (bf16[128,256]{1,0:T(8,128)(2,1)S(1)}, bf16[128,256]{1,0:T(8,128)(2,1)S(1)}, u32[]{:S(2)}, u32[]{:S(2)}) collective-permute-start(bf16[128,256]{1,0:T(8,128)(2,1)S(1)} %get-tuple-element.147), channel_id=1, source_target_pairs={{0,2},{1,3},{2,0},{3,1},{4,6},{5,7},{6,4},{7,5},{8,10},{9,11},{10,... | collective-permute-start | bytes 196616 | tf_op jit(solution)/shard_map/ppermute | solution.py:31
  114.8 4.5 %collective-permute-start.18 = (bf16[128,256]{1,0:T(8,128)(2,1)S(1)}, bf16[128,256]{1,0:T(8,128)(2,1)S(1)}, u32[]{:S(2)}, u32[]{:S(2)}) collective-permute-start(bf16[128,256]{1,0:T(8,128)(2,1)S(1)} %get-tuple-element.146), channel_id=1, source_target_pairs={{0,3},{1,0},{2,1},{3,2},{4,7},{5,4},{6,5},{7,6},{8,11},{9,8},{10,9... | collective-permute-start | bytes 196616 | tf_op jit(solution)/shard_map/ppermute | solution.py:31
  124.1 11.0 %collective-permute-start.19 = (bf16[4,128,256]{2,1,0:T(8,128)(2,1)S(1)}, bf16[4,128,256]{2,1,0:T(8,128)(2,1)S(1)}, u32[]{:S(2)}, u32[]{:S(2)}) collective-permute-start(bf16[4,128,256]{2,1,0:T(8,128)(2,1)S(1)} %get-tuple-element.101), channel_id=1, source_target_pairs={{0,1},{1,2},{2,3},{3,0},{4,5},{5,6},{6,7},{7,4},{8,9},{9,10},{10,1... | collective-permute-start | bytes 786440 | tf_op jit(solution)/shard_map/ppermute | solution.py:31
  129.6 10.0 %collective-permute-start.20 = (bf16[4,128,256]{2,1,0:T(8,128)(2,1)S(1)}, bf16[4,128,256]{2,1,0:T(8,128)(2,1)S(1)}, u32[]{:S(2)}, u32[]{:S(2)}) collective-permute-start(bf16[4,128,256]{2,1,0:T(8,128)(2,1)S(1)} %get-tuple-element.102), channel_id=1, source_target_pairs={{0,3},{1,0},{2,1},{3,2},{4,7},{5,4},{6,5},{7,6},{8,11},{9,8},{10,9... | collective-permute-start | bytes 786440 | tf_op jit(solution)/shard_map/ppermute | solution.py:31
  139.7 6.3 %collective-permute-start.27 = (bf16[2,128,256]{2,1,0:T(8,128)(2,1)S(1)}, bf16[2,128,256]{2,1,0:T(8,128)(2,1)S(1)}, u32[]{:S(2)}, u32[]{:S(2)}) collective-permute-start(bf16[2,128,256]{2,1,0:T(8,128)(2,1)S(1)} %get-tuple-element.123), channel_id=1, source_target_pairs={{0,28},{4,0},{8,4},{12,8},{16,12},{20,16},{24,20},{28,24},{1,29},{... | collective-permute-start | bytes 393224 | tf_op jit(solution)/shard_map/ppermute | solution.py:31
  139.7 6.4 %collective-permute-start.23 = (bf16[2,128,256]{2,1,0:T(8,128)(2,1)S(1)}, bf16[2,128,256]{2,1,0:T(8,128)(2,1)S(1)}, u32[]{:S(2)}, u32[]{:S(2)}) collective-permute-start(bf16[2,128,256]{2,1,0:T(8,128)(2,1)S(1)} %get-tuple-element.119), channel_id=1, source_target_pairs={{0,4},{4,8},{8,12},{12,16},{16,20},{20,24},{24,28},{28,0},{1,5},{5... | collective-permute-start | bytes 393224 | tf_op jit(solution)/shard_map/ppermute | solution.py:31
  141.8 24.9 %collective-permute-start.21 = (bf16[8,128,256]{2,1,0:T(8,128)(2,1)S(1)}, bf16[8,128,256]{2,1,0:T(8,128)(2,1)S(1)}, u32[]{:S(2)}, u32[]{:S(2)}) collective-permute-start(bf16[8,128,256]{2,1,0:T(8,128)(2,1)S(1)} %add_convert_fusion.2), channel_id=1, source_target_pairs={{0,1},{1,2},{2,3},{3,0},{4,5},{5,6},{6,7},{7,4},{8,9},{9,10},{10,1... | collective-permute-start | bytes 1572872 | tf_op jit(solution)/shard_map/ppermute | solution.py:31
  146.0 6.5 %collective-permute-start.28 = (bf16[4,128,256]{2,1,0:T(8,128)(2,1)S(1)}, bf16[4,128,256]{2,1,0:T(8,128)(2,1)S(1)}, u32[]{:S(2)}, u32[]{:S(2)}) collective-permute-start(bf16[4,128,256]{2,1,0:T(8,128)(2,1)S(1)} %add_convert_fusion.8), channel_id=1, source_target_pairs={{0,28},{4,0},{8,4},{12,8},{16,12},{20,16},{24,20},{28,24},{1,29},{... | collective-permute-start | bytes 786440 | tf_op jit(solution)/shard_map/ppermute | solution.py:31
  146.1 7.7 %collective-permute-start.24 = (bf16[4,128,256]{2,1,0:T(8,128)(2,1)S(1)}, bf16[4,128,256]{2,1,0:T(8,128)(2,1)S(1)}, u32[]{:S(2)}, u32[]{:S(2)}) collective-permute-start(bf16[4,128,256]{2,1,0:T(8,128)(2,1)S(1)} %add_convert_fusion.11), channel_id=1, source_target_pairs={{0,4},{4,8},{8,12},{12,16},{16,20},{20,24},{24,28},{28,0},{1,5},{5... | collective-permute-start | bytes 786440 | tf_op jit(solution)/shard_map/ppermute | solution.py:31
  148.3 18.3 %collective-permute-start.22 = (bf16[8,128,256]{2,1,0:T(8,128)(2,1)S(1)}, bf16[8,128,256]{2,1,0:T(8,128)(2,1)S(1)}, u32[]{:S(2)}, u32[]{:S(2)}) collective-permute-start(bf16[8,128,256]{2,1,0:T(8,128)(2,1)S(1)} %add_convert_fusion.1), channel_id=1, source_target_pairs={{0,3},{1,0},{2,1},{3,2},{4,7},{5,4},{6,5},{7,6},{8,11},{9,8},{10,9... | collective-permute-start | bytes 1572872 | tf_op jit(solution)/shard_map/ppermute | solution.py:31
  152.5 11.8 %collective-permute-start.29 = (bf16[4,128,256]{2,1,0:T(8,128)(2,1)S(1)}, bf16[4,128,256]{2,1,0:T(8,128)(2,1)S(1)}, u32[]{:S(2)}, u32[]{:S(2)}) collective-permute-start(bf16[4,128,256]{2,1,0:T(8,128)(2,1)S(1)} %add_convert_fusion.7), channel_id=1, source_target_pairs={{0,28},{4,0},{8,4},{12,8},{16,12},{20,16},{24,20},{28,24},{1,29},{... | collective-permute-start | bytes 786440 | tf_op jit(solution)/shard_map/ppermute | solution.py:31
  153.9 12.3 %collective-permute-start.25 = (bf16[4,128,256]{2,1,0:T(8,128)(2,1)S(1)}, bf16[4,128,256]{2,1,0:T(8,128)(2,1)S(1)}, u32[]{:S(2)}, u32[]{:S(2)}) collective-permute-start(bf16[4,128,256]{2,1,0:T(8,128)(2,1)S(1)} %add_convert_fusion.10), channel_id=1, source_target_pairs={{0,4},{4,8},{8,12},{12,16},{16,20},{20,24},{24,28},{28,0},{1,5},{5... | collective-permute-start | bytes 786440 | tf_op jit(solution)/shard_map/ppermute | solution.py:31
  164.4 6.5 %collective-permute-start.30 = (bf16[4,128,256]{2,1,0:T(8,128)(2,1)S(1)}, bf16[4,128,256]{2,1,0:T(8,128)(2,1)S(1)}, u32[]{:S(2)}, u32[]{:S(2)}) collective-permute-start(bf16[4,128,256]{2,1,0:T(8,128)(2,1)S(1)} %add_convert_fusion.6), channel_id=1, source_target_pairs={{0,28},{4,0},{8,4},{12,8},{16,12},{20,16},{24,20},{28,24},{1,29},{... | collective-permute-start | bytes 786440 | tf_op jit(solution)/shard_map/ppermute | solution.py:31
  166.2 7.7 %collective-permute-start.26 = (bf16[4,128,256]{2,1,0:T(8,128)(2,1)S(1)}, bf16[4,128,256]{2,1,0:T(8,128)(2,1)S(1)}, u32[]{:S(2)}, u32[]{:S(2)}) collective-permute-start(bf16[4,128,256]{2,1,0:T(8,128)(2,1)S(1)} %add_convert_fusion.9), channel_id=1, source_target_pairs={{0,4},{4,8},{8,12},{12,16},{16,20},{20,24},{24,28},{28,0},{1,5},{5... | collective-permute-start | bytes 786440 | tf_op jit(solution)/shard_map/ppermute | solution.py:31
  173.9 17.8 %all-to-all-start.2 = ((bf16[8,128,256]{2,1,0:T(8,128)(2,1)}), bf16[8,128,256]{2,1,0:T(8,128)(2,1)S(1)}, u32[]{:S(2)}, u32[]{:S(2)}) async-start(bf16[8,128,256]{2,1,0:T(8,128)(2,1)} %add_convert_fusion), calls=%async_computation.2 | async-start | bytes 1048576 | tf_op jit(solution)/shard_map/all_to_all | solution.py:321
  178.4 5.6 %collective-permute-start.31 = (bf16[128,256]{1,0:T(8,128)(2,1)S(1)}, bf16[128,256]{1,0:T(8,128)(2,1)S(1)}, u32[]{:S(2)}, u32[]{:S(2)}) collective-permute-start(bf16[128,256]{1,0:T(8,128)(2,1)S(1)} %get-tuple-element.142), channel_id=1, source_target_pairs={{0,1},{1,2},{2,3},{3,0},{4,5},{5,6},{6,7},{7,4},{8,9},{9,10},{10,1... | collective-permute-start | bytes 196616 | tf_op jit(solution)/shard_map/ppermute | solution.py:31
  180.8 5.8 %collective-permute-start.32 = (bf16[128,256]{1,0:T(8,128)(2,1)S(1)}, bf16[128,256]{1,0:T(8,128)(2,1)S(1)}, u32[]{:S(2)}, u32[]{:S(2)}) collective-permute-start(bf16[128,256]{1,0:T(8,128)(2,1)S(1)} %get-tuple-element.144), channel_id=1, source_target_pairs={{0,2},{1,3},{2,0},{3,1},{4,6},{5,7},{6,4},{7,5},{8,10},{9,11},{10,... | collective-permute-start | bytes 196616 | tf_op jit(solution)/shard_map/ppermute | solution.py:31
  182.0 4.6 %collective-permute-start.33 = (bf16[128,256]{1,0:T(8,128)(2,1)S(1)}, bf16[128,256]{1,0:T(8,128)(2,1)S(1)}, u32[]{:S(2)}, u32[]{:S(2)}) collective-permute-start(bf16[128,256]{1,0:T(8,128)(2,1)S(1)} %get-tuple-element.143), channel_id=1, source_target_pairs={{0,3},{1,0},{2,1},{3,2},{4,7},{5,4},{6,5},{7,6},{8,11},{9,8},{10,9... | collective-permute-start | bytes 196616 | tf_op jit(solution)/shard_map/ppermute | solution.py:31

commit v3 on v2

--- a/solution.py
+++ b/solution.py
@@ -112,7 +112,7 @@
             )
 
     size = count * CHUNK
-    unroll = 2
+    unroll = 8
 
     @pl.loop(0, chunks // (2 * unroll))
     def _(step):
@@ -300,20 +300,18 @@
 
 
 def target_sums(apply_y, apply_z):
-    y_up, y_down, up, down, y_here = apply_y()
-    y_up_got, y_down_got = along(y_up, Y, 1), along(y_down, Y, -1)
     z_parts = apply_z()
-    y_up_got, y_down_got, *z_parts = lax.optimization_barrier((y_up_got, y_down_got, *z_parts))
     z_half = z_parts[0].shape[0]
-    going_up, going_down = z_parts[:2]
-    for k in range(2, len(z_parts) - 1, 2):
-        up_got, down_got = along(going_up, Z, 1), along(going_down, Z, -1)
-        if k == 2:
-            going_up, going_down = add_at(z_parts[k], up_got, 0), add_at(z_parts[k + 1], down_got, z_half)
-        else:
-            going_up, going_down = add(z_parts[k], up_got), add(z_parts[k + 1], down_got)
-    up = add_at(up, y_up_got, 0)
-    down = add_at(down, y_down_got, y_up.shape[0])
+    got = along(z_parts[0], Z, 1), along(z_parts[1], Z, -1)
+    y_parts = apply_y()
+    got = lax.optimization_barrier((*got, *y_parts))[:2]
+    y_up, y_down, up, down, y_here = y_parts
+    going_up, going_down = add_at(z_parts[2], got[0], 0), add_at(z_parts[3], got[1], z_half)
+    for k in range(4, len(z_parts) - 1, 2):
+        got = along(going_up, Z, 1), along(going_down, Z, -1)
+        going_up, going_down = add(z_parts[k], got[0]), add(z_parts[k + 1], got[1])
+    up = add_at(up, along(y_up, Y, 1), 0)
+    down = add_at(down, along(y_down, Y, -1), y_up.shape[0])
     column = add(y_here, along(up, Y, 1), along(down, Y, -1))
     column, *arrived = lax.optimization_barrier(
         (column, z_parts[-1], along(going_up, Z, 1), along(going_down, Z, -1))

time: 208 us -> 193 us (0.928)
  starting transfers between devices: 84.6 us -> 77.8 us
  waiting for transfers between devices: 64.1 us -> 58.8 us
    ppermute x30, starting transfers between devices: 53.9 us -> 42.4 us  [along(): lax.ppermute(value, axis, [(i, (i + steps) % count) for i in range(count)])]
    ppermute x30, waiting for transfers between devices: 48.1 us -> 36.9 us  [along(): lax.ppermute(value, axis, [(i, (i + steps) % count) for i in range(count)])]
    all_to_all x2, waiting for transfers between devices: 4.98 us -> 11 us  [target_sums(): high = lax.all_to_all(column, Z, 0, 0, tiled=True)]
    all_to_all x2, starting transfers between devices: 7.96 us -> 12.6 us  [target_sums(): high = lax.all_to_all(column, Z, 0, 0, tiled=True)]
  transfers between devices with their start and end apart: 37 -> 37, of which waited for: 21 -> 16; matrix products, arithmetic and copies ran while one was open for 3% -> 3% of each run, Pallas kernels for 9% -> 8%
where the time goes in v3:
time: 193 us
  starting transfers between devices  77.8 us (40%)
  waiting for transfers between devices  58.8 us (30%)
  Pallas kernels  34.5 us (18%)
  blocking collectives  13.5 us (7%)
  other arithmetic  4.88 us (3%)
    ppermute x30, starting transfers between devices, along(): lax.ppermute(value, axis, [(i, (i + steps) % count) for i in range(count)])  42.4 us
    ppermute x30, waiting for transfers between devices, along(): lax.ppermute(value, axis, [(i, (i + steps) % count) for i in range(count)])  36.9 us
    pallas_call x4, Pallas kernels, apply(): pl.pallas_call(functools.partial(apply_kernel, row_from, ranges), out_sha...  19.1 us
    pallas_call x2, Pallas kernels, carry(): pl.pallas_call(functools.partial(carry_kernel, flip), out_shape=jax.Shape...  13.9 us
    all_to_all x1, blocking collectives, local(): moments = lax.all_to_all(moments, SECTOR, 0, 0, tiled=True)  13.5 us
    all_to_all x2, starting transfers between devices, target_sums(): high = lax.all_to_all(column, Z, 0, 0, tiled=True)  12.6 us
    all_to_all x1, starting transfers between devices, local(): norm = jnp.sum(lax.all_to_all(norm, SECTOR, 0, 0, tiled=True), 0)[:1]  11.5 us
    ppermute x4, starting transfers between devices, to_region(): lax.ppermute(value, REGION, [(i, i + steps) for i in range(leading, last)])  11.3 us
  transfers between devices with their start and end apart: 37, of which 16 were waited for; matrix products, arithmetic and copies ran while one was open for 3% of the time, Pallas kernels for 8%

profile of v3, /device:TPU:6, one launch (start us, length us, event | category | flops | bytes accessed | tf_op | source)
XLA Modules:
  0.0 192.5 jit_solution(14226118838790356504)
XLA Ops:
  1.3 7.0 %shard_map.104 = bf16[18,256,256]{2,1,0:T(8,128)(2,1)} custom-call(s32[1]{0:T(128)} %copy.11.size_ref, f32[18,18]{1,0:T(8,128)} %coeff_ref.2, s32[18,18]{1,0:T(8,128)} %pattern_ref.3, bf16[256,256]{1,0:T(8,128)(2,1)} %bitcast.80, bf16[18,256,256]{2,1,0:T(8,128)(2,1)} %bitcast.75), custom_call_target="tpu_custom_call" | custom-call | flops 2415919104 | bytes 4718592 | tf_op jit(solution)/shard_map/pallas_call | solution.py:152
  8.2 2.2 %collective-permute-start.3 = (bf16[18,256,256]{2,1,0:T(8,128)(2,1)}, bf16[18,256,256]{2,1,0:T(8,128)(2,1)}, u32[]{:S(2)}, u32[]{:S(2)}) collective-permute-start(bf16[18,256,256]{2,1,0:T(8,128)(2,1)} %shard_map.104), channel_id=1, source_target_pairs={{32,0},{64,32},{96,64},{128,96},{160,128},{192,160},{224,192},{33,... | collective-permute-start | bytes 7077896 | tf_op jit(solution)/shard_map/ppermute | solution.py:37
  10.5 7.0 %shard_map.105 = bf16[18,256,256]{2,1,0:T(8,128)(2,1)} custom-call(s32[1]{0:T(128)} %copy.11.size_ref, f32[18,18]{1,0:T(8,128)} %coeff_ref.3, s32[18,18]{1,0:T(8,128)} %pattern_ref.3, bf16[256,256]{1,0:T(8,128)(2,1)} %bitcast.81, bf16[18,256,256]{2,1,0:T(8,128)(2,1)} %bitcast.70), custom_call_target="tpu_custom_call" | custom-call | flops 2415919104 | bytes 4718592 | tf_op jit(solution)/shard_map/pallas_call | solution.py:152
  17.5 3.5 %collective-permute-start.2 = (bf16[18,256,256]{2,1,0:T(8,128)(2,1)}, bf16[18,256,256]{2,1,0:T(8,128)(2,1)}, u32[]{:S(2)}, u32[]{:S(2)}) collective-permute-start(bf16[18,256,256]{2,1,0:T(8,128)(2,1)} %shard_map.105), channel_id=1, source_target_pairs={{0,32},{32,64},{64,96},{96,128},{128,160},{160,192},{192,224},{1,3... | collective-permute-start | bytes 7077896 | tf_op jit(solution)/shard_map/ppermute | solution.py:37
  21.8 1.4 broadcast_in_dim.4
  23.2 11.5 %all-to-all-start = ((f32[32,8,128]{2,1,0:T(8,128)}), f32[32,8,128]{2,1,0:T(8,128)S(1)}, u32[]{:S(2)}, u32[]{:S(2)}) async-start(f32[32,8,128]{2,1,0:T(8,128)} %broadcast_in_dim.4), calls=%async_computation | async-start | bytes 262144 | tf_op jit(solution)/shard_map/all_to_all | solution.py:476
  35.4 9.8 %all-to-all-done = f32[32,8,128]{2,1,0:T(8,128)S(1)} async-done(((f32[32,8,128]{2,1,0:T(8,128)}), f32[32,8,128]{2,1,0:T(8,128)S(1)}, u32[]{:S(2)}, u32[]{:S(2)}) %all-to-all-start) | async-done | bytes 131104 | tf_op jit(solution)/shard_map/all_to_all | solution.py:476
  45.3 1.9 collective-permute-start
  47.2 3.6 %collective-permute-start.1 = (f32[1,256]{1,0:T(1,128)S(1)}, f32[1,256]{1,0:T(1,128)S(1)}, u32[]{:S(2)}, u32[]{:S(2)}) collective-permute-start(f32[1,256]{1,0:T(1,128)S(1)} %pad_maximum_fusion), channel_id=1, source_target_pairs={{32,0},{64,32},{96,64},{128,96},{160,128},{192,160},{224,192},{33,... | collective-permute-start | bytes 3080 | tf_op jit(solution)/shard_map/ppermute | solution.py:37
  51.0 1.1 collective-permute-done.1.right_norm
  52.1 5.0 %shard_map.107 = (bf16[2,128,256]{2,1,0:T(8,128)(2,1)S(1)}, bf16[2,128,256]{2,1,0:T(8,128)(2,1)S(1)}, bf16[4,128,256]{2,1,0:T(8,128)(2,1)S(1)}, bf16[4,128,256]{...) custom-call(s32[2]{0:T(128)S(1)} %add_convert_fusion.24.place_ref, ...), custom_call_target="tpu_custom_call" | custom-call | flops 603979776 | bytes 9437184 | tf_op jit(solution)/shard_map/pallas_call | solution.py:260
  58.0 2.4 %collective-permute-start.9 = (bf16[2,128,256]{2,1,0:T(8,128)(2,1)S(1)}, bf16[2,128,256]{2,1,0:T(8,128)(2,1)S(1)}, u32[]{:S(2)}, u32[]{:S(2)}) collective-permute-start(bf16[2,128,256]{2,1,0:T(8,128)(2,1)S(1)} %get-tuple-element.60), channel_id=1, source_target_pairs={{0,28},{4,0},{8,4},{12,8},{16,12},{20,16},{24,20},{28,24},{1,29},{... | collective-permute-start | bytes 393224 | tf_op jit(solution)/shard_map/ppermute | solution.py:31
  60.5 4.6 %shard_map.106 = (bf16[4,128,256]{2,1,0:T(8,128)(2,1)S(1)}, bf16[4,128,256]{2,1,0:T(8,128)(2,1)S(1)}, bf16[8,128,256]{2,1,0:T(8,128)(2,1)S(1)}, bf16[8,128,256]{2,1,0:T(8,128)(2,1)S(1)}, bf16[8,128,256]{2,1,0:T(8,128)(2,1)S(1)}) custom-call(s32[2]{0:T(128)S(1)} %add_convert_fusion.24.place_ref, s32[2,18]{1,0:T(2,128)S(1)} %pad_add_fusion.table_ref, ...), custom_call_target="tpu_custom_call" | custom-call | flops 603979776 | bytes 9437184 | tf_op jit(solution)/shard_map/pallas_call | solution.py:260
  65.2 3.1 %collective-permute-start.6 = (bf16[4,128,256]{2,1,0:T(8,128)(2,1)S(1)}, bf16[4,128,256]{2,1,0:T(8,128)(2,1)S(1)}, u32[]{:S(2)}, u32[]{:S(2)}) collective-permute-start(bf16[4,128,256]{2,1,0:T(8,128)(2,1)S(1)} %get-tuple-element.54), channel_id=1, source_target_pairs={{0,3},{1,0},{2,1},{3,2},{4,7},{5,4},{6,5},{7,6},{8,11},{9,8},{10,9... | collective-permute-start | bytes 786440 | tf_op jit(solution)/shard_map/ppermute | solution.py:31
  69.0 1.6 collective-permute-start.10
  70.6 2.6 %collective-permute-done.4 = bf16[4,128,256]{2,1,0:T(8,128)(2,1)S(1)} collective-permute-done((bf16[4,128,256]{2,1,0:T(8,128)(2,1)S(1)}, bf16[4,128,256]{2,1,0:T(8,128)(2,1)S(1)}, u32[]{:S(2)}, u32[]{:S(2)}) %collective-permute-start.4) | collective-permute-done | bytes 262176 | tf_op jit(solution)/shard_map/ppermute | solution.py:31
  73.5 3.3 %collective-permute-start.7 = (bf16[8,128,256]{2,1,0:T(8,128)(2,1)S(1)}, bf16[8,128,256]{2,1,0:T(8,128)(2,1)S(1)}, u32[]{:S(2)}, u32[]{:S(2)}) collective-permute-start(bf16[8,128,256]{2,1,0:T(8,128)(2,1)S(1)} %add_convert_fusion.4), channel_id=1, source_target_pairs={{0,3},{1,0},{2,1},{3,2},{4,7},{5,4},{6,5},{7,6},{8,11},{9,8},{10,9... | collective-permute-start | bytes 1572872 | tf_op jit(solution)/shard_map/ppermute | solution.py:31
  77.5 1.8 collective-permute-start.11
  79.3 5.0 %collective-permute-done.14 = bf16[4,128,256]{2,1,0:T(8,128)(2,1)S(1)} collective-permute-done((bf16[4,128,256]{2,1,0:T(8,128)(2,1)S(1)}, bf16[4,128,256]{2,1,0:T(8,128)(2,1)S(1)}, u32[]{:S(2)}, u32[]{:S(2)}) %collective-permute-start.14) | collective-permute-done | bytes 262176 | tf_op jit(solution)/shard_map/ppermute | solution.py:31
  85.2 1.7 collective-permute-start.12
  86.9 1.0 add_convert_fusion.3
  87.9 2.9 %collective-permute-done.15 = bf16[4,128,256]{2,1,0:T(8,128)(2,1)S(1)} collective-permute-done((bf16[4,128,256]{2,1,0:T(8,128)(2,1)S(1)}, bf16[4,128,256]{2,1,0:T(8,128)(2,1)S(1)}, u32[]{:S(2)}, u32[]{:S(2)}) %collective-permute-start.15) | collective-permute-done | bytes 262176 | tf_op jit(solution)/shard_map/ppermute | solution.py:31
  90.8 2.1 %collective-permute-done.12 = bf16[4,128,256]{2,1,0:T(8,128)(2,1)S(1)} collective-permute-done((bf16[4,128,256]{2,1,0:T(8,128)(2,1)S(1)}, bf16[4,128,256]{2,1,0:T(8,128)(2,1)S(1)}, u32[]{:S(2)}, u32[]{:S(2)}) %collective-permute-start.12) | collective-permute-done | bytes 262176 | tf_op jit(solution)/shard_map/ppermute | solution.py:31
  92.9 6.8 %all-to-all-start.1 = ((bf16[8,128,256]{2,1,0:T(8,128)(2,1)}), bf16[8,128,256]{2,1,0:T(8,128)(2,1)S(1)}, u32[]{:S(2)}, u32[]{:S(2)}) async-start(bf16[8,128,256]{2,1,0:T(8,128)(2,1)} %add_convert_fusion.3), calls=%async_computation.1 | async-start | bytes 1048576 | tf_op jit(solution)/shard_map/all_to_all | solution.py:319
  100.7 3.2 %collective-permute-start.17 = (bf16[128,256]{1,0:T(8,128)(2,1)S(1)}, bf16[128,256]{1,0:T(8,128)(2,1)S(1)}, u32[]{:S(2)}, u32[]{:S(2)}) collective-permute-start(bf16[128,256]{1,0:T(8,128)(2,1)S(1)} %get-tuple-element.111), channel_id=1, source_target_pairs={{0,2},{1,3},{2,0},{3,1},{4,6},{5,7},{6,4},{7,5},{8,10},{9,11},{10,... | collective-permute-start | bytes 196616 | tf_op jit(solution)/shard_map/ppermute | solution.py:31
  103.9 1.3 collective-permute-start.18
  105.4 1.5 collective-permute-done.17
  106.8 1.3 collective-permute-done.18
  108.2 5.0 %all-to-all-done.1.refs_1_ = bf16[8,128,256]{2,1,0:T(8,128)(2,1)S(1)} async-done(((bf16[8,128,256]{2,1,0:T(8,128)(2,1)}), bf16[8,128,256]{2,1,0:T(8,128)(2,1)S(1)}, u32[]{:S(2)}, u32[]{:S(2)}) %all-to-all-start.1) | async-done | bytes 524320 | tf_op jit(solution)/shard_map/all_to_all | solution.py:319
  113.3 5.0 %shard_map.110 = (bf16[2,128,256]{2,1,0:T(8,128)(2,1)S(1)}, bf16[2,128,256]{2,1,0:T(8,128)(2,1)S(1)}, bf16[4,128,256]{2,1,0:T(8,128)(2,1)S(1)}, bf16[4,128,256]{...) custom-call(s32[2]{0:T(128)S(1)} %add_convert_fusion.24.place_ref, ...), custom_call_target="tpu_custom_call" | custom-call | flops 603979776 | bytes 9437184 | tf_op jit(solution)/shard_map/pallas_call | solution.py:260
  118.9 2.7 %collective-permute-start.24 = (bf16[2,128,256]{2,1,0:T(8,128)(2,1)S(1)}, bf16[2,128,256]{2,1,0:T(8,128)(2,1)S(1)}, u32[]{:S(2)}, u32[]{:S(2)}) collective-permute-start(bf16[2,128,256]{2,1,0:T(8,128)(2,1)S(1)} %get-tuple-element.82), channel_id=1, source_target_pairs={{0,28},{4,0},{8,4},{12,8},{16,12},{20,16},{24,20},{28,24},{1,29},{... | collective-permute-start | bytes 393224 | tf_op jit(solution)/shard_map/ppermute | solution.py:31
  121.7 4.6 %shard_map.109 = (bf16[4,128,256]{2,1,0:T(8,128)(2,1)S(1)}, bf16[4,128,256]{2,1,0:T(8,128)(2,1)S(1)}, bf16[8,128,256]{2,1,0:T(8,128)(2,1)S(1)}, bf16[8,128,256]{2,1,0:T(8,128)(2,1)S(1)}, bf16[8,128,256]{2,1,0:T(8,128)(2,1)S(1)}) custom-call(s32[2]{0:T(128)S(1)} %add_convert_fusion.24.place_ref, s32[2,18]{1,0:T(2,128)S(1)} %pad_add_fusion.table_ref, ...), custom_call_target="tpu_custom_call" | custom-call | flops 603979776 | bytes 9437184 | tf_op jit(solution)/shard_map/pallas_call | solution.py:260
  126.2 1.1 collective-permute-start.19
  127.4 2.2 %collective-permute-start.21 = (bf16[4,128,256]{2,1,0:T(8,128)(2,1)S(1)}, bf16[4,128,256]{2,1,0:T(8,128)(2,1)S(1)}, u32[]{:S(2)}, u32[]{:S(2)}) collective-permute-start(bf16[4,128,256]{2,1,0:T(8,128)(2,1)S(1)} %get-tuple-element.76), channel_id=1, source_target_pairs={{0,3},{1,0},{2,1},{3,2},{4,7},{5,4},{6,5},{7,6},{8,11},{9,8},{10,9... | collective-permute-start | bytes 786440 | tf_op jit(solution)/shard_map/ppermute | solution.py:31
  129.7 2.1 %collective-permute-start.25 = (bf16[4,128,256]{2,1,0:T(8,128)(2,1)S(1)}, bf16[4,128,256]{2,1,0:T(8,128)(2,1)S(1)}, u32[]{:S(2)}, u32[]{:S(2)}) collective-permute-start(bf16[4,128,256]{2,1,0:T(8,128)(2,1)S(1)} %add_convert_fusion.11), channel_id=1, source_target_pairs={{0,4},{4,8},{8,12},{12,16},{16,20},{20,24},{24,28},{28,0},{1,5},{5... | collective-permute-start | bytes 786440 | tf_op jit(solution)/shard_map/ppermute | solution.py:31
  131.8 5.0 %collective-permute-done.19 = bf16[4,128,256]{2,1,0:T(8,128)(2,1)S(1)} collective-permute-done((bf16[4,128,256]{2,1,0:T(8,128)(2,1)S(1)}, bf16[4,128,256]{2,1,0:T(8,128)(2,1)S(1)}, u32[]{:S(2)}, u32[]{:S(2)}) %collective-permute-start.19) | collective-permute-done | bytes 262176 | tf_op jit(solution)/shard_map/ppermute | solution.py:31
  137.2 3.3 %collective-permute-start.22 = (bf16[8,128,256]{2,1,0:T(8,128)(2,1)S(1)}, bf16[8,128,256]{2,1,0:T(8,128)(2,1)S(1)}, u32[]{:S(2)}, u32[]{:S(2)}) collective-permute-start(bf16[8,128,256]{2,1,0:T(8,128)(2,1)S(1)} %add_convert_fusion.1), channel_id=1, source_target_pairs={{0,3},{1,0},{2,1},{3,2},{4,7},{5,4},{6,5},{7,6},{8,11},{9,8},{10,9... | collective-permute-start | bytes 1572872 | tf_op jit(solution)/shard_map/ppermute | solution.py:31
  140.8 2.1 %collective-permute-start.26 = (bf16[4,128,256]{2,1,0:T(8,128)(2,1)S(1)}, bf16[4,128,256]{2,1,0:T(8,128)(2,1)S(1)}, u32[]{:S(2)}, u32[]{:S(2)}) collective-permute-start(bf16[4,128,256]{2,1,0:T(8,128)(2,1)S(1)} %add_convert_fusion.10), channel_id=1, source_target_pairs={{0,4},{4,8},{8,12},{12,16},{16,20},{20,24},{24,28},{28,0},{1,5},{5... | collective-permute-start | bytes 786440 | tf_op jit(solution)/shard_map/ppermute | solution.py:31
  142.9 4.2 %collective-permute-done.29 = bf16[4,128,256]{2,1,0:T(8,128)(2,1)S(1)} collective-permute-done((bf16[4,128,256]{2,1,0:T(8,128)(2,1)S(1)}, bf16[4,128,256]{2,1,0:T(8,128)(2,1)S(1)}, u32[]{:S(2)}, u32[]{:S(2)}) %collective-permute-start.29) | collective-permute-done | bytes 262176 | tf_op jit(solution)/shard_map/ppermute | solution.py:31
  147.1 1.3 collective-permute-start.30
  149.4 1.0 add_convert_fusion
  150.4 8.1 %collective-permute-done.30 = bf16[4,128,256]{2,1,0:T(8,128)(2,1)S(1)} collective-permute-done((bf16[4,128,256]{2,1,0:T(8,128)(2,1)S(1)}, bf16[4,128,256]{2,1,0:T(8,128)(2,1)S(1)}, u32[]{:S(2)}, u32[]{:S(2)}) %collective-permute-start.30) | collective-permute-done | bytes 262176 | tf_op jit(solution)/shard_map/ppermute | solution.py:31
  158.5 5.8 %all-to-all-start.2 = ((bf16[8,128,256]{2,1,0:T(8,128)(2,1)}), bf16[8,128,256]{2,1,0:T(8,128)(2,1)S(1)}, u32[]{:S(2)}, u32[]{:S(2)}) async-start(bf16[8,128,256]{2,1,0:T(8,128)(2,1)} %add_convert_fusion), calls=%async_computation.2 | async-start | bytes 1048576 | tf_op jit(solution)/shard_map/all_to_all | solution.py:319
  164.8 2.8 %collective-permute-start.33 = (bf16[128,256]{1,0:T(8,128)(2,1)S(1)}, bf16[128,256]{1,0:T(8,128)(2,1)S(1)}, u32[]{:S(2)}, u32[]{:S(2)}) collective-permute-start(bf16[128,256]{1,0:T(8,128)(2,1)S(1)} %get-tuple-element.107), channel_id=1, source_target_pairs={{0,3},{1,0},{2,1},{3,2},{4,7},{5,4},{6,5},{7,6},{8,11},{9,8},{10,9... | collective-permute-start | bytes 196616 | tf_op jit(solution)/shard_map/ppermute | solution.py:31
  167.6 3.0 %collective-permute-done.31 = bf16[128,256]{1,0:T(8,128)(2,1)S(1)} collective-permute-done((bf16[128,256]{1,0:T(8,128)(2,1)S(1)}, bf16[128,256]{1,0:T(8,128)(2,1)S(1)}, u32[]{:S(2)}, u32[]{:S(2)}) %collective-permute-start.31) | collective-permute-done | bytes 65568 | tf_op jit(solution)/shard_map/ppermute | solution.py:31
  170.6 1.0 collective-permute-done.33
  171.7 6.0 %all-to-all-done.2.refs_1_ = bf16[8,128,256]{2,1,0:T(8,128)(2,1)S(1)} async-done(((bf16[8,128,256]{2,1,0:T(8,128)(2,1)}), bf16[8,128,256]{2,1,0:T(8,128)(2,1)S(1)}, u32[]{:S(2)}, u32[]{:S(2)}) %all-to-all-start.2) | async-done | bytes 524320 | tf_op jit(solution)/shard_map/all_to_all | solution.py:319
  178.1 13.5 %all_to_all.20.moments_ref = f32[32,8,128]{2,1,0:T(8,128)S(1)} all-to-all(f32[32,8,128]{2,1,0:T(8,128)S(1)} %get-tuple-element.92), channel_id=1, replica_groups=mesh['x'=4,'core'=2,'z'=8,'y'=4] {'z','y'}, dimensions={0} | all-to-all | bytes 262144 | tf_op jit(solution)/shard_map/all_to_all | solution.py:501
  (83 shorter events, 10.9 us)
Async XLA Ops:
  8.2 43.9 %collective-permute-start.3 = (bf16[18,256,256]{2,1,0:T(8,128)(2,1)}, bf16[18,256,256]{2,1,0:T(8,128)(2,1)}, u32[]{:S(2)}, u32[]{:S(2)}) collective-permute-start(bf16[18,256,256]{2,1,0:T(8,128)(2,1)} %shard_map.104), channel_id=1, source_target_pairs={{32,0},{64,32},{96,64},{128,96},{160,128},{192,160},{224,192},{33,... | collective-permute-start | bytes 7077896 | tf_op jit(solution)/shard_map/ppermute | solution.py:37
  10.4 10.6 %copy-start.1 = (bf16[1,1,256,256]{3,2,1,0:T(8,128)(2,1)S(1)}, bf16[1,1,256,256]{3,2,1,0:T(8,128)(2,1)}, u32[]{:S(2)}) copy-start(bf16[1,1,256,256]{3,2,1,0:T(8,128)(2,1)} %param.9) | copy-start | bytes 393220
  10.4 24.3 %copy-start.2 = (s32[1,18]{1,0:T(1,128)S(1)}, s32[1,18]{1,0:T(1,128)}, u32[]{:S(2)}) copy-start(s32[1,18]{1,0:T(1,128)} %param.16) | copy-start | bytes 220
  17.5 34.7 %collective-permute-start.2 = (bf16[18,256,256]{2,1,0:T(8,128)(2,1)}, bf16[18,256,256]{2,1,0:T(8,128)(2,1)}, u32[]{:S(2)}, u32[]{:S(2)}) collective-permute-start(bf16[18,256,256]{2,1,0:T(8,128)(2,1)} %shard_map.105), channel_id=1, source_target_pairs={{0,32},{32,64},{64,96},{96,128},{128,160},{160,192},{192,224},{1,3... | collective-permute-start | bytes 7077896 | tf_op jit(solution)/shard_map/ppermute | solution.py:37
  23.2 22.0 %all-to-all-start = ((f32[32,8,128]{2,1,0:T(8,128)}), f32[32,8,128]{2,1,0:T(8,128)S(1)}, u32[]{:S(2)}, u32[]{:S(2)}) async-start(f32[32,8,128]{2,1,0:T(8,128)} %broadcast_in_dim.4), calls=%async_computation | async-start | bytes 262144 | tf_op jit(solution)/shard_map/all_to_all | solution.py:476
  45.3 5.7 %collective-permute-start = (f32[1,256]{1,0:T(1,128)S(1)}, f32[1,256]{1,0:T(1,128)S(1)}, u32[]{:S(2)}, u32[]{:S(2)}) collective-permute-start(f32[1,256]{1,0:T(1,128)S(1)} %pad_maximum_fusion), channel_id=1, source_target_pairs={{0,32},{32,64},{64,96},{96,128},{128,160},{160,192},{192,224},{1,3... | collective-permute-start | bytes 3080 | tf_op jit(solution)/shard_map/ppermute | solution.py:37
  47.2 4.9 %collective-permute-start.1 = (f32[1,256]{1,0:T(1,128)S(1)}, f32[1,256]{1,0:T(1,128)S(1)}, u32[]{:S(2)}, u32[]{:S(2)}) collective-permute-start(f32[1,256]{1,0:T(1,128)S(1)} %pad_maximum_fusion), channel_id=1, source_target_pairs={{32,0},{64,32},{96,64},{128,96},{160,128},{192,160},{224,192},{33,... | collective-permute-start | bytes 3080 | tf_op jit(solution)/shard_map/ppermute | solution.py:37
  57.1 11.2 %collective-permute-start.8 = (bf16[2,128,256]{2,1,0:T(8,128)(2,1)S(1)}, bf16[2,128,256]{2,1,0:T(8,128)(2,1)S(1)}, u32[]{:S(2)}, u32[]{:S(2)}) collective-permute-start(bf16[2,128,256]{2,1,0:T(8,128)(2,1)S(1)} %get-tuple-element.59), channel_id=1, source_target_pairs={{0,4},{4,8},{8,12},{12,16},{16,20},{20,24},{24,28},{28,0},{1,5},{5... | collective-permute-start | bytes 393224 | tf_op jit(solution)/shard_map/ppermute | solution.py:31
  58.0 10.3 %collective-permute-start.9 = (bf16[2,128,256]{2,1,0:T(8,128)(2,1)S(1)}, bf16[2,128,256]{2,1,0:T(8,128)(2,1)S(1)}, u32[]{:S(2)}, u32[]{:S(2)}) collective-permute-start(bf16[2,128,256]{2,1,0:T(8,128)(2,1)S(1)} %get-tuple-element.60), channel_id=1, source_target_pairs={{0,28},{4,0},{8,4},{12,8},{16,12},{20,16},{24,20},{28,24},{1,29},{... | collective-permute-start | bytes 393224 | tf_op jit(solution)/shard_map/ppermute | solution.py:31
  65.0 8.2 %collective-permute-start.4 = (bf16[4,128,256]{2,1,0:T(8,128)(2,1)S(1)}, bf16[4,128,256]{2,1,0:T(8,128)(2,1)S(1)}, u32[]{:S(2)}, u32[]{:S(2)}) collective-permute-start(bf16[4,128,256]{2,1,0:T(8,128)(2,1)S(1)} %get-tuple-element.52), channel_id=1, source_target_pairs={{0,1},{1,2},{2,3},{3,0},{4,5},{5,6},{6,7},{7,4},{8,9},{9,10},{10,1... | collective-permute-start | bytes 786440 | tf_op jit(solution)/shard_map/ppermute | solution.py:31
  65.2 8.2 %collective-permute-start.6 = (bf16[4,128,256]{2,1,0:T(8,128)(2,1)S(1)}, bf16[4,128,256]{2,1,0:T(8,128)(2,1)S(1)}, u32[]{:S(2)}, u32[]{:S(2)}) collective-permute-start(bf16[4,128,256]{2,1,0:T(8,128)(2,1)S(1)} %get-tuple-element.54), channel_id=1, source_target_pairs={{0,3},{1,0},{2,1},{3,2},{4,7},{5,4},{6,5},{7,6},{8,11},{9,8},{10,9... | collective-permute-start | bytes 786440 | tf_op jit(solution)/shard_map/ppermute | solution.py:31
  68.4 8.4 %collective-permute-start.13 = (bf16[4,128,256]{2,1,0:T(8,128)(2,1)S(1)}, bf16[4,128,256]{2,1,0:T(8,128)(2,1)S(1)}, u32[]{:S(2)}, u32[]{:S(2)}) collective-permute-start(bf16[4,128,256]{2,1,0:T(8,128)(2,1)S(1)} %add_convert_fusion.14), channel_id=1, source_target_pairs={{0,28},{4,0},{8,4},{12,8},{16,12},{20,16},{24,20},{28,24},{1,29},{... | collective-permute-start | bytes 786440 | tf_op jit(solution)/shard_map/ppermute | solution.py:31
  69.0 8.4 %collective-permute-start.10 = (bf16[4,128,256]{2,1,0:T(8,128)(2,1)S(1)}, bf16[4,128,256]{2,1,0:T(8,128)(2,1)S(1)}, u32[]{:S(2)}, u32[]{:S(2)}) collective-permute-start(bf16[4,128,256]{2,1,0:T(8,128)(2,1)S(1)} %add_convert_fusion.17), channel_id=1, source_target_pairs={{0,4},{4,8},{8,12},{12,16},{16,20},{20,24},{24,28},{28,0},{1,5},{5... | collective-permute-start | bytes 786440 | tf_op jit(solution)/shard_map/ppermute | solution.py:31
  73.3 13.6 %collective-permute-start.5 = (bf16[8,128,256]{2,1,0:T(8,128)(2,1)S(1)}, bf16[8,128,256]{2,1,0:T(8,128)(2,1)S(1)}, u32[]{:S(2)}, u32[]{:S(2)}) collective-permute-start(bf16[8,128,256]{2,1,0:T(8,128)(2,1)S(1)} %add_convert_fusion.5), channel_id=1, source_target_pairs={{0,1},{1,2},{2,3},{3,0},{4,5},{5,6},{6,7},{7,4},{8,9},{9,10},{10,1... | collective-permute-start | bytes 1572872 | tf_op jit(solution)/shard_map/ppermute | solution.py:31
  73.5 13.4 %collective-permute-start.7 = (bf16[8,128,256]{2,1,0:T(8,128)(2,1)S(1)}, bf16[8,128,256]{2,1,0:T(8,128)(2,1)S(1)}, u32[]{:S(2)}, u32[]{:S(2)}) collective-permute-start(bf16[8,128,256]{2,1,0:T(8,128)(2,1)S(1)} %add_convert_fusion.4), channel_id=1, source_target_pairs={{0,3},{1,0},{2,1},{3,2},{4,7},{5,4},{6,5},{7,6},{8,11},{9,8},{10,9... | collective-permute-start | bytes 1572872 | tf_op jit(solution)/shard_map/ppermute | solution.py:31
  76.9 7.4 %collective-permute-start.14 = (bf16[4,128,256]{2,1,0:T(8,128)(2,1)S(1)}, bf16[4,128,256]{2,1,0:T(8,128)(2,1)S(1)}, u32[]{:S(2)}, u32[]{:S(2)}) collective-permute-start(bf16[4,128,256]{2,1,0:T(8,128)(2,1)S(1)} %add_convert_fusion.13), channel_id=1, source_target_pairs={{0,28},{4,0},{8,4},{12,8},{16,12},{20,16},{24,20},{28,24},{1,29},{... | collective-permute-start | bytes 786440 | tf_op jit(solution)/shard_map/ppermute | solution.py:31
  77.5 7.7 %collective-permute-start.11 = (bf16[4,128,256]{2,1,0:T(8,128)(2,1)S(1)}, bf16[4,128,256]{2,1,0:T(8,128)(2,1)S(1)}, u32[]{:S(2)}, u32[]{:S(2)}) collective-permute-start(bf16[4,128,256]{2,1,0:T(8,128)(2,1)S(1)} %add_convert_fusion.16), channel_id=1, source_target_pairs={{0,4},{4,8},{8,12},{12,16},{16,20},{20,24},{24,28},{28,0},{1,5},{5... | collective-permute-start | bytes 786440 | tf_op jit(solution)/shard_map/ppermute | solution.py:31
  84.4 6.5 %collective-permute-start.15 = (bf16[4,128,256]{2,1,0:T(8,128)(2,1)S(1)}, bf16[4,128,256]{2,1,0:T(8,128)(2,1)S(1)}, u32[]{:S(2)}, u32[]{:S(2)}) collective-permute-start(bf16[4,128,256]{2,1,0:T(8,128)(2,1)S(1)} %add_convert_fusion.12), channel_id=1, source_target_pairs={{0,28},{4,0},{8,4},{12,8},{16,12},{20,16},{24,20},{28,24},{1,29},{... | collective-permute-start | bytes 786440 | tf_op jit(solution)/shard_map/ppermute | solution.py:31
  85.2 28.0 %copy-start = (bf16[1,1,256,256]{3,2,1,0:T(8,128)(2,1)S(1)}, bf16[1,1,256,256]{3,2,1,0:T(8,128)(2,1)}, u32[]{:S(2)}) copy-start(bf16[1,1,256,256]{3,2,1,0:T(8,128)(2,1)} %param.12) | copy-start | bytes 393220
  85.2 7.7 %collective-permute-start.12 = (bf16[4,128,256]{2,1,0:T(8,128)(2,1)S(1)}, bf16[4,128,256]{2,1,0:T(8,128)(2,1)S(1)}, u32[]{:S(2)}, u32[]{:S(2)}) collective-permute-start(bf16[4,128,256]{2,1,0:T(8,128)(2,1)S(1)} %add_convert_fusion.15), channel_id=1, source_target_pairs={{0,4},{4,8},{8,12},{12,16},{16,20},{20,24},{24,28},{28,0},{1,5},{5... | collective-permute-start | bytes 786440 | tf_op jit(solution)/shard_map/ppermute | solution.py:31
  92.9 20.3 %all-to-all-start.1 = ((bf16[8,128,256]{2,1,0:T(8,128)(2,1)}), bf16[8,128,256]{2,1,0:T(8,128)(2,1)S(1)}, u32[]{:S(2)}, u32[]{:S(2)}) async-start(bf16[8,128,256]{2,1,0:T(8,128)(2,1)} %add_convert_fusion.3), calls=%async_computation.1 | async-start | bytes 1048576 | tf_op jit(solution)/shard_map/all_to_all | solution.py:319
  99.8 5.6 %collective-permute-start.16 = (bf16[128,256]{1,0:T(8,128)(2,1)S(1)}, bf16[128,256]{1,0:T(8,128)(2,1)S(1)}, u32[]{:S(2)}, u32[]{:S(2)}) collective-permute-start(bf16[128,256]{1,0:T(8,128)(2,1)S(1)} %get-tuple-element.109), channel_id=1, source_target_pairs={{0,1},{1,2},{2,3},{3,0},{4,5},{5,6},{6,7},{7,4},{8,9},{9,10},{10,1... | collective-permute-start | bytes 196616 | tf_op jit(solution)/shard_map/ppermute | solution.py:31
  100.7 6.1 %collective-permute-start.17 = (bf16[128,256]{1,0:T(8,128)(2,1)S(1)}, bf16[128,256]{1,0:T(8,128)(2,1)S(1)}, u32[]{:S(2)}, u32[]{:S(2)}) collective-permute-start(bf16[128,256]{1,0:T(8,128)(2,1)S(1)} %get-tuple-element.111), channel_id=1, source_target_pairs={{0,2},{1,3},{2,0},{3,1},{4,6},{5,7},{6,4},{7,5},{8,10},{9,11},{10,... | collective-permute-start | bytes 196616 | tf_op jit(solution)/shard_map/ppermute | solution.py:31
  103.9 4.3 %collective-permute-start.18 = (bf16[128,256]{1,0:T(8,128)(2,1)S(1)}, bf16[128,256]{1,0:T(8,128)(2,1)S(1)}, u32[]{:S(2)}, u32[]{:S(2)}) collective-permute-start(bf16[128,256]{1,0:T(8,128)(2,1)S(1)} %get-tuple-element.110), channel_id=1, source_target_pairs={{0,3},{1,0},{2,1},{3,2},{4,7},{5,4},{6,5},{7,6},{8,11},{9,8},{10,9... | collective-permute-start | bytes 196616 | tf_op jit(solution)/shard_map/ppermute | solution.py:31
  118.4 11.2 %collective-permute-start.23 = (bf16[2,128,256]{2,1,0:T(8,128)(2,1)S(1)}, bf16[2,128,256]{2,1,0:T(8,128)(2,1)S(1)}, u32[]{:S(2)}, u32[]{:S(2)}) collective-permute-start(bf16[2,128,256]{2,1,0:T(8,128)(2,1)S(1)} %get-tuple-element.81), channel_id=1, source_target_pairs={{0,4},{4,8},{8,12},{12,16},{16,20},{20,24},{24,28},{28,0},{1,5},{5... | collective-permute-start | bytes 393224 | tf_op jit(solution)/shard_map/ppermute | solution.py:31
  118.9 10.6 %collective-permute-start.24 = (bf16[2,128,256]{2,1,0:T(8,128)(2,1)S(1)}, bf16[2,128,256]{2,1,0:T(8,128)(2,1)S(1)}, u32[]{:S(2)}, u32[]{:S(2)}) collective-permute-start(bf16[2,128,256]{2,1,0:T(8,128)(2,1)S(1)} %get-tuple-element.82), channel_id=1, source_target_pairs={{0,28},{4,0},{8,4},{12,8},{16,12},{20,16},{24,20},{28,24},{1,29},{... | collective-permute-start | bytes 393224 | tf_op jit(solution)/shard_map/ppermute | solution.py:31
  126.2 10.5 %collective-permute-start.19 = (bf16[4,128,256]{2,1,0:T(8,128)(2,1)S(1)}, bf16[4,128,256]{2,1,0:T(8,128)(2,1)S(1)}, u32[]{:S(2)}, u32[]{:S(2)}) collective-permute-start(bf16[4,128,256]{2,1,0:T(8,128)(2,1)S(1)} %get-tuple-element.74), channel_id=1, source_target_pairs={{0,1},{1,2},{2,3},{3,0},{4,5},{5,6},{6,7},{7,4},{8,9},{9,10},{10,1... | collective-permute-start | bytes 786440 | tf_op jit(solution)/shard_map/ppermute | solution.py:31
  127.4 9.8 %collective-permute-start.21 = (bf16[4,128,256]{2,1,0:T(8,128)(2,1)S(1)}, bf16[4,128,256]{2,1,0:T(8,128)(2,1)S(1)}, u32[]{:S(2)}, u32[]{:S(2)}) collective-permute-start(bf16[4,128,256]{2,1,0:T(8,128)(2,1)S(1)} %get-tuple-element.76), channel_id=1, source_target_pairs={{0,3},{1,0},{2,1},{3,2},{4,7},{5,4},{6,5},{7,6},{8,11},{9,8},{10,9... | collective-permute-start | bytes 786440 | tf_op jit(solution)/shard_map/ppermute | solution.py:31
  129.6 10.9 %collective-permute-start.28 = (bf16[4,128,256]{2,1,0:T(8,128)(2,1)S(1)}, bf16[4,128,256]{2,1,0:T(8,128)(2,1)S(1)}, u32[]{:S(2)}, u32[]{:S(2)}) collective-permute-start(bf16[4,128,256]{2,1,0:T(8,128)(2,1)S(1)} %add_convert_fusion.8), channel_id=1, source_target_pairs={{0,28},{4,0},{8,4},{12,8},{16,12},{20,16},{24,20},{28,24},{1,29},{... | collective-permute-start | bytes 786440 | tf_op jit(solution)/shard_map/ppermute | solution.py:31
  129.7 11.0 %collective-permute-start.25 = (bf16[4,128,256]{2,1,0:T(8,128)(2,1)S(1)}, bf16[4,128,256]{2,1,0:T(8,128)(2,1)S(1)}, u32[]{:S(2)}, u32[]{:S(2)}) collective-permute-start(bf16[4,128,256]{2,1,0:T(8,128)(2,1)S(1)} %add_convert_fusion.11), channel_id=1, source_target_pairs={{0,4},{4,8},{8,12},{12,16},{16,20},{20,24},{24,28},{28,0},{1,5},{5... | collective-permute-start | bytes 786440 | tf_op jit(solution)/shard_map/ppermute | solution.py:31
  136.8 12.5 %collective-permute-start.20 = (bf16[8,128,256]{2,1,0:T(8,128)(2,1)S(1)}, bf16[8,128,256]{2,1,0:T(8,128)(2,1)S(1)}, u32[]{:S(2)}, u32[]{:S(2)}) collective-permute-start(bf16[8,128,256]{2,1,0:T(8,128)(2,1)S(1)} %add_convert_fusion.2), channel_id=1, source_target_pairs={{0,1},{1,2},{2,3},{3,0},{4,5},{5,6},{6,7},{7,4},{8,9},{9,10},{10,1... | collective-permute-start | bytes 1572872 | tf_op jit(solution)/shard_map/ppermute | solution.py:31
  137.2 12.1 %collective-permute-start.22 = (bf16[8,128,256]{2,1,0:T(8,128)(2,1)S(1)}, bf16[8,128,256]{2,1,0:T(8,128)(2,1)S(1)}, u32[]{:S(2)}, u32[]{:S(2)}) collective-permute-start(bf16[8,128,256]{2,1,0:T(8,128)(2,1)S(1)} %add_convert_fusion.1), channel_id=1, source_target_pairs={{0,3},{1,0},{2,1},{3,2},{4,7},{5,4},{6,5},{7,6},{8,11},{9,8},{10,9... | collective-permute-start | bytes 1572872 | tf_op jit(solution)/shard_map/ppermute | solution.py:31
  140.6 6.5 %collective-permute-start.29 = (bf16[4,128,256]{2,1,0:T(8,128)(2,1)S(1)}, bf16[4,128,256]{2,1,0:T(8,128)(2,1)S(1)}, u32[]{:S(2)}, u32[]{:S(2)}) collective-permute-start(bf16[4,128,256]{2,1,0:T(8,128)(2,1)S(1)} %add_convert_fusion.7), channel_id=1, source_target_pairs={{0,28},{4,0},{8,4},{12,8},{16,12},{20,16},{24,20},{28,24},{1,29},{... | collective-permute-start | bytes 786440 | tf_op jit(solution)/shard_map/ppermute | solution.py:31
  140.8 7.7 %collective-permute-start.26 = (bf16[4,128,256]{2,1,0:T(8,128)(2,1)S(1)}, bf16[4,128,256]{2,1,0:T(8,128)(2,1)S(1)}, u32[]{:S(2)}, u32[]{:S(2)}) collective-permute-start(bf16[4,128,256]{2,1,0:T(8,128)(2,1)S(1)} %add_convert_fusion.10), channel_id=1, source_target_pairs={{0,4},{4,8},{8,12},{12,16},{16,20},{20,24},{24,28},{28,0},{1,5},{5... | collective-permute-start | bytes 786440 | tf_op jit(solution)/shard_map/ppermute | solution.py:31
  147.1 11.3 %collective-permute-start.30 = (bf16[4,128,256]{2,1,0:T(8,128)(2,1)S(1)}, bf16[4,128,256]{2,1,0:T(8,128)(2,1)S(1)}, u32[]{:S(2)}, u32[]{:S(2)}) collective-permute-start(bf16[4,128,256]{2,1,0:T(8,128)(2,1)S(1)} %add_convert_fusion.6), channel_id=1, source_target_pairs={{0,28},{4,0},{8,4},{12,8},{16,12},{20,16},{24,20},{28,24},{1,29},{... | collective-permute-start | bytes 786440 | tf_op jit(solution)/shard_map/ppermute | solution.py:31
  148.5 10.0 %collective-permute-start.27 = (bf16[4,128,256]{2,1,0:T(8,128)(2,1)S(1)}, bf16[4,128,256]{2,1,0:T(8,128)(2,1)S(1)}, u32[]{:S(2)}, u32[]{:S(2)}) collective-permute-start(bf16[4,128,256]{2,1,0:T(8,128)(2,1)S(1)} %add_convert_fusion.9), channel_id=1, source_target_pairs={{0,4},{4,8},{8,12},{12,16},{16,20},{20,24},{24,28},{28,0},{1,5},{5... | collective-permute-start | bytes 786440 | tf_op jit(solution)/shard_map/ppermute | solution.py:31
  158.5 19.2 %all-to-all-start.2 = ((bf16[8,128,256]{2,1,0:T(8,128)(2,1)}), bf16[8,128,256]{2,1,0:T(8,128)(2,1)S(1)}, u32[]{:S(2)}, u32[]{:S(2)}) async-start(bf16[8,128,256]{2,1,0:T(8,128)(2,1)} %add_convert_fusion), calls=%async_computation.2 | async-start | bytes 1048576 | tf_op jit(solution)/shard_map/all_to_all | solution.py:319
  164.3 6.3 %collective-permute-start.31 = (bf16[128,256]{1,0:T(8,128)(2,1)S(1)}, bf16[128,256]{1,0:T(8,128)(2,1)S(1)}, u32[]{:S(2)}, u32[]{:S(2)}) collective-permute-start(bf16[128,256]{1,0:T(8,128)(2,1)S(1)} %get-tuple-element.106), channel_id=1, source_target_pairs={{0,1},{1,2},{2,3},{3,0},{4,5},{5,6},{6,7},{7,4},{8,9},{9,10},{10,1... | collective-permute-start | bytes 196616 | tf_op jit(solution)/shard_map/ppermute | solution.py:31
  164.4 6.3 %collective-permute-start.32 = (bf16[128,256]{1,0:T(8,128)(2,1)S(1)}, bf16[128,256]{1,0:T(8,128)(2,1)S(1)}, u32[]{:S(2)}, u32[]{:S(2)}) collective-permute-start(bf16[128,256]{1,0:T(8,128)(2,1)S(1)} %get-tuple-element.108), channel_id=1, source_target_pairs={{0,2},{1,3},{2,0},{3,1},{4,6},{5,7},{6,4},{7,5},{8,10},{9,11},{10,... | collective-permute-start | bytes 196616 | tf_op jit(solution)/shard_map/ppermute | solution.py:31
  164.8 6.8 %collective-permute-start.33 = (bf16[128,256]{1,0:T(8,128)(2,1)S(1)}, bf16[128,256]{1,0:T(8,128)(2,1)S(1)}, u32[]{:S(2)}, u32[]{:S(2)}) collective-permute-start(bf16[128,256]{1,0:T(8,128)(2,1)S(1)} %get-tuple-element.107), channel_id=1, source_target_pairs={{0,3},{1,0},{2,1},{3,2},{4,7},{5,4},{6,5},{7,6},{8,11},{9,8},{10,9... | collective-permute-start | bytes 196616 | tf_op jit(solution)/shard_map/ppermute | solution.py:31

commit v4 on v3

--- a/solution.py
+++ b/solution.py
@@ -78,14 +78,25 @@
 
 
 def carry_kernel(
-    flip, size_ref, coeff_ref, pattern_ref, psi_ref, source, target,
-    env_ref, out_ref, mix_ref, first_ref, second_ref, half_ref, mixed_ref, in_sem, out_sem,
+    flip, size_ref, coeff_from, pattern_from, psi_from, source, target,
+    env_ref, out_ref, mix_ref, first_ref, second_ref, half_ref, mixed_ref,
+    coeff_ref, pattern_ref, psi_ref, in_sem, out_sem, small_sem,
 ):
     count, width, _ = env_ref.shape
     pairs, chunks = count // 2, width // CHUNK
+    small = [
+        pltpu.make_async_copy(here, there, small_sem.at[k])
+        for k, (here, there) in enumerate(
+            ((psi_from, psi_ref), (coeff_from, coeff_ref), (pattern_from, pattern_ref))
+        )
+    ]
+    for copy in small:
+        copy.start()
     for pair in range(pairs):
         two = pl.ds(2 * pair, 2)
         pltpu.make_async_copy(source.at[two], env_ref.at[two], in_sem.at[pair]).start()
+    for copy in small:
+        copy.wait()
     masked = jnp.where(live(size_ref[0], width), psi_ref[...].astype(F32), 0.0)
     turned = masked.T
     first_ref[...] = (turned if flip else masked).astype(BF16)
@@ -152,7 +163,7 @@
     return pl.pallas_call(
         functools.partial(carry_kernel, flip),
         out_shape=jax.ShapeDtypeStruct(env.shape, BF16),
-        in_specs=[SMEM_SPEC] + [pl.BlockSpec()] * 3 + [HBM_SPEC],
+        in_specs=[SMEM_SPEC] + [HBM_SPEC] * 4,
         out_specs=HBM_SPEC,
         scratch_shapes=[
             pltpu.VMEM(env.shape, BF16),
@@ -162,8 +173,12 @@
             pltpu.VMEM((width, width), BF16),
             pltpu.VMEM((chunks, count // 2, 2 * CHUNK, width), BF16),
             pltpu.VMEM((count, width, width), BF16),
+            pltpu.VMEM(coeff.shape, F32),
+            pltpu.VMEM(pattern.shape, jnp.int32),
+            pltpu.VMEM(psi.shape, BF16),
             pltpu.SemaphoreType.DMA((count // 2,)),
             pltpu.SemaphoreType.DMA((count,)),
+            pltpu.SemaphoreType.DMA((3,)),
         ],
         compiler_params=CARRY_PARAMS,
         cost_estimate=pl.CostEstimate(

time: 193 us -> 193 us (level)
  no operation moved by 1% of the time
where the time goes in v4:
time: 193 us; the launch traced here: 192 us
  starting transfers between devices  77.8 us (40%)
  waiting for transfers between devices  58.8 us (30%)
  Pallas kernels  34 us (18%)
  blocking collectives  13.5 us (7%)
  other arithmetic  4.88 us (3%)
    ppermute x30, starting transfers between devices, along(): lax.ppermute(value, axis, [(i, (i + steps) % count) for i in range(count)])  42.4 us
    ppermute x30, waiting for transfers between devices, along(): lax.ppermute(value, axis, [(i, (i + steps) % count) for i in range(count)])  36.8 us
    pallas_call x4, Pallas kernels, apply(): pl.pallas_call(functools.partial(apply_kernel, row_from, ranges), out_sha...  19.1 us
    all_to_all x1, blocking collectives, local(): moments = lax.all_to_all(moments, SECTOR, 0, 0, tiled=True)  13.5 us
    pallas_call x2, Pallas kernels, carry(): pl.pallas_call(functools.partial(carry_kernel, flip), out_shape=jax.Shape...  13.5 us
    all_to_all x2, starting transfers between devices, target_sums(): high = lax.all_to_all(column, Z, 0, 0, tiled=True)  12.6 us
    all_to_all x1, starting transfers between devices, local(): norm = jnp.sum(lax.all_to_all(norm, SECTOR, 0, 0, tiled=True), 0)[:1]  11.5 us
    ppermute x4, starting transfers between devices, to_region(): lax.ppermute(value, REGION, [(i, i + steps) for i in range(leading, last)])  11.3 us
  transfers between devices with their start and end apart: 37, of which 16 were waited for; matrix products, arithmetic and copies ran while one was open for 3% of the time, Pallas kernels for 8%

profile of v4, /device:TPU:6, one launch (start us, length us, event | category | flops | bytes accessed | tf_op | source)
XLA Modules:
  0.0 192.0 jit_solution(3196350383400126884)
XLA Ops:
  1.3 6.7 %shard_map.104 = bf16[18,256,256]{2,1,0:T(8,128)(2,1)} custom-call(s32[1]{0:T(128)} %copy.11.size_ref, f32[18,18]{1,0:T(8,128)} %coeff_from.2, s32[18,18]{1,0:T(8,128)} %pattern_from.3, bf16[256,256]{1,0:T(8,128)(2,1)} %bitcast.80, bf16[18,256,256]{2,1,0:T(8,128)(2,1)} %bitcast.75), custom_call_target="tpu_custom_call" | custom-call | flops 2415919104 | bytes 4718592 | tf_op jit(solution)/shard_map/pallas_call | solution.py:163
  7.9 2.2 %collective-permute-start.3 = (bf16[18,256,256]{2,1,0:T(8,128)(2,1)}, bf16[18,256,256]{2,1,0:T(8,128)(2,1)}, u32[]{:S(2)}, u32[]{:S(2)}) collective-permute-start(bf16[18,256,256]{2,1,0:T(8,128)(2,1)} %shard_map.104), channel_id=1, source_target_pairs={{32,0},{64,32},{96,64},{128,96},{160,128},{192,160},{224,192},{33,... | collective-permute-start | bytes 7077896 | tf_op jit(solution)/shard_map/ppermute | solution.py:37
  10.2 6.8 %shard_map.105 = bf16[18,256,256]{2,1,0:T(8,128)(2,1)} custom-call(s32[1]{0:T(128)} %copy.11.size_ref, f32[18,18]{1,0:T(8,128)} %coeff_from.3, s32[18,18]{1,0:T(8,128)} %pattern_from.3, bf16[256,256]{1,0:T(8,128)(2,1)} %bitcast.81, bf16[18,256,256]{2,1,0:T(8,128)(2,1)} %bitcast.70), custom_call_target="tpu_custom_call" | custom-call | flops 2415919104 | bytes 4718592 | tf_op jit(solution)/shard_map/pallas_call | solution.py:163
  17.0 3.5 %collective-permute-start.2 = (bf16[18,256,256]{2,1,0:T(8,128)(2,1)}, bf16[18,256,256]{2,1,0:T(8,128)(2,1)}, u32[]{:S(2)}, u32[]{:S(2)}) collective-permute-start(bf16[18,256,256]{2,1,0:T(8,128)(2,1)} %shard_map.105), channel_id=1, source_target_pairs={{0,32},{32,64},{64,96},{96,128},{128,160},{160,192},{192,224},{1,3... | collective-permute-start | bytes 7077896 | tf_op jit(solution)/shard_map/ppermute | solution.py:37
  21.4 1.4 broadcast_in_dim.4
  22.7 11.5 %all-to-all-start = ((f32[32,8,128]{2,1,0:T(8,128)}), f32[32,8,128]{2,1,0:T(8,128)S(1)}, u32[]{:S(2)}, u32[]{:S(2)}) async-start(f32[32,8,128]{2,1,0:T(8,128)} %broadcast_in_dim.4), calls=%async_computation | async-start | bytes 262144 | tf_op jit(solution)/shard_map/all_to_all | solution.py:491
  34.9 9.8 %all-to-all-done = f32[32,8,128]{2,1,0:T(8,128)S(1)} async-done(((f32[32,8,128]{2,1,0:T(8,128)}), f32[32,8,128]{2,1,0:T(8,128)S(1)}, u32[]{:S(2)}, u32[]{:S(2)}) %all-to-all-start) | async-done | bytes 131104 | tf_op jit(solution)/shard_map/all_to_all | solution.py:491
  44.8 1.9 %collective-permute-start = (f32[1,256]{1,0:T(1,128)S(1)}, f32[1,256]{1,0:T(1,128)S(1)}, u32[]{:S(2)}, u32[]{:S(2)}) collective-permute-start(f32[1,256]{1,0:T(1,128)S(1)} %pad_maximum_fusion), channel_id=1, source_target_pairs={{0,32},{32,64},{64,96},{96,128},{128,160},{160,192},{192,224},{1,3... | collective-permute-start | bytes 3080 | tf_op jit(solution)/shard_map/ppermute | solution.py:37
  46.7 3.6 %collective-permute-start.1 = (f32[1,256]{1,0:T(1,128)S(1)}, f32[1,256]{1,0:T(1,128)S(1)}, u32[]{:S(2)}, u32[]{:S(2)}) collective-permute-start(f32[1,256]{1,0:T(1,128)S(1)} %pad_maximum_fusion), channel_id=1, source_target_pairs={{32,0},{64,32},{96,64},{128,96},{160,128},{192,160},{224,192},{33,... | collective-permute-start | bytes 3080 | tf_op jit(solution)/shard_map/ppermute | solution.py:37
  50.5 1.1 collective-permute-done.1.right_norm
  51.7 5.0 %shard_map.107 = (bf16[2,128,256]{2,1,0:T(8,128)(2,1)S(1)}, bf16[2,128,256]{2,1,0:T(8,128)(2,1)S(1)}, bf16[4,128,256]{2,1,0:T(8,128)(2,1)S(1)}, bf16[4,128,256]{...) custom-call(s32[2]{0:T(128)S(1)} %add_convert_fusion.24.place_ref, ...), custom_call_target="tpu_custom_call" | custom-call | flops 603979776 | bytes 9437184 | tf_op jit(solution)/shard_map/pallas_call | solution.py:275
  57.5 2.4 %collective-permute-start.9 = (bf16[2,128,256]{2,1,0:T(8,128)(2,1)S(1)}, bf16[2,128,256]{2,1,0:T(8,128)(2,1)S(1)}, u32[]{:S(2)}, u32[]{:S(2)}) collective-permute-start(bf16[2,128,256]{2,1,0:T(8,128)(2,1)S(1)} %get-tuple-element.60), channel_id=1, source_target_pairs={{0,28},{4,0},{8,4},{12,8},{16,12},{20,16},{24,20},{28,24},{1,29},{... | collective-permute-start | bytes 393224 | tf_op jit(solution)/shard_map/ppermute | solution.py:31
  60.0 4.6 %shard_map.106 = (bf16[4,128,256]{2,1,0:T(8,128)(2,1)S(1)}, bf16[4,128,256]{2,1,0:T(8,128)(2,1)S(1)}, bf16[8,128,256]{2,1,0:T(8,128)(2,1)S(1)}, bf16[8,128,256]{2,1,0:T(8,128)(2,1)S(1)}, bf16[8,128,256]{2,1,0:T(8,128)(2,1)S(1)}) custom-call(s32[2]{0:T(128)S(1)} %add_convert_fusion.24.place_ref, s32[2,18]{1,0:T(2,128)S(1)} %pad_add_fusion.table_ref, ...), custom_call_target="tpu_custom_call" | custom-call | flops 603979776 | bytes 9437184 | tf_op jit(solution)/shard_map/pallas_call | solution.py:275
  64.7 3.1 %collective-permute-start.6 = (bf16[4,128,256]{2,1,0:T(8,128)(2,1)S(1)}, bf16[4,128,256]{2,1,0:T(8,128)(2,1)S(1)}, u32[]{:S(2)}, u32[]{:S(2)}) collective-permute-start(bf16[4,128,256]{2,1,0:T(8,128)(2,1)S(1)} %get-tuple-element.54), channel_id=1, source_target_pairs={{0,3},{1,0},{2,1},{3,2},{4,7},{5,4},{6,5},{7,6},{8,11},{9,8},{10,9... | collective-permute-start | bytes 786440 | tf_op jit(solution)/shard_map/ppermute | solution.py:31
  68.5 1.6 collective-permute-start.10
  70.1 2.6 %collective-permute-done.4 = bf16[4,128,256]{2,1,0:T(8,128)(2,1)S(1)} collective-permute-done((bf16[4,128,256]{2,1,0:T(8,128)(2,1)S(1)}, bf16[4,128,256]{2,1,0:T(8,128)(2,1)S(1)}, u32[]{:S(2)}, u32[]{:S(2)}) %collective-permute-start.4) | collective-permute-done | bytes 262176 | tf_op jit(solution)/shard_map/ppermute | solution.py:31
  73.0 3.3 %collective-permute-start.7 = (bf16[8,128,256]{2,1,0:T(8,128)(2,1)S(1)}, bf16[8,128,256]{2,1,0:T(8,128)(2,1)S(1)}, u32[]{:S(2)}, u32[]{:S(2)}) collective-permute-start(bf16[8,128,256]{2,1,0:T(8,128)(2,1)S(1)} %add_convert_fusion.4), channel_id=1, source_target_pairs={{0,3},{1,0},{2,1},{3,2},{4,7},{5,4},{6,5},{7,6},{8,11},{9,8},{10,9... | collective-permute-start | bytes 1572872 | tf_op jit(solution)/shard_map/ppermute | solution.py:31
  77.0 1.8 collective-permute-start.11
  78.8 5.0 %collective-permute-done.14 = bf16[4,128,256]{2,1,0:T(8,128)(2,1)S(1)} collective-permute-done((bf16[4,128,256]{2,1,0:T(8,128)(2,1)S(1)}, bf16[4,128,256]{2,1,0:T(8,128)(2,1)S(1)}, u32[]{:S(2)}, u32[]{:S(2)}) %collective-permute-start.14) | collective-permute-done | bytes 262176 | tf_op jit(solution)/shard_map/ppermute | solution.py:31
  84.7 1.7 collective-permute-start.12
  86.4 1.0 add_convert_fusion.3
  87.4 2.9 %collective-permute-done.15 = bf16[4,128,256]{2,1,0:T(8,128)(2,1)S(1)} collective-permute-done((bf16[4,128,256]{2,1,0:T(8,128)(2,1)S(1)}, bf16[4,128,256]{2,1,0:T(8,128)(2,1)S(1)}, u32[]{:S(2)}, u32[]{:S(2)}) %collective-permute-start.15) | collective-permute-done | bytes 262176 | tf_op jit(solution)/shard_map/ppermute | solution.py:31
  90.3 2.1 %collective-permute-done.12 = bf16[4,128,256]{2,1,0:T(8,128)(2,1)S(1)} collective-permute-done((bf16[4,128,256]{2,1,0:T(8,128)(2,1)S(1)}, bf16[4,128,256]{2,1,0:T(8,128)(2,1)S(1)}, u32[]{:S(2)}, u32[]{:S(2)}) %collective-permute-start.12) | collective-permute-done | bytes 262176 | tf_op jit(solution)/shard_map/ppermute | solution.py:31
  92.4 6.9 %all-to-all-start.1 = ((bf16[8,128,256]{2,1,0:T(8,128)(2,1)}), bf16[8,128,256]{2,1,0:T(8,128)(2,1)S(1)}, u32[]{:S(2)}, u32[]{:S(2)}) async-start(bf16[8,128,256]{2,1,0:T(8,128)(2,1)} %add_convert_fusion.3), calls=%async_computation.1 | async-start | bytes 1048576 | tf_op jit(solution)/shard_map/all_to_all | solution.py:334
  100.2 3.2 %collective-permute-start.17 = (bf16[128,256]{1,0:T(8,128)(2,1)S(1)}, bf16[128,256]{1,0:T(8,128)(2,1)S(1)}, u32[]{:S(2)}, u32[]{:S(2)}) collective-permute-start(bf16[128,256]{1,0:T(8,128)(2,1)S(1)} %get-tuple-element.111), channel_id=1, source_target_pairs={{0,2},{1,3},{2,0},{3,1},{4,6},{5,7},{6,4},{7,5},{8,10},{9,11},{10,... | collective-permute-start | bytes 196616 | tf_op jit(solution)/shard_map/ppermute | solution.py:31
  103.4 1.3 collective-permute-start.18
  104.9 1.5 collective-permute-done.17
  106.3 1.3 collective-permute-done.18
  107.7 5.0 %all-to-all-done.1.refs_1_ = bf16[8,128,256]{2,1,0:T(8,128)(2,1)S(1)} async-done(((bf16[8,128,256]{2,1,0:T(8,128)(2,1)}), bf16[8,128,256]{2,1,0:T(8,128)(2,1)S(1)}, u32[]{:S(2)}, u32[]{:S(2)}) %all-to-all-start.1) | async-done | bytes 524320 | tf_op jit(solution)/shard_map/all_to_all | solution.py:334
  112.9 5.0 %shard_map.110 = (bf16[2,128,256]{2,1,0:T(8,128)(2,1)S(1)}, bf16[2,128,256]{2,1,0:T(8,128)(2,1)S(1)}, bf16[4,128,256]{2,1,0:T(8,128)(2,1)S(1)}, bf16[4,128,256]{...) custom-call(s32[2]{0:T(128)S(1)} %add_convert_fusion.24.place_ref, ...), custom_call_target="tpu_custom_call" | custom-call | flops 603979776 | bytes 9437184 | tf_op jit(solution)/shard_map/pallas_call | solution.py:275
  118.4 2.8 %collective-permute-start.24 = (bf16[2,128,256]{2,1,0:T(8,128)(2,1)S(1)}, bf16[2,128,256]{2,1,0:T(8,128)(2,1)S(1)}, u32[]{:S(2)}, u32[]{:S(2)}) collective-permute-start(bf16[2,128,256]{2,1,0:T(8,128)(2,1)S(1)} %get-tuple-element.82), channel_id=1, source_target_pairs={{0,28},{4,0},{8,4},{12,8},{16,12},{20,16},{24,20},{28,24},{1,29},{... | collective-permute-start | bytes 393224 | tf_op jit(solution)/shard_map/ppermute | solution.py:31
  121.2 4.6 %shard_map.109 = (bf16[4,128,256]{2,1,0:T(8,128)(2,1)S(1)}, bf16[4,128,256]{2,1,0:T(8,128)(2,1)S(1)}, bf16[8,128,256]{2,1,0:T(8,128)(2,1)S(1)}, bf16[8,128,256]{2,1,0:T(8,128)(2,1)S(1)}, bf16[8,128,256]{2,1,0:T(8,128)(2,1)S(1)}) custom-call(s32[2]{0:T(128)S(1)} %add_convert_fusion.24.place_ref, s32[2,18]{1,0:T(2,128)S(1)} %pad_add_fusion.table_ref, ...), custom_call_target="tpu_custom_call" | custom-call | flops 603979776 | bytes 9437184 | tf_op jit(solution)/shard_map/pallas_call | solution.py:275
  125.8 1.1 collective-permute-start.19
  126.9 2.2 %collective-permute-start.21 = (bf16[4,128,256]{2,1,0:T(8,128)(2,1)S(1)}, bf16[4,128,256]{2,1,0:T(8,128)(2,1)S(1)}, u32[]{:S(2)}, u32[]{:S(2)}) collective-permute-start(bf16[4,128,256]{2,1,0:T(8,128)(2,1)S(1)} %get-tuple-element.76), channel_id=1, source_target_pairs={{0,3},{1,0},{2,1},{3,2},{4,7},{5,4},{6,5},{7,6},{8,11},{9,8},{10,9... | collective-permute-start | bytes 786440 | tf_op jit(solution)/shard_map/ppermute | solution.py:31
  129.3 2.1 %collective-permute-start.25 = (bf16[4,128,256]{2,1,0:T(8,128)(2,1)S(1)}, bf16[4,128,256]{2,1,0:T(8,128)(2,1)S(1)}, u32[]{:S(2)}, u32[]{:S(2)}) collective-permute-start(bf16[4,128,256]{2,1,0:T(8,128)(2,1)S(1)} %add_convert_fusion.11), channel_id=1, source_target_pairs={{0,4},{4,8},{8,12},{12,16},{16,20},{20,24},{24,28},{28,0},{1,5},{5... | collective-permute-start | bytes 786440 | tf_op jit(solution)/shard_map/ppermute | solution.py:31
  131.3 5.0 %collective-permute-done.19 = bf16[4,128,256]{2,1,0:T(8,128)(2,1)S(1)} collective-permute-done((bf16[4,128,256]{2,1,0:T(8,128)(2,1)S(1)}, bf16[4,128,256]{2,1,0:T(8,128)(2,1)S(1)}, u32[]{:S(2)}, u32[]{:S(2)}) %collective-permute-start.19) | collective-permute-done | bytes 262176 | tf_op jit(solution)/shard_map/ppermute | solution.py:31
  136.8 3.3 %collective-permute-start.22 = (bf16[8,128,256]{2,1,0:T(8,128)(2,1)S(1)}, bf16[8,128,256]{2,1,0:T(8,128)(2,1)S(1)}, u32[]{:S(2)}, u32[]{:S(2)}) collective-permute-start(bf16[8,128,256]{2,1,0:T(8,128)(2,1)S(1)} %add_convert_fusion.1), channel_id=1, source_target_pairs={{0,3},{1,0},{2,1},{3,2},{4,7},{5,4},{6,5},{7,6},{8,11},{9,8},{10,9... | collective-permute-start | bytes 1572872 | tf_op jit(solution)/shard_map/ppermute | solution.py:31
  140.3 2.1 %collective-permute-start.26 = (bf16[4,128,256]{2,1,0:T(8,128)(2,1)S(1)}, bf16[4,128,256]{2,1,0:T(8,128)(2,1)S(1)}, u32[]{:S(2)}, u32[]{:S(2)}) collective-permute-start(bf16[4,128,256]{2,1,0:T(8,128)(2,1)S(1)} %add_convert_fusion.10), channel_id=1, source_target_pairs={{0,4},{4,8},{8,12},{12,16},{16,20},{20,24},{24,28},{28,0},{1,5},{5... | collective-permute-start | bytes 786440 | tf_op jit(solution)/shard_map/ppermute | solution.py:31
  142.4 4.2 %collective-permute-done.29 = bf16[4,128,256]{2,1,0:T(8,128)(2,1)S(1)} collective-permute-done((bf16[4,128,256]{2,1,0:T(8,128)(2,1)S(1)}, bf16[4,128,256]{2,1,0:T(8,128)(2,1)S(1)}, u32[]{:S(2)}, u32[]{:S(2)}) %collective-permute-start.29) | collective-permute-done | bytes 262176 | tf_op jit(solution)/shard_map/ppermute | solution.py:31
  146.6 1.3 collective-permute-start.30
  148.9 1.0 add_convert_fusion
  149.9 8.1 %collective-permute-done.30 = bf16[4,128,256]{2,1,0:T(8,128)(2,1)S(1)} collective-permute-done((bf16[4,128,256]{2,1,0:T(8,128)(2,1)S(1)}, bf16[4,128,256]{2,1,0:T(8,128)(2,1)S(1)}, u32[]{:S(2)}, u32[]{:S(2)}) %collective-permute-start.30) | collective-permute-done | bytes 262176 | tf_op jit(solution)/shard_map/ppermute | solution.py:31
  157.9 5.8 %all-to-all-start.2 = ((bf16[8,128,256]{2,1,0:T(8,128)(2,1)}), bf16[8,128,256]{2,1,0:T(8,128)(2,1)S(1)}, u32[]{:S(2)}, u32[]{:S(2)}) async-start(bf16[8,128,256]{2,1,0:T(8,128)(2,1)} %add_convert_fusion), calls=%async_computation.2 | async-start | bytes 1048576 | tf_op jit(solution)/shard_map/all_to_all | solution.py:334
  164.3 2.8 %collective-permute-start.33 = (bf16[128,256]{1,0:T(8,128)(2,1)S(1)}, bf16[128,256]{1,0:T(8,128)(2,1)S(1)}, u32[]{:S(2)}, u32[]{:S(2)}) collective-permute-start(bf16[128,256]{1,0:T(8,128)(2,1)S(1)} %get-tuple-element.107), channel_id=1, source_target_pairs={{0,3},{1,0},{2,1},{3,2},{4,7},{5,4},{6,5},{7,6},{8,11},{9,8},{10,9... | collective-permute-start | bytes 196616 | tf_op jit(solution)/shard_map/ppermute | solution.py:31
  167.1 3.0 %collective-permute-done.31 = bf16[128,256]{1,0:T(8,128)(2,1)S(1)} collective-permute-done((bf16[128,256]{1,0:T(8,128)(2,1)S(1)}, bf16[128,256]{1,0:T(8,128)(2,1)S(1)}, u32[]{:S(2)}, u32[]{:S(2)}) %collective-permute-start.31) | collective-permute-done | bytes 65568 | tf_op jit(solution)/shard_map/ppermute | solution.py:31
  170.1 1.0 collective-permute-done.33
  171.2 6.0 %all-to-all-done.2.refs_1_ = bf16[8,128,256]{2,1,0:T(8,128)(2,1)S(1)} async-done(((bf16[8,128,256]{2,1,0:T(8,128)(2,1)}), bf16[8,128,256]{2,1,0:T(8,128)(2,1)S(1)}, u32[]{:S(2)}, u32[]{:S(2)}) %all-to-all-start.2) | async-done | bytes 524320 | tf_op jit(solution)/shard_map/all_to_all | solution.py:334
  177.6 13.5 %all_to_all.20.moments_ref = f32[32,8,128]{2,1,0:T(8,128)S(1)} all-to-all(f32[32,8,128]{2,1,0:T(8,128)S(1)} %get-tuple-element.92), channel_id=1, replica_groups=mesh['x'=4,'core'=2,'z'=8,'y'=4] {'z','y'}, dimensions={0} | all-to-all | bytes 262144 | tf_op jit(solution)/shard_map/all_to_all | solution.py:516
  (83 shorter events, 10.9 us)
Async XLA Ops:
  7.9 43.7 %collective-permute-start.3 = (bf16[18,256,256]{2,1,0:T(8,128)(2,1)}, bf16[18,256,256]{2,1,0:T(8,128)(2,1)}, u32[]{:S(2)}, u32[]{:S(2)}) collective-permute-start(bf16[18,256,256]{2,1,0:T(8,128)(2,1)} %shard_map.104), channel_id=1, source_target_pairs={{32,0},{64,32},{96,64},{128,96},{160,128},{192,160},{224,192},{33,... | collective-permute-start | bytes 7077896 | tf_op jit(solution)/shard_map/ppermute | solution.py:37
  10.1 10.4 %copy-start.1 = (bf16[1,1,256,256]{3,2,1,0:T(8,128)(2,1)S(1)}, bf16[1,1,256,256]{3,2,1,0:T(8,128)(2,1)}, u32[]{:S(2)}) copy-start(bf16[1,1,256,256]{3,2,1,0:T(8,128)(2,1)} %param.9) | copy-start | bytes 393220
  10.1 24.1 %copy-start.2 = (s32[1,18]{1,0:T(1,128)S(1)}, s32[1,18]{1,0:T(1,128)}, u32[]{:S(2)}) copy-start(s32[1,18]{1,0:T(1,128)} %param.16) | copy-start | bytes 220
  17.0 34.7 %collective-permute-start.2 = (bf16[18,256,256]{2,1,0:T(8,128)(2,1)}, bf16[18,256,256]{2,1,0:T(8,128)(2,1)}, u32[]{:S(2)}, u32[]{:S(2)}) collective-permute-start(bf16[18,256,256]{2,1,0:T(8,128)(2,1)} %shard_map.105), channel_id=1, source_target_pairs={{0,32},{32,64},{64,96},{96,128},{128,160},{160,192},{192,224},{1,3... | collective-permute-start | bytes 7077896 | tf_op jit(solution)/shard_map/ppermute | solution.py:37
  22.7 22.0 %all-to-all-start = ((f32[32,8,128]{2,1,0:T(8,128)}), f32[32,8,128]{2,1,0:T(8,128)S(1)}, u32[]{:S(2)}, u32[]{:S(2)}) async-start(f32[32,8,128]{2,1,0:T(8,128)} %broadcast_in_dim.4), calls=%async_computation | async-start | bytes 262144 | tf_op jit(solution)/shard_map/all_to_all | solution.py:491
  44.8 5.7 %collective-permute-start = (f32[1,256]{1,0:T(1,128)S(1)}, f32[1,256]{1,0:T(1,128)S(1)}, u32[]{:S(2)}, u32[]{:S(2)}) collective-permute-start(f32[1,256]{1,0:T(1,128)S(1)} %pad_maximum_fusion), channel_id=1, source_target_pairs={{0,32},{32,64},{64,96},{96,128},{128,160},{160,192},{192,224},{1,3... | collective-permute-start | bytes 3080 | tf_op jit(solution)/shard_map/ppermute | solution.py:37
  46.7 4.9 %collective-permute-start.1 = (f32[1,256]{1,0:T(1,128)S(1)}, f32[1,256]{1,0:T(1,128)S(1)}, u32[]{:S(2)}, u32[]{:S(2)}) collective-permute-start(f32[1,256]{1,0:T(1,128)S(1)} %pad_maximum_fusion), channel_id=1, source_target_pairs={{32,0},{64,32},{96,64},{128,96},{160,128},{192,160},{224,192},{33,... | collective-permute-start | bytes 3080 | tf_op jit(solution)/shard_map/ppermute | solution.py:37
  56.7 11.2 %collective-permute-start.8 = (bf16[2,128,256]{2,1,0:T(8,128)(2,1)S(1)}, bf16[2,128,256]{2,1,0:T(8,128)(2,1)S(1)}, u32[]{:S(2)}, u32[]{:S(2)}) collective-permute-start(bf16[2,128,256]{2,1,0:T(8,128)(2,1)S(1)} %get-tuple-element.59), channel_id=1, source_target_pairs={{0,4},{4,8},{8,12},{12,16},{16,20},{20,24},{24,28},{28,0},{1,5},{5... | collective-permute-start | bytes 393224 | tf_op jit(solution)/shard_map/ppermute | solution.py:31
  57.5 10.3 %collective-permute-start.9 = (bf16[2,128,256]{2,1,0:T(8,128)(2,1)S(1)}, bf16[2,128,256]{2,1,0:T(8,128)(2,1)S(1)}, u32[]{:S(2)}, u32[]{:S(2)}) collective-permute-start(bf16[2,128,256]{2,1,0:T(8,128)(2,1)S(1)} %get-tuple-element.60), channel_id=1, source_target_pairs={{0,28},{4,0},{8,4},{12,8},{16,12},{20,16},{24,20},{28,24},{1,29},{... | collective-permute-start | bytes 393224 | tf_op jit(solution)/shard_map/ppermute | solution.py:31
  64.5 8.2 %collective-permute-start.4 = (bf16[4,128,256]{2,1,0:T(8,128)(2,1)S(1)}, bf16[4,128,256]{2,1,0:T(8,128)(2,1)S(1)}, u32[]{:S(2)}, u32[]{:S(2)}) collective-permute-start(bf16[4,128,256]{2,1,0:T(8,128)(2,1)S(1)} %get-tuple-element.52), channel_id=1, source_target_pairs={{0,1},{1,2},{2,3},{3,0},{4,5},{5,6},{6,7},{7,4},{8,9},{9,10},{10,1... | collective-permute-start | bytes 786440 | tf_op jit(solution)/shard_map/ppermute | solution.py:31
  64.7 8.2 %collective-permute-start.6 = (bf16[4,128,256]{2,1,0:T(8,128)(2,1)S(1)}, bf16[4,128,256]{2,1,0:T(8,128)(2,1)S(1)}, u32[]{:S(2)}, u32[]{:S(2)}) collective-permute-start(bf16[4,128,256]{2,1,0:T(8,128)(2,1)S(1)} %get-tuple-element.54), channel_id=1, source_target_pairs={{0,3},{1,0},{2,1},{3,2},{4,7},{5,4},{6,5},{7,6},{8,11},{9,8},{10,9... | collective-permute-start | bytes 786440 | tf_op jit(solution)/shard_map/ppermute | solution.py:31
  67.9 8.4 %collective-permute-start.13 = (bf16[4,128,256]{2,1,0:T(8,128)(2,1)S(1)}, bf16[4,128,256]{2,1,0:T(8,128)(2,1)S(1)}, u32[]{:S(2)}, u32[]{:S(2)}) collective-permute-start(bf16[4,128,256]{2,1,0:T(8,128)(2,1)S(1)} %add_convert_fusion.14), channel_id=1, source_target_pairs={{0,28},{4,0},{8,4},{12,8},{16,12},{20,16},{24,20},{28,24},{1,29},{... | collective-permute-start | bytes 786440 | tf_op jit(solution)/shard_map/ppermute | solution.py:31
  68.5 8.4 %collective-permute-start.10 = (bf16[4,128,256]{2,1,0:T(8,128)(2,1)S(1)}, bf16[4,128,256]{2,1,0:T(8,128)(2,1)S(1)}, u32[]{:S(2)}, u32[]{:S(2)}) collective-permute-start(bf16[4,128,256]{2,1,0:T(8,128)(2,1)S(1)} %add_convert_fusion.17), channel_id=1, source_target_pairs={{0,4},{4,8},{8,12},{12,16},{16,20},{20,24},{24,28},{28,0},{1,5},{5... | collective-permute-start | bytes 786440 | tf_op jit(solution)/shard_map/ppermute | solution.py:31
  72.8 13.6 %collective-permute-start.5 = (bf16[8,128,256]{2,1,0:T(8,128)(2,1)S(1)}, bf16[8,128,256]{2,1,0:T(8,128)(2,1)S(1)}, u32[]{:S(2)}, u32[]{:S(2)}) collective-permute-start(bf16[8,128,256]{2,1,0:T(8,128)(2,1)S(1)} %add_convert_fusion.5), channel_id=1, source_target_pairs={{0,1},{1,2},{2,3},{3,0},{4,5},{5,6},{6,7},{7,4},{8,9},{9,10},{10,1... | collective-permute-start | bytes 1572872 | tf_op jit(solution)/shard_map/ppermute | solution.py:31
  73.0 13.4 %collective-permute-start.7 = (bf16[8,128,256]{2,1,0:T(8,128)(2,1)S(1)}, bf16[8,128,256]{2,1,0:T(8,128)(2,1)S(1)}, u32[]{:S(2)}, u32[]{:S(2)}) collective-permute-start(bf16[8,128,256]{2,1,0:T(8,128)(2,1)S(1)} %add_convert_fusion.4), channel_id=1, source_target_pairs={{0,3},{1,0},{2,1},{3,2},{4,7},{5,4},{6,5},{7,6},{8,11},{9,8},{10,9... | collective-permute-start | bytes 1572872 | tf_op jit(solution)/shard_map/ppermute | solution.py:31
  76.4 7.4 %collective-permute-start.14 = (bf16[4,128,256]{2,1,0:T(8,128)(2,1)S(1)}, bf16[4,128,256]{2,1,0:T(8,128)(2,1)S(1)}, u32[]{:S(2)}, u32[]{:S(2)}) collective-permute-start(bf16[4,128,256]{2,1,0:T(8,128)(2,1)S(1)} %add_convert_fusion.13), channel_id=1, source_target_pairs={{0,28},{4,0},{8,4},{12,8},{16,12},{20,16},{24,20},{28,24},{1,29},{... | collective-permute-start | bytes 786440 | tf_op jit(solution)/shard_map/ppermute | solution.py:31
  77.0 7.7 %collective-permute-start.11 = (bf16[4,128,256]{2,1,0:T(8,128)(2,1)S(1)}, bf16[4,128,256]{2,1,0:T(8,128)(2,1)S(1)}, u32[]{:S(2)}, u32[]{:S(2)}) collective-permute-start(bf16[4,128,256]{2,1,0:T(8,128)(2,1)S(1)} %add_convert_fusion.16), channel_id=1, source_target_pairs={{0,4},{4,8},{8,12},{12,16},{16,20},{20,24},{24,28},{28,0},{1,5},{5... | collective-permute-start | bytes 786440 | tf_op jit(solution)/shard_map/ppermute | solution.py:31
  83.9 6.5 %collective-permute-start.15 = (bf16[4,128,256]{2,1,0:T(8,128)(2,1)S(1)}, bf16[4,128,256]{2,1,0:T(8,128)(2,1)S(1)}, u32[]{:S(2)}, u32[]{:S(2)}) collective-permute-start(bf16[4,128,256]{2,1,0:T(8,128)(2,1)S(1)} %add_convert_fusion.12), channel_id=1, source_target_pairs={{0,28},{4,0},{8,4},{12,8},{16,12},{20,16},{24,20},{28,24},{1,29},{... | collective-permute-start | bytes 786440 | tf_op jit(solution)/shard_map/ppermute | solution.py:31
  84.7 28.0 %copy-start = (bf16[1,1,256,256]{3,2,1,0:T(8,128)(2,1)S(1)}, bf16[1,1,256,256]{3,2,1,0:T(8,128)(2,1)}, u32[]{:S(2)}) copy-start(bf16[1,1,256,256]{3,2,1,0:T(8,128)(2,1)} %param.12) | copy-start | bytes 393220
  84.7 7.7 %collective-permute-start.12 = (bf16[4,128,256]{2,1,0:T(8,128)(2,1)S(1)}, bf16[4,128,256]{2,1,0:T(8,128)(2,1)S(1)}, u32[]{:S(2)}, u32[]{:S(2)}) collective-permute-start(bf16[4,128,256]{2,1,0:T(8,128)(2,1)S(1)} %add_convert_fusion.15), channel_id=1, source_target_pairs={{0,4},{4,8},{8,12},{12,16},{16,20},{20,24},{24,28},{28,0},{1,5},{5... | collective-permute-start | bytes 786440 | tf_op jit(solution)/shard_map/ppermute | solution.py:31
  92.4 20.3 %all-to-all-start.1 = ((bf16[8,128,256]{2,1,0:T(8,128)(2,1)}), bf16[8,128,256]{2,1,0:T(8,128)(2,1)S(1)}, u32[]{:S(2)}, u32[]{:S(2)}) async-start(bf16[8,128,256]{2,1,0:T(8,128)(2,1)} %add_convert_fusion.3), calls=%async_computation.1 | async-start | bytes 1048576 | tf_op jit(solution)/shard_map/all_to_all | solution.py:334
  99.3 5.6 %collective-permute-start.16 = (bf16[128,256]{1,0:T(8,128)(2,1)S(1)}, bf16[128,256]{1,0:T(8,128)(2,1)S(1)}, u32[]{:S(2)}, u32[]{:S(2)}) collective-permute-start(bf16[128,256]{1,0:T(8,128)(2,1)S(1)} %get-tuple-element.109), channel_id=1, source_target_pairs={{0,1},{1,2},{2,3},{3,0},{4,5},{5,6},{6,7},{7,4},{8,9},{9,10},{10,1... | collective-permute-start | bytes 196616 | tf_op jit(solution)/shard_map/ppermute | solution.py:31
  100.2 6.1 %collective-permute-start.17 = (bf16[128,256]{1,0:T(8,128)(2,1)S(1)}, bf16[128,256]{1,0:T(8,128)(2,1)S(1)}, u32[]{:S(2)}, u32[]{:S(2)}) collective-permute-start(bf16[128,256]{1,0:T(8,128)(2,1)S(1)} %get-tuple-element.111), channel_id=1, source_target_pairs={{0,2},{1,3},{2,0},{3,1},{4,6},{5,7},{6,4},{7,5},{8,10},{9,11},{10,... | collective-permute-start | bytes 196616 | tf_op jit(solution)/shard_map/ppermute | solution.py:31
  103.4 4.3 %collective-permute-start.18 = (bf16[128,256]{1,0:T(8,128)(2,1)S(1)}, bf16[128,256]{1,0:T(8,128)(2,1)S(1)}, u32[]{:S(2)}, u32[]{:S(2)}) collective-permute-start(bf16[128,256]{1,0:T(8,128)(2,1)S(1)} %get-tuple-element.110), channel_id=1, source_target_pairs={{0,3},{1,0},{2,1},{3,2},{4,7},{5,4},{6,5},{7,6},{8,11},{9,8},{10,9... | collective-permute-start | bytes 196616 | tf_op jit(solution)/shard_map/ppermute | solution.py:31
  117.9 11.2 %collective-permute-start.23 = (bf16[2,128,256]{2,1,0:T(8,128)(2,1)S(1)}, bf16[2,128,256]{2,1,0:T(8,128)(2,1)S(1)}, u32[]{:S(2)}, u32[]{:S(2)}) collective-permute-start(bf16[2,128,256]{2,1,0:T(8,128)(2,1)S(1)} %get-tuple-element.81), channel_id=1, source_target_pairs={{0,4},{4,8},{8,12},{12,16},{16,20},{20,24},{24,28},{28,0},{1,5},{5... | collective-permute-start | bytes 393224 | tf_op jit(solution)/shard_map/ppermute | solution.py:31
  118.4 10.6 %collective-permute-start.24 = (bf16[2,128,256]{2,1,0:T(8,128)(2,1)S(1)}, bf16[2,128,256]{2,1,0:T(8,128)(2,1)S(1)}, u32[]{:S(2)}, u32[]{:S(2)}) collective-permute-start(bf16[2,128,256]{2,1,0:T(8,128)(2,1)S(1)} %get-tuple-element.82), channel_id=1, source_target_pairs={{0,28},{4,0},{8,4},{12,8},{16,12},{20,16},{24,20},{28,24},{1,29},{... | collective-permute-start | bytes 393224 | tf_op jit(solution)/shard_map/ppermute | solution.py:31
  125.8 10.5 %collective-permute-start.19 = (bf16[4,128,256]{2,1,0:T(8,128)(2,1)S(1)}, bf16[4,128,256]{2,1,0:T(8,128)(2,1)S(1)}, u32[]{:S(2)}, u32[]{:S(2)}) collective-permute-start(bf16[4,128,256]{2,1,0:T(8,128)(2,1)S(1)} %get-tuple-element.74), channel_id=1, source_target_pairs={{0,1},{1,2},{2,3},{3,0},{4,5},{5,6},{6,7},{7,4},{8,9},{9,10},{10,1... | collective-permute-start | bytes 786440 | tf_op jit(solution)/shard_map/ppermute | solution.py:31
  126.9 9.8 %collective-permute-start.21 = (bf16[4,128,256]{2,1,0:T(8,128)(2,1)S(1)}, bf16[4,128,256]{2,1,0:T(8,128)(2,1)S(1)}, u32[]{:S(2)}, u32[]{:S(2)}) collective-permute-start(bf16[4,128,256]{2,1,0:T(8,128)(2,1)S(1)} %get-tuple-element.76), channel_id=1, source_target_pairs={{0,3},{1,0},{2,1},{3,2},{4,7},{5,4},{6,5},{7,6},{8,11},{9,8},{10,9... | collective-permute-start | bytes 786440 | tf_op jit(solution)/shard_map/ppermute | solution.py:31
  129.1 10.9 %collective-permute-start.28 = (bf16[4,128,256]{2,1,0:T(8,128)(2,1)S(1)}, bf16[4,128,256]{2,1,0:T(8,128)(2,1)S(1)}, u32[]{:S(2)}, u32[]{:S(2)}) collective-permute-start(bf16[4,128,256]{2,1,0:T(8,128)(2,1)S(1)} %add_convert_fusion.8), channel_id=1, source_target_pairs={{0,28},{4,0},{8,4},{12,8},{16,12},{20,16},{24,20},{28,24},{1,29},{... | collective-permute-start | bytes 786440 | tf_op jit(solution)/shard_map/ppermute | solution.py:31
  129.3 11.0 %collective-permute-start.25 = (bf16[4,128,256]{2,1,0:T(8,128)(2,1)S(1)}, bf16[4,128,256]{2,1,0:T(8,128)(2,1)S(1)}, u32[]{:S(2)}, u32[]{:S(2)}) collective-permute-start(bf16[4,128,256]{2,1,0:T(8,128)(2,1)S(1)} %add_convert_fusion.11), channel_id=1, source_target_pairs={{0,4},{4,8},{8,12},{12,16},{16,20},{20,24},{24,28},{28,0},{1,5},{5... | collective-permute-start | bytes 786440 | tf_op jit(solution)/shard_map/ppermute | solution.py:31
  136.4 12.5 %collective-permute-start.20 = (bf16[8,128,256]{2,1,0:T(8,128)(2,1)S(1)}, bf16[8,128,256]{2,1,0:T(8,128)(2,1)S(1)}, u32[]{:S(2)}, u32[]{:S(2)}) collective-permute-start(bf16[8,128,256]{2,1,0:T(8,128)(2,1)S(1)} %add_convert_fusion.2), channel_id=1, source_target_pairs={{0,1},{1,2},{2,3},{3,0},{4,5},{5,6},{6,7},{7,4},{8,9},{9,10},{10,1... | collective-permute-start | bytes 1572872 | tf_op jit(solution)/shard_map/ppermute | solution.py:31
  136.8 12.1 %collective-permute-start.22 = (bf16[8,128,256]{2,1,0:T(8,128)(2,1)S(1)}, bf16[8,128,256]{2,1,0:T(8,128)(2,1)S(1)}, u32[]{:S(2)}, u32[]{:S(2)}) collective-permute-start(bf16[8,128,256]{2,1,0:T(8,128)(2,1)S(1)} %add_convert_fusion.1), channel_id=1, source_target_pairs={{0,3},{1,0},{2,1},{3,2},{4,7},{5,4},{6,5},{7,6},{8,11},{9,8},{10,9... | collective-permute-start | bytes 1572872 | tf_op jit(solution)/shard_map/ppermute | solution.py:31
  140.1 6.5 %collective-permute-start.29 = (bf16[4,128,256]{2,1,0:T(8,128)(2,1)S(1)}, bf16[4,128,256]{2,1,0:T(8,128)(2,1)S(1)}, u32[]{:S(2)}, u32[]{:S(2)}) collective-permute-start(bf16[4,128,256]{2,1,0:T(8,128)(2,1)S(1)} %add_convert_fusion.7), channel_id=1, source_target_pairs={{0,28},{4,0},{8,4},{12,8},{16,12},{20,16},{24,20},{28,24},{1,29},{... | collective-permute-start | bytes 786440 | tf_op jit(solution)/shard_map/ppermute | solution.py:31
  140.3 7.7 %collective-permute-start.26 = (bf16[4,128,256]{2,1,0:T(8,128)(2,1)S(1)}, bf16[4,128,256]{2,1,0:T(8,128)(2,1)S(1)}, u32[]{:S(2)}, u32[]{:S(2)}) collective-permute-start(bf16[4,128,256]{2,1,0:T(8,128)(2,1)S(1)} %add_convert_fusion.10), channel_id=1, source_target_pairs={{0,4},{4,8},{8,12},{12,16},{16,20},{20,24},{24,28},{28,0},{1,5},{5... | collective-permute-start | bytes 786440 | tf_op jit(solution)/shard_map/ppermute | solution.py:31
  146.6 11.3 %collective-permute-start.30 = (bf16[4,128,256]{2,1,0:T(8,128)(2,1)S(1)}, bf16[4,128,256]{2,1,0:T(8,128)(2,1)S(1)}, u32[]{:S(2)}, u32[]{:S(2)}) collective-permute-start(bf16[4,128,256]{2,1,0:T(8,128)(2,1)S(1)} %add_convert_fusion.6), channel_id=1, source_target_pairs={{0,28},{4,0},{8,4},{12,8},{16,12},{20,16},{24,20},{28,24},{1,29},{... | collective-permute-start | bytes 786440 | tf_op jit(solution)/shard_map/ppermute | solution.py:31
  148.0 9.9 %collective-permute-start.27 = (bf16[4,128,256]{2,1,0:T(8,128)(2,1)S(1)}, bf16[4,128,256]{2,1,0:T(8,128)(2,1)S(1)}, u32[]{:S(2)}, u32[]{:S(2)}) collective-permute-start(bf16[4,128,256]{2,1,0:T(8,128)(2,1)S(1)} %add_convert_fusion.9), channel_id=1, source_target_pairs={{0,4},{4,8},{8,12},{12,16},{16,20},{20,24},{24,28},{28,0},{1,5},{5... | collective-permute-start | bytes 786440 | tf_op jit(solution)/shard_map/ppermute | solution.py:31
  157.9 19.2 %all-to-all-start.2 = ((bf16[8,128,256]{2,1,0:T(8,128)(2,1)}), bf16[8,128,256]{2,1,0:T(8,128)(2,1)S(1)}, u32[]{:S(2)}, u32[]{:S(2)}) async-start(bf16[8,128,256]{2,1,0:T(8,128)(2,1)} %add_convert_fusion), calls=%async_computation.2 | async-start | bytes 1048576 | tf_op jit(solution)/shard_map/all_to_all | solution.py:334
  163.8 6.3 %collective-permute-start.31 = (bf16[128,256]{1,0:T(8,128)(2,1)S(1)}, bf16[128,256]{1,0:T(8,128)(2,1)S(1)}, u32[]{:S(2)}, u32[]{:S(2)}) collective-permute-start(bf16[128,256]{1,0:T(8,128)(2,1)S(1)} %get-tuple-element.106), channel_id=1, source_target_pairs={{0,1},{1,2},{2,3},{3,0},{4,5},{5,6},{6,7},{7,4},{8,9},{9,10},{10,1... | collective-permute-start | bytes 196616 | tf_op jit(solution)/shard_map/ppermute | solution.py:31
  163.9 6.3 %collective-permute-start.32 = (bf16[128,256]{1,0:T(8,128)(2,1)S(1)}, bf16[128,256]{1,0:T(8,128)(2,1)S(1)}, u32[]{:S(2)}, u32[]{:S(2)}) collective-permute-start(bf16[128,256]{1,0:T(8,128)(2,1)S(1)} %get-tuple-element.108), channel_id=1, source_target_pairs={{0,2},{1,3},{2,0},{3,1},{4,6},{5,7},{6,4},{7,5},{8,10},{9,11},{10,... | collective-permute-start | bytes 196616 | tf_op jit(solution)/shard_map/ppermute | solution.py:31
  164.3 6.8 %collective-permute-start.33 = (bf16[128,256]{1,0:T(8,128)(2,1)S(1)}, bf16[128,256]{1,0:T(8,128)(2,1)S(1)}, u32[]{:S(2)}, u32[]{:S(2)}) collective-permute-start(bf16[128,256]{1,0:T(8,128)(2,1)S(1)} %get-tuple-element.107), channel_id=1, source_target_pairs={{0,3},{1,0},{2,1},{3,2},{4,7},{5,4},{6,5},{7,6},{8,11},{9,8},{10,9... | collective-permute-start | bytes 196616 | tf_op jit(solution)/shard_map/ppermute | solution.py:31
